TPU v7x, 32 devices: a whole 2x2x4 slice. The times are simulated.
32 devices in a mesh: dp: 8 (over z, x), adapter: 2 (over y), mp: 2 (over core).
Axes of the slice: x: 2, y: 2, z: 4, core: 2. Of those that a mesh axis runs over, the one named last changes fastest.
Arguments:
- tokens: bfloat16 [3456, 8192], P(('dp', 'adapter')), may hold values from -6 to 6
- base_weight: bfloat16 [8192, 512], P('dp', 'mp'), may hold values from -0.0625 to 0.0625
- adapter_a: bfloat16 [2, 64, 8192], P('adapter'), may hold values from -0.0625 to 0.0625
- adapter_b: bfloat16 [2, 64, 512], P('adapter', None, 'mp'), may hold values from -0.75 to 0.75
- cotangent: bfloat16 [3456, 512], P(('dp', 'adapter'), 'mp'), may hold values from -0.15625 to 0.15625
- adapter_ids: int32 [3456], P(('dp', 'adapter')), may hold values from 0 to 1, as said below
Outputs:
- projected: bfloat16 [3456, 512], P(('dp', 'adapter'), 'mp')
- grad_a: float32 [2, 64, 8192], P('adapter', 'dp', 'mp')
- up_gradient: float32 [2, 64, 512], P('adapter', 'dp', 'mp')
Inputs may be any that keep to these rules, and one draw needn't show every extreme that they name: Among the 216 tokens of one device (aligned blocks of adapter_ids), no adapter occurs more than 144 times, some adapter occurs exactly 144 times, and every adapter occurs at least once.
All inputs are finite; a program needn't handle non-finite values.
Results may differ from a plain program's by a relative error of at most 0.0056.
Values may be sent and summed in bfloat16 or wider, within the bound.
No kernel may reach another device: no remote copies, remote signals or barrier semaphores. Data moves between devices by JAX's collectives and lax.ppermute only.
A program may use at most 64 MiB of HBM per device.

v0:
```python
import jax
import jax.numpy as jnp
from jax import lax
from jax.sharding import PartitionSpec as P

adapter_scale = 2.0


def reduce_over_rows(left, right):
    return lax.dot_general(
        left, right, (((0,), (0,)), ((), ())), preferred_element_type=jnp.float32
    )


def contract_cols(left, right):
    return lax.dot_general(
        left, right, (((1,), (1,)), ((), ())), preferred_element_type=jnp.float32
    )


def on_device(tokens, base_weight, adapter_a, adapter_b, cotangent, adapter_ids):
    owners = lax.axis_size("adapter")
    cores = lax.axis_size("mp")
    token_count, width = tokens.shape
    slot_rows = 4 * token_count // (3 * owners)
    column_part = width // cores
    member = lax.axis_index("mp")
    owner_ids = jnp.arange(owners, dtype=jnp.int32)
    onehot = (adapter_ids[:, None] == owner_ids[None, :]).astype(jnp.int32)
    ranking = jnp.sum((jnp.cumsum(onehot, axis=0) - 1) * onehot, axis=1)
    target = adapter_ids * slot_rows + ranking
    send_tokens = (
        jnp.zeros((owners * slot_rows, tokens.shape[1]), jnp.bfloat16).at[target].set(tokens)
    )
    send_grads = (
        jnp.zeros((owners * slot_rows, cotangent.shape[1]), jnp.bfloat16).at[target].set(cotangent)
    )
    recv_tokens, recv_grads = (
        lax.all_to_all(
            send_tokens.reshape(owners, slot_rows, tokens.shape[1]),
            "adapter",
            split_axis=0,
            concat_axis=0,
            tiled=True,
        ),
        lax.all_to_all(
            send_grads.reshape(owners, slot_rows, cotangent.shape[1]),
            "adapter",
            split_axis=0,
            concat_axis=0,
            tiled=True,
        ),
    )
    arrived = recv_tokens.reshape(owners * slot_rows, tokens.shape[1])
    incoming_gradient = recv_grads.reshape(owners * slot_rows, cotangent.shape[1])
    own_a = adapter_a[0]
    owned_up_weight = adapter_b[0]
    low_sum = contract_cols(arrived, own_a)
    feature_cols = lax.dynamic_slice_in_dim(arrived, member * column_part, column_part, 1)
    rank_activations = low_sum.astype(jnp.bfloat16)
    value_update = (
        adapter_scale
        * jnp.dot(rank_activations, owned_up_weight, preferred_element_type=jnp.float32)
    ).astype(jnp.bfloat16)
    returned = lax.all_to_all(
        value_update.reshape(owners, slot_rows, owned_up_weight.shape[1]),
        "adapter",
        split_axis=0,
        concat_axis=0,
        tiled=True,
    )
    delta_tokens = returned.reshape(owners * slot_rows, owned_up_weight.shape[1])[target]
    base = jnp.dot(
        tokens,
        lax.all_gather(base_weight, "dp", axis=0, tiled=True),
        preferred_element_type=jnp.float32,
    )
    projected = (base + delta_tokens.astype(jnp.float32)).astype(jnp.bfloat16)
    backward_total = lax.psum(contract_cols(incoming_gradient, owned_up_weight), "mp")
    backward_rows = (adapter_scale * backward_total).astype(jnp.bfloat16)
    up_term = adapter_scale * reduce_over_rows(rank_activations, incoming_gradient)
    term_a = reduce_over_rows(backward_rows, feature_cols)
    grad_a, up_gradient = (
        lax.psum_scatter(term_a[None], "dp", scatter_dimension=1, tiled=True),
        lax.psum_scatter(up_term[None], "dp", scatter_dimension=1, tiled=True),
    )
    return (projected, grad_a, up_gradient)


def solution(mesh):
    return jax.shard_map(
        on_device,
        mesh=mesh,
        in_specs=(
            P(("dp", "adapter"), None),
            P("dp", "mp"),
            P("adapter", None, None),
            P("adapter", None, "mp"),
            P(("dp", "adapter"), "mp"),
            P(("dp", "adapter")),
        ),
        out_specs=(P(("dp", "adapter"), "mp"), P("adapter", "dp", "mp"), P("adapter", "dp", "mp")),
        check_vma=False,
    )
```

profile of v0, /device:TPU:0, one launch (start us, length us, event | category | flops | bytes accessed | tf_op | source)
XLA Modules:
  0.0 236.8 jit_solution(878731729490074795)
XLA Ops:
  8.0 0.0 copy-start
  8.0 0.0 all-reduce.3.cloned.1.call-start
  8.1 0.8 iota_compare_fusion
  8.8 0.6 reduce-window.6
  9.5 0.2 slice_reduce_fusion
  9.7 0.2 reduce-window.9
  9.9 0.1 add_bitcast_fusion
  9.9 0.7 fusion.13
  10.6 0.7 compare_select_fusion
  11.3 1.7 scatter_custom_fusion.1
  13.0 8.6 %all_to_all.15 = bf16[2,144,256]{2,1,0:T(8,128)(2,1)S(1)} all-to-all(bf16[2,144,256]{2,1,0:T(8,128)(2,1)S(1)} %bitcast.38), channel_id=1, replica_groups=mesh['dp'=8,'adapter'=2,'mp'=2] {'adapter'}, dimensions={0} | all-to-all | bytes 294912 | tf_op jit(solution)/shard_map/all_to_all | solution.py:46
  21.6 1.6 fusion.10
  23.2 0.0 all-reduce.3.cloned.1.call-update
  23.3 0.0 all-gather.2.cloned.1.call-start
  23.3 0.5 all-gather.2.cloned.1.call-update
  23.8 9.5 %scatter_custom_fusion = bf16[288,8192]{1,0:T(8,128)(2,1)} fusion(s32[216]{0:T(256)S(1)} %compare_select_fusion, bf16[216,8192]{1,0:T(8,128)(2,1)} %param.6, bf16[]{:T(256)} %constant.10.clone.1), kind=kCustom, calls=%fused_computation.5 | custom fusion | bytes 4719104 | tf_op jit(solution)/shard_map/scatter | solution.py:33
  33.3 5.8 %all-to-all-start = ((bf16[2,144,8192]{2,1,0:T(8,128)(2,1)}), bf16[2,144,8192]{2,1,0:T(8,128)(2,1)}, u32[]{:S(2)}, u32[]{:S(2)}) async-start(bf16[2,144,8192]{2,1,0:T(8,128)(2,1)} %bitcast.34), calls=%async_computation | async-start | bytes 9437184 | tf_op jit(solution)/shard_map/all_to_all | solution.py:39
  39.1 0.0 reduce-scatter.5.cloned.1.call-start
  39.1 52.0 %all-to-all-done = bf16[2,144,8192]{2,1,0:T(8,128)(2,1)} async-done(((bf16[2,144,8192]{2,1,0:T(8,128)(2,1)}), bf16[2,144,8192]{2,1,0:T(8,128)(2,1)}, u32[]{:S(2)}, u32[]{:S(2)}) %all-to-all-start) | async-done | bytes 4718624 | tf_op jit(solution)/shard_map/all_to_all | solution.py:39
  91.1 0.0 copy-done
  91.1 4.0 %convolution_convert_fusion = bf16[288,64]{0,1:T(8,128)(2,1)S(1)} fusion(bf16[288,8192]{1,0:T(8,128)(2,1)} %bitcast.2, bf16[1,64,8192]{2,1,0:T(8,128)(2,1)S(1)} %copy-done), kind=kOutput, calls=%fused_computation.11 | convolution fusion | flops 302008320 | bytes 5804032 | tf_op jit(solution)/shard_map/dot_general | solution.py:16
  95.1 0.0 copy-start.1
  95.1 0.8 fusion.5
  95.9 0.0 reduce-scatter.5.cloned.1.call-update
  95.9 0.0 reduce-scatter.3.cloned.1.call-start
  96.0 0.0 all-reduce.3.cloned.1.call-done
  96.0 3.4 %convolution_bitcast_fusion = f32[1,64,4096]{2,1,0:T(8,128)} fusion(bf16[288,8192]{1,0:T(8,128)(2,1)} %bitcast.2, s32[]{:T(128)S(6)} %select_n.9, f32[288,64]{1,0:T(8,128)} %all-reduce.3.cloned.1.call-done), kind=kOutput, calls=%fused_computation.3 | convolution fusion | flops 151031808 | bytes 3555332 | tf_op jit(solution)/shard_map/dot_general | solution.py:10
  99.4 0.0 reduce-scatter.3.cloned.1.call-update
  99.4 0.0 copy-done.1
  99.5 0.9 fusion.3
  100.3 3.4 %all-to-all-start.1 = ((bf16[2,144,256]{2,1,0:T(8,128)(2,1)}), bf16[2,144,256]{2,1,0:T(8,128)(2,1)S(1)}, u32[]{:S(2)}, u32[]{:S(2)}) async-start(bf16[2,144,256]{2,1,0:T(8,128)(2,1)} %bitcast.5), calls=%async_computation.1 | async-start | bytes 294912 | tf_op jit(solution)/shard_map/all_to_all | solution.py:65
  103.8 4.5 %all-to-all-done.1 = bf16[2,144,256]{2,1,0:T(8,128)(2,1)S(1)} async-done(((bf16[2,144,256]{2,1,0:T(8,128)(2,1)}), bf16[2,144,256]{2,1,0:T(8,128)(2,1)S(1)}, u32[]{:S(2)}, u32[]{:S(2)}) %all-to-all-start.1) | async-done | bytes 147488 | tf_op jit(solution)/shard_map/all_to_all | solution.py:65
  108.3 1.1 gather_fusion
  109.4 0.0 all-gather.2.cloned.1.call-done
  109.4 5.0 %fusion.4 = bf16[216,256]{1,0:T(8,128)(2,1)} fusion(bf16[216,8192]{1,0:T(8,128)(2,1)} %param.6, bf16[8192,256]{1,0:T(8,128)(2,1)} %all-gather.2.cloned.1.call-done, bf16[216,256]{1,0:T(8,128)(2,1)S(1)} %gather_fusion), kind=kOutput, calls=%fused_computation.10 | convolution fusion | flops 906135552 | bytes 7954432 | tf_op jit(solution)/shard_map/dot_general | solution.py:73
  114.4 48.3 %reduce-scatter.5.cloned.1.call-done = f32[1,8,256]{2,1,0:T(8,128)} async-done(((f32[1,64,256]{2,1,0:T(8,128)}), f32[1,8,256]{2,1,0:T(8,128)}) %reduce-scatter.5.cloned.1.call-update) | async-done | bytes 8208 | tf_op jit(solution)/shard_map/reduce_scatter | solution.py:85
  162.8 66.4 %reduce-scatter.3.cloned.1.call-done = f32[1,8,4096]{2,1,0:T(8,128)} async-done(((f32[1,64,4096]{2,1,0:T(8,128)}), f32[1,8,4096]{2,1,0:T(8,128)}) %reduce-scatter.3.cloned.1.call-update) | async-done | bytes 131088 | tf_op jit(solution)/shard_map/reduce_scatter | solution.py:84
  (4 shorter events, 0.0 us)
Async XLA Ops:
  8.0 83.1 %copy-start = (bf16[1,64,8192]{2,1,0:T(8,128)(2,1)S(1)}, bf16[1,64,8192]{2,1,0:T(8,128)(2,1)}, u32[]{:S(2)}) copy-start(bf16[1,64,8192]{2,1,0:T(8,128)(2,1)} %param.8) | copy-start | bytes 3145732
  8.0 88.0 %all-reduce.3.cloned.1.call-start = ((), (), s32[]{:S(2)}) async-start(), calls=%async_computation.6 | async-start | bytes 294912 | tf_op jit(solution)/shard_map/psum | solution.py:79
  23.3 86.1 %all-gather.2.cloned.1.call-start = ((), (), s32[]{:S(2)}) async-start(), calls=%async_computation.5 | async-start | bytes 4718592 | tf_op jit(solution)/shard_map/all_gather | solution.py:75
  33.3 57.8 %all-to-all-start = ((bf16[2,144,8192]{2,1,0:T(8,128)(2,1)}), bf16[2,144,8192]{2,1,0:T(8,128)(2,1)}, u32[]{:S(2)}, u32[]{:S(2)}) async-start(bf16[2,144,8192]{2,1,0:T(8,128)(2,1)} %bitcast.34), calls=%async_computation | async-start | bytes 9437184 | tf_op jit(solution)/shard_map/all_to_all | solution.py:39
  39.1 123.7 %reduce-scatter.5.cloned.1.call-start = ((), (), s32[]{:S(2)}) async-start(), calls=%async_computation.8 | async-start | bytes 73728 | tf_op jit(solution)/shard_map/reduce_scatter | solution.py:85
  95.1 4.4 %copy-start.1 = (bf16[1,64,256]{2,1,0:T(8,128)(2,1)S(1)}, bf16[1,64,256]{2,1,0:T(8,128)(2,1)}, u32[]{:S(2)}) copy-start(bf16[1,64,256]{2,1,0:T(8,128)(2,1)} %param.9) | copy-start | bytes 98308
  95.9 133.3 %reduce-scatter.3.cloned.1.call-start = ((), (), s32[]{:S(2)}) async-start(), calls=%async_computation.7 | async-start | bytes 1179648 | tf_op jit(solution)/shard_map/reduce_scatter | solution.py:84
  100.3 8.0 %all-to-all-start.1 = ((bf16[2,144,256]{2,1,0:T(8,128)(2,1)}), bf16[2,144,256]{2,1,0:T(8,128)(2,1)S(1)}, u32[]{:S(2)}, u32[]{:S(2)}) async-start(bf16[2,144,256]{2,1,0:T(8,128)(2,1)} %bitcast.5), calls=%async_computation.1 | async-start | bytes 294912 | tf_op jit(solution)/shard_map/all_to_all | solution.py:65
Sparse Core Ops, SparseCore 0:
  23.4 18.2 all-reduce.2
Sparse Core Ops, SparseCore 1:
  25.9 73.2 all-gather.1
  103.0 59.8 reduce-scatter.4
  166.6 62.5 reduce-scatter.2
where the time goes:
time: 237 us
  waiting for transfers between devices  172 us (73%)
  matrix products  15.7 us (7%)
  between operations  15.7 us (7%)
  local copies, waits for them, and re-layouts  12.5 us (5%)
  starting transfers between devices  9.36 us (4%)
  blocking collectives  8.59 us (4%)
  other arithmetic  3.04 us (1%)
    reduce_scatter x1, waiting for transfers between devices, on_device(): lax.psum_scatter(term_a[None], 'dp', scatter_dimension=1, tiled=True)  66.4 us
    all_to_all x1, waiting for transfers between devices, on_device(): lax.all_to_all(send_tokens.reshape(owners, slot_rows, tokens.shape[1]), '...  52 us
    reduce_scatter x1, waiting for transfers between devices, on_device(): lax.psum_scatter(up_term[None], 'dp', scatter_dimension=1, tiled=True)  48.3 us
    scatter x1, local copies, waits for them, and re-layouts, on_device(): jnp.zeros((owners * slot_rows, tokens.shape[1]), jnp.bfloat16).at[target]  9.46 us
    all_to_all x1, blocking collectives, on_device(): lax.all_to_all(send_grads.reshape(owners, slot_rows, cotangent.shape[1]),...  8.59 us
    all_to_all x1, starting transfers between devices, on_device(): lax.all_to_all(send_tokens.reshape(owners, slot_rows, tokens.shape[1]), '...  5.77 us
    dot_general x2, matrix products, contract_cols(): lax.dot_general(left, right, (((1,), (1,)), ((), ())), preferred_element_...  5.58 us
    dot_general x1, matrix products, on_device(): jnp.dot(tokens, lax.all_gather(base_weight, 'dp', axis=0, tiled=True), pr...  5.02 us
  transfers between devices with their start and end apart: 6, of which 4 were waited for; matrix products, arithmetic and copies ran while one was open for 10% of the time, Pallas kernels for 0%

commit v1 on v0

v1 whole, which is shorter than its diff:
```python
import jax
import jax.numpy as jnp
from jax import lax
from jax.sharding import PartitionSpec as P

adapter_scale = 2.0


def reduce_over_rows(left, right):
    return lax.dot_general(
        left, right, (((0,), (0,)), ((), ())), preferred_element_type=jnp.float32
    )


def contract_cols(left, right):
    return lax.dot_general(
        left, right, (((1,), (1,)), ((), ())), preferred_element_type=jnp.float32
    )


def matmul(left, right):
    return jnp.dot(left, right, preferred_element_type=jnp.float32)


def by_owner(tokens, base_weight, adapter_a, adapter_b, cotangent, adapter_ids):
    owners = lax.axis_size("adapter")
    cores = lax.axis_size("mp")
    token_count, width = tokens.shape
    slot_rows = 4 * token_count // (3 * owners)
    column_part = width // cores
    member = lax.axis_index("mp")
    owner_ids = jnp.arange(owners, dtype=jnp.int32)
    onehot = (adapter_ids[:, None] == owner_ids[None, :]).astype(jnp.int32)
    ranking = jnp.sum((jnp.cumsum(onehot, axis=0) - 1) * onehot, axis=1)
    target = adapter_ids * slot_rows + ranking

    def exchange(rows):
        there = lax.all_to_all(
            rows.reshape(owners, slot_rows, rows.shape[1]),
            "adapter",
            split_axis=0,
            concat_axis=0,
            tiled=True,
        )
        return there.reshape(owners * slot_rows, rows.shape[1])

    def slotted(rows):
        return jnp.zeros((owners * slot_rows, rows.shape[1]), rows.dtype).at[target].set(rows)

    arrived = exchange(slotted(tokens))
    incoming_gradient = exchange(slotted(cotangent))
    own_a = adapter_a[0]
    own_b = adapter_b[0]
    feature_cols = lax.dynamic_slice_in_dim(arrived, member * column_part, column_part, 1)
    low = contract_cols(arrived, own_a).astype(jnp.bfloat16)
    value_update = (adapter_scale * matmul(low, own_b)).astype(jnp.bfloat16)
    delta_tokens = exchange(value_update)[target]
    base = matmul(tokens, lax.all_gather(base_weight, "dp", axis=0, tiled=True))
    projected = (base + delta_tokens.astype(jnp.float32)).astype(jnp.bfloat16)
    backward_total = lax.psum(contract_cols(incoming_gradient, own_b), "mp")
    backward_rows = (adapter_scale * backward_total).astype(jnp.bfloat16)
    up_term = adapter_scale * reduce_over_rows(low, incoming_gradient)
    term_a = reduce_over_rows(backward_rows, feature_cols)
    return (
        projected,
        lax.psum_scatter(term_a[None], "dp", scatter_dimension=1, tiled=True),
        lax.psum_scatter(up_term[None], "dp", scatter_dimension=1, tiled=True),
    )


AXES = ("dp", "adapter", "mp")


def by_width(tokens, base_weight, adapter_a, adapter_b, cotangent, adapter_ids):
    members = lax.axis_size("dp")
    line = members // 2
    half = line // 2
    count, width = tokens.shape
    features = cotangent.shape[1]
    rank = adapter_a.shape[1]
    block = width // (4 * line)
    part = half * block
    rows = rank // members
    expanded = 2 * rank
    padded = count + 8

    d = lax.axis_index("dp")
    z, x = d // 2, d % 2
    y = lax.axis_index("adapter")
    c = lax.axis_index("mp")

    def swap(array, dz=0, dx=0, dy=0, dc=0):
        pairs = []
        for here in range(members * 4):
            at_z, at_x, at_y, at_c = here // 8, here // 4 % 2, here // 2 % 2, here % 2
            there = (((at_z ^ dz) * 2 + (at_x ^ dx)) * 2 + (at_y ^ dy)) * 2 + (at_c ^ dc)
            pairs.append((here, there))
        return lax.ppermute(array, AXES, pairs)

    def columns(array, core, side, owner):
        return jnp.concatenate(
            [
                lax.dynamic_slice_in_dim(
                    array, (((core * half + j) * 2 + side) * 2 + owner) * block, block, 1
                )
                for j in range(half)
            ],
            axis=1,
        )

    own_a, own_b = adapter_a[0], adapter_b[0]
    part_x = swap(columns(tokens, c, 1 - x, y), dx=1)
    part_y = swap(
        jnp.concatenate([columns(tokens, c, x, 1 - y), columns(own_a, c, x, 1 - y)], axis=0), dy=1
    )
    part_d = swap(columns(tokens, c, 1 - x, 1 - y), dx=1, dy=1)
    id_rows = jnp.broadcast_to(
        jnp.pad(adapter_ids.astype(jnp.bfloat16), (0, features - count))[None], (8, features)
    )
    own_grads = jnp.concatenate([cotangent, id_rows], axis=0)
    grads_y = swap(jnp.concatenate([own_grads, own_b], axis=0), dy=1)
    grads_x = swap(own_grads, dx=1)
    grads_d = swap(own_grads, dx=1, dy=1)
    own_weight = lax.dynamic_slice_in_dim(base_weight, y * block, block, 0)
    weights = [own_weight] + [swap(own_weight, dz=k) for k in range(1, line)]

    grads = jnp.concatenate(
        [own_grads, grads_x, grads_y[:padded], grads_d, own_b, grads_y[padded:]], axis=0
    )
    grads_other = swap(grads, dc=1)

    def interleave(mine, theirs):
        owner = lax.broadcasted_iota(jnp.int32, (members, 2, rows, mine.shape[1]), 1)
        return jnp.where(
            owner == y, mine.reshape(members, 1, rows, -1), theirs.reshape(members, 1, rows, -1)
        ).reshape(expanded, -1)

    tail = 4 * padded
    up_here = interleave(grads[tail : tail + rank], grads[tail + rank :])
    up_other = interleave(grads_other[tail : tail + rank], grads_other[tail + rank :])
    owner_of_row = lax.broadcasted_iota(jnp.int32, (expanded, 1), 0) // rows % 2
    masks = [
        grads[s * padded + count, :count][None] == owner_of_row.astype(jnp.bfloat16)
        for s in range(4)
    ]
    back_sum = contract_cols(up_here, grads[:tail]) + contract_cols(up_other, grads_other[:tail])
    back = [
        jnp.where(
            masks[s], adapter_scale * back_sum[:, s * padded : s * padded + count], 0.0
        ).astype(jnp.bfloat16)
        for s in range(4)
    ]

    other_x, other_y, other_d = (swap(p, dc=1) for p in (part_x, part_y, part_d))
    here = [columns(tokens, c, x, y), part_x, part_y[:count], part_d]
    other = [columns(tokens, 1 - c, x, y), other_x, other_y[:count], other_d]
    down_here = interleave(columns(own_a, c, x, y), part_y[count:])
    down_other = interleave(columns(own_a, 1 - c, x, y), other_y[count:])

    grad_sum = 0.0
    up_sum = 0.0
    lows = []
    for s in range(4):
        grad_sum += matmul(back[s], here[s])
        low = contract_cols(down_here, here[s]) + contract_cols(down_other, other[s])
        low = adapter_scale * jnp.where(masks[s], low, 0.0)
        high = low.astype(jnp.bfloat16)
        rest = (low - high.astype(jnp.float32)).astype(jnp.bfloat16)
        lows.append((high, rest))
        up_sum += matmul(high, grads[s * padded : s * padded + count])

    terms = jnp.concatenate([grad_sum, up_sum], axis=1).astype(jnp.bfloat16)
    gathered = lax.all_to_all(terms, ("dp", "adapter"), split_axis=0, concat_axis=0, tiled=True)
    gathered = gathered.reshape(line, 2, 2, rows, part + features)
    total = jnp.sum(gathered.astype(jnp.float32), axis=0)
    up_gradient = jnp.sum(total[..., part:], axis=(0, 1))[None]
    grad_a = jnp.concatenate(
        [
            total[side, owner, :, j * block : (j + 1) * block]
            for j in range(half)
            for side in range(2)
            for owner in range(2)
        ],
        axis=1,
    )[None]

    flip_half, flip_low = (z // half) ^ c, z % half

    def pick(j, flip):
        index = flip * half + (flip_low ^ j)
        chosen = weights[0]
        for k in range(1, line):
            chosen = jnp.where(index == k, weights[k], chosen)
        return chosen

    weight_here = jnp.concatenate([pick(j, flip_half) for j in range(half)], axis=0)
    weight_other = jnp.concatenate([pick(j, 1 - flip_half) for j in range(half)], axis=0)
    values = []
    for s in range(4):
        high, rest = lows[s]
        values.append(
            matmul(here[s], weight_here)
            + matmul(other[s], weight_other)
            + reduce_over_rows(high, up_here)
            + reduce_over_rows(rest, up_here)
        )
    projected = (
        values[0]
        + swap(values[1].astype(jnp.bfloat16), dx=1).astype(jnp.float32)
        + swap(values[2].astype(jnp.bfloat16), dy=1).astype(jnp.float32)
        + swap(values[3].astype(jnp.bfloat16), dx=1, dy=1).astype(jnp.float32)
    ).astype(jnp.bfloat16)
    return projected, grad_a, up_gradient


def solution(mesh):
    line = mesh.shape["dp"] // 2
    square = mesh.shape["adapter"] == 2 and mesh.shape["mp"] == 2 and mesh.shape["dp"] % 4 == 0
    return jax.shard_map(
        by_width if square and line & (line - 1) == 0 else by_owner,
        mesh=mesh,
        in_specs=(
            P(("dp", "adapter"), None),
            P("dp", "mp"),
            P("adapter", None, None),
            P("adapter", None, "mp"),
            P(("dp", "adapter"), "mp"),
            P(("dp", "adapter")),
        ),
        out_specs=(P(("dp", "adapter"), "mp"), P("adapter", "dp", "mp"), P("adapter", "dp", "mp")),
        check_vma=False,
    )
```

time: 237 us -> 81.7 us (0.34)
  waiting for transfers between devices: 172 us -> 25.3 us
  between operations: 15.7 us -> 1.23 us
  starting transfers between devices: 9.36 us -> 23.8 us
  blocking collectives: 8.59 us -> 0 us
  other arithmetic: 3.04 us -> 6.1 us
    reduce_scatter x2 -> x0, waiting for transfers between devices: 115 us -> none  [the longest x1 66.4 us: on_device(): lax.psum_scatter(term_a[None], 'dp', scatter_dimension=1, tiled=True)]
    all_to_all x2 -> x1, waiting for transfers between devices: 56.5 us -> 0.01 us  [by_width(): lax.all_to_all(terms, ('dp', 'adapter'), split_axis=0, concat_axis=0, til...]
    ppermute x0 -> x16, waiting for transfers between devices: none -> 25.3 us  [swap(): return lax.ppermute(array, AXES, pairs)]
    ppermute x0 -> x16, starting transfers between devices: none -> 18 us  [swap(): return lax.ppermute(array, AXES, pairs)]
    scatter x2 -> x0, local copies, waits for them, and re-layouts: 11.2 us -> none  [the longest x1 9.46 us: on_device(): jnp.zeros((owners * slot_rows, tokens.shape[1]), jnp.bfloat16).at[target]]
    all_to_all x1 -> x0, blocking collectives: 8.59 us -> none  [on_device(): lax.all_to_all(send_grads.reshape(owners, slot_rows, cotangent.shape[1]),...]
    unnamed x5 -> x44, local copies, waits for them, and re-layouts: 0.02 us -> 4.81 us
    concatenate x0 -> x6, other arithmetic: none -> 4.2 us  [the longest x2 1.66 us: columns(): jnp.concatenate([lax.dynamic_slice_in_dim(array, (((core * half + j) * 2...]
  transfers between devices with their start and end apart: 6 -> 17, of which waited for: 4 -> 7; matrix products, arithmetic and copies ran while one was open for 10% -> 32% of each run, Pallas kernels for 0% -> 0%
where the time goes in v1:
time: 81.7 us; the launch traced here: 81.3 us
  waiting for transfers between devices  25.3 us (31%)
  starting transfers between devices  23.8 us (29%)
  matrix products  13.9 us (17%)
  local copies, waits for them, and re-layouts  11 us (13%)
  other arithmetic  6.1 us (7%)
  between operations  1.23 us (2%)
    ppermute x16, waiting for transfers between devices, swap(): return lax.ppermute(array, AXES, pairs)  25.3 us
    ppermute x16, starting transfers between devices, swap(): return lax.ppermute(array, AXES, pairs)  18 us
    dot_general x16, matrix products, matmul(): return jnp.dot(left, right, preferred_element_type=jnp.float32)  8.28 us
    all_to_all x1, starting transfers between devices, by_width(): lax.all_to_all(terms, ('dp', 'adapter'), split_axis=0, concat_axis=0, til...  5.78 us
    unnamed x44, local copies, waits for them, and re-layouts  4.81 us
    dot_general x10, matrix products, contract_cols(): lax.dot_general(left, right, (((1,), (1,)), ((), ())), preferred_element_...  2.9 us
    dot_general x8, matrix products, reduce_over_rows(): lax.dot_general(left, right, (((0,), (0,)), ((), ())), preferred_element_...  2.73 us
    dynamic_slice x1, local copies, waits for them, and re-layouts, columns(): lax.dynamic_slice_in_dim(array, (((core * half + j) * 2 + side) * 2 + own...  2.62 us
  transfers between devices with their start and end apart: 17, of which 7 were waited for; matrix products, arithmetic and copies ran while one was open for 32% of the time, Pallas kernels for 0%

profile of v1, /device:TPU:0, one launch (start us, length us, event | category | flops | bytes accessed | tf_op | source)
XLA Modules:
  0.0 81.3 jit_solution(11354916680808254175)
XLA Ops:
  0.7 0.7 convert_element_type.99
  1.4 0.9 %pad_maximum_fusion.13 = bf16[224,256]{1,0:T(8,128)(2,1)S(1)} fusion(bf16[8,256]{1,0:T(8,128)(2,1)S(1)} %broadcast_in_dim.123, bf16[216,256]{1,0:T(8,128)(2,1)} %param.10), kind=kLoop, calls=%fused_computation.75 | loop fusion | flops 229376 | bytes 229376 | tf_op jit(solution)/shard_map/concatenate | solution.py:120
  2.3 2.9 %collective-permute-start.8 = (bf16[224,256]{1,0:T(8,128)(2,1)S(1)}, bf16[224,256]{1,0:T(8,128)(2,1)S(1)}, u32[]{:S(2)}, u32[]{:S(2)}) collective-permute-start(bf16[224,256]{1,0:T(8,128)(2,1)S(1)} %pad_maximum_fusion.13), channel_id=1, source_target_pairs={{0,4},{1,5},{2,6},{3,7},{4,0},{5,1},{6,2},{7,3},{8,12},{9,13},{10,... | collective-permute-start | bytes 344072 | tf_op jit(solution)/shard_map/ppermute | solution.py:98
  5.2 1.5 %collective-permute-start.13 = (bf16[224,256]{1,0:T(8,128)(2,1)S(1)}, bf16[224,256]{1,0:T(8,128)(2,1)S(1)}, u32[]{:S(2)}, u32[]{:S(2)}) collective-permute-start(bf16[224,256]{1,0:T(8,128)(2,1)S(1)} %pad_maximum_fusion.13), channel_id=1, source_target_pairs={{0,6},{1,7},{2,4},{3,5},{4,2},{5,3},{6,0},{7,1},{8,14},{9,15},{10,... | collective-permute-start | bytes 344072 | tf_op jit(solution)/shard_map/ppermute | solution.py:98
  6.7 1.0 %constant_dynamic-slice_fusion.8 = bf16[512,256]{1,0:T(8,128)(2,1)S(1)} fusion(bf16[1024,256]{1,0:T(8,128)(2,1)} %param.7, s32[]{:T(128)S(6)} %select_n.214), kind=kLoop, calls=%fused_computation.157 | loop fusion | bytes 524292 | tf_op jit(solution)/shard_map/dynamic_slice | solution.py:124
  7.7 3.7 %collective-permute-start = (bf16[512,256]{1,0:T(8,128)(2,1)S(1)}, bf16[512,256]{1,0:T(8,128)(2,1)S(1)}, u32[]{:S(2)}, u32[]{:S(2)}) collective-permute-start(bf16[512,256]{1,0:T(8,128)(2,1)S(1)} %constant_dynamic-slice_fusion.8), channel_id=1, source_target_pairs={{0,24},{1,25},{2,26},{3,27},{4,28},{5,29},{6,30},{7,31},{8,16},{9,... | collective-permute-start | bytes 786440 | tf_op jit(solution)/shard_map/ppermute | solution.py:98
  11.4 0.8 collective-permute-start.2
  12.1 1.5 %constant_dynamic-update-slice_fusion.3 = (bf16[896,256]{1,0:T(8,128)(2,1)S(1)}, bf16[1024,256]{1,0:T(8,128)(2,1)}) fusion(bf16[216,256]{1,0:T(8,128)(2,1)} %param.10), kind=kLoop, calls=%fused_computation.114 | loop fusion | bytes 331776
  13.7 0.6 constant_dynamic-update-slice_fusion.2
  14.3 1.0 %dynamic-slice_bitcast_fusion.1 = (bf16[8,1,8,512]{3,2,0,1:T(8,128)(2,1)S(1)}, bf16[64,512]{1,0:T(8,128)(2,1)S(1)}, bf16[64,512]{1,0:T(8,128)(2,1)S(1)}, bf16[8,...) fusion(bf16[1,64,8192]{2,1,0:T(8,128)(2,1)} %param.8, ...), kind=kLoop, calls=%fused_computation.97 | loop fusion | bytes 786456 | tf_op jit(solution)/shard_map/concatenate | solution.py:101
  15.3 2.6 %constant_dynamic-slice_fusion.7 = (bf16[216,512]{1,0:T(8,128)(2,1)}, bf16[216,512]{1,0:T(8,128)(2,1)S(1)}, bf16[216,512]{1,0:T(8,128)(2,1)S(1)}, bf16[216,512]{...) fusion(bf16[216,8192]{1,0:T(8,128)(2,1)} %param.6, ...), kind=kLoop, calls=%fused_computation.156 | loop fusion | bytes 4423720 | tf_op jit(solution)/shard_map/dynamic_slice | solution.py:103
  18.0 0.8 %pad_maximum_fusion.4 = bf16[216,1024]{1,0:T(8,128)(2,1)} fusion(bf16[216,512]{1,0:T(8,128)(2,1)S(1)} %get-tuple-element.4, bf16[216,512]{1,0:T(8,128)(2,1)S(1)} %get-tuple-element.5), kind=kLoop, calls=%fused_computation.46 | loop fusion | flops 884736 | bytes 884736 | tf_op jit(solution)/shard_map/concatenate | solution.py:101
  18.8 0.8 %pad_maximum_fusion.5 = bf16[216,1024]{1,0:T(8,128)(2,1)} fusion(bf16[216,512]{1,0:T(8,128)(2,1)S(1)} %get-tuple-element.11, bf16[216,512]{1,0:T(8,128)(2,1)S(1)} %get-tuple-element.12), kind=kLoop, calls=%fused_computation.47 | loop fusion | flops 884736 | bytes 884736 | tf_op jit(solution)/shard_map/concatenate | solution.py:101
  19.6 0.9 %maximum_maximum_fusion = bf16[280,1024]{1,0:T(8,128)(2,1)} fusion(bf16[64,512]{1,0:T(8,128)(2,1)S(1)} %get-tuple-element.18, bf16[64,512]{1,0:T(8,128)(2,1)S(1)} %get-tuple-element.19, bf16[216,512]{1,0:T(8,128)(2,1)S(1)} %get-tuple-element.6, bf16[216,512]{1,0:T(8,128)(2,1)S(1)} %get-tuple-element.7), kind=kLoop, calls=%fused_computation.39 | loop fusion | flops 2293760 | bytes 1146880 | tf_op jit(solution)/shard_map/concatenate | solution.py:114
  20.8 0.4 collective-permute-start.5
  21.3 1.7 %collective-permute-start.6 = (bf16[216,1024]{1,0:T(8,128)(2,1)}, bf16[216,1024]{1,0:T(8,128)(2,1)S(1)}, u32[]{:S(2)}, u32[]{:S(2)}) collective-permute-start(bf16[216,1024]{1,0:T(8,128)(2,1)} %pad_maximum_fusion.4), channel_id=1, source_target_pairs={{0,4},{1,5},{2,6},{3,7},{4,0},{5,1},{6,2},{7,3},{8,12},{9,13},{10,... | collective-permute-start | bytes 1327112 | tf_op jit(solution)/shard_map/ppermute | solution.py:98
  23.0 0.7 constant_dynamic-update-slice_fusion.1
  23.7 2.4 %collective-permute-done.5 = bf16[288,256]{1,0:T(8,128)(2,1)S(1)} collective-permute-done((bf16[288,256]{1,0:T(8,128)(2,1)S(1)}, bf16[288,256]{1,0:T(8,128)(2,1)S(1)}, u32[]{:S(2)}, u32[]{:S(2)}) %collective-permute-start.5) | collective-permute-done | bytes 147488 | tf_op jit(solution)/shard_map/ppermute | solution.py:98
  26.0 1.4 %collective-permute-start.11 = (bf16[216,1024]{1,0:T(8,128)(2,1)}, bf16[216,1024]{1,0:T(8,128)(2,1)S(1)}, u32[]{:S(2)}, u32[]{:S(2)}) collective-permute-start(bf16[216,1024]{1,0:T(8,128)(2,1)} %pad_maximum_fusion.5), channel_id=1, source_target_pairs={{0,6},{1,7},{2,4},{3,5},{4,2},{5,3},{6,0},{7,1},{8,14},{9,15},{10,... | collective-permute-start | bytes 1327112 | tf_op jit(solution)/shard_map/ppermute | solution.py:98
  27.5 0.7 slice_dynamic-update-slice_fusion.1
  28.1 0.7 constant_dynamic-update-slice_fusion
  28.8 0.6 constant_dynamic-update-slice_fusion.5
  29.4 0.6 constant_dynamic-update-slice_fusion.4
  30.0 1.6 %collective-permute-start.3 = (bf16[280,1024]{1,0:T(8,128)(2,1)}, bf16[280,1024]{1,0:T(8,128)(2,1)S(1)}, u32[]{:S(2)}, u32[]{:S(2)}) collective-permute-start(bf16[280,1024]{1,0:T(8,128)(2,1)} %maximum_maximum_fusion), channel_id=1, source_target_pairs={{0,2},{1,3},{2,0},{3,1},{4,6},{5,7},{6,4},{7,5},{8,10},{9,11},{10,... | collective-permute-start | bytes 1720328 | tf_op jit(solution)/shard_map/ppermute | solution.py:98
  31.6 1.5 %collective-permute-done.1 = bf16[512,256]{1,0:T(8,128)(2,1)S(1)} collective-permute-done((bf16[512,256]{1,0:T(8,128)(2,1)S(1)}, bf16[512,256]{1,0:T(8,128)(2,1)S(1)}, u32[]{:S(2)}, u32[]{:S(2)}) %collective-permute-start.1) | collective-permute-done | bytes 262176 | tf_op jit(solution)/shard_map/ppermute | solution.py:98
  33.1 0.3 select_select_fusion.1
  33.5 1.0 %fusion.30 = f32[216,256]{1,0:T(8,128)} fusion(bf16[216,512]{1,0:T(8,128)(2,1)S(1)} %copy-done.10, bf16[216,512]{1,0:T(8,128)(2,1)S(1)} %copy-done.9, bf16[512,256]{1,0:T(8,128)(2,1)S(1)} %get-tuple-element.14, bf16[512,256]{1,0:T(8,128)(2,1)S(1)} %get-tuple-element.13), kind=kOutput, calls=%fused_computation.56 | convolution fusion | flops 115179520 | bytes 1187840 | tf_op jit(solution)/shard_map/dot_general | solution.py:22
  34.7 0.3 collective-permute-start.7
  35.0 7.6 %collective-permute-done.11 = bf16[216,1024]{1,0:T(8,128)(2,1)S(1)} collective-permute-done((bf16[216,1024]{1,0:T(8,128)(2,1)}, bf16[216,1024]{1,0:T(8,128)(2,1)S(1)}, u32[]{:S(2)}, u32[]{:S(2)}) %collective-permute-start.11) | collective-permute-done | bytes 442400 | tf_op jit(solution)/shard_map/ppermute | solution.py:98
  42.6 1.0 %fusion.95 = f32[216,256]{1,0:T(8,128)} fusion(bf16[216,1024]{1,0:T(8,128)(2,1)S(1)} %collective-permute-done.6, bf16[512,256]{1,0:T(8,128)(2,1)S(1)} %get-tuple-element.15, bf16[512,256]{1,0:T(8,128)(2,1)S(1)} %get-tuple-element.16), kind=kOutput, calls=%fused_computation.204 | convolution fusion | flops 114294784 | bytes 1187840 | tf_op jit(solution)/shard_map/dot_general | solution.py:22
  43.6 1.0 %fusion.94 = f32[216,256]{1,0:T(8,128)} fusion(bf16[216,1024]{1,0:T(8,128)(2,1)S(1)} %collective-permute-done.11, bf16[512,256]{1,0:T(8,128)(2,1)S(1)} %get-tuple-element.15, bf16[512,256]{1,0:T(8,128)(2,1)S(1)} %get-tuple-element.16), kind=kOutput, calls=%fused_computation.203 | convolution fusion | flops 114294784 | bytes 1187840 | tf_op jit(solution)/shard_map/dot_general | solution.py:22
  44.6 7.2 %collective-permute-done.3 = bf16[280,1024]{1,0:T(8,128)(2,1)S(1)} collective-permute-done((bf16[280,1024]{1,0:T(8,128)(2,1)}, bf16[280,1024]{1,0:T(8,128)(2,1)S(1)}, u32[]{:S(2)}, u32[]{:S(2)}) %collective-permute-start.3) | collective-permute-done | bytes 573472 | tf_op jit(solution)/shard_map/ppermute | solution.py:98
  51.8 1.0 %fusion.28 = f32[216,256]{1,0:T(8,128)} fusion(bf16[280,1024]{1,0:T(8,128)(2,1)S(1)} %collective-permute-done.3, bf16[512,256]{1,0:T(8,128)(2,1)S(1)} %get-tuple-element.15, bf16[512,256]{1,0:T(8,128)(2,1)S(1)} %get-tuple-element.16), kind=kOutput, calls=%fused_computation.53 | convolution fusion | flops 114294784 | bytes 1187840 | tf_op jit(solution)/shard_map/dot_general | solution.py:22
  53.5 0.3 fusion.41
  53.8 0.3 fusion.31
  54.2 0.3 convolution_add_fusion.1
  54.5 0.3 fusion.2
  57.0 0.9 %fusion.75 = f32[216,256]{1,0:T(8,128)} fusion(bf16[128,256]{1,0:T(8,128)(2,1)S(1)} %get-tuple-element.38, f32[128,216]{0,1:T(8,128)S(1)} %fusion.14), kind=kOutput, calls=%fused_computation.184 | convolution fusion | flops 14183424 | bytes 397312 | tf_op jit(solution)/shard_map/dot_general | solution.py:10
  59.5 0.7 pad_maximum_fusion.6
  60.2 5.8 %all-to-all-start = ((bf16[16,8,1280]{2,1,0:T(8,128)(2,1)}), bf16[16,8,1280]{2,1,0:T(8,128)(2,1)S(1)}, u32[]{:S(2)}, u32[]{:S(2)}) async-start(bf16[16,8,1280]{2,1,0:T(8,128)(2,1)} %pad_maximum_fusion.6), calls=%async_computation | async-start | bytes 655360 | tf_op jit(solution)/shard_map/all_to_all | solution.py:173
  66.0 1.3 %fusion.4 = f32[216,256]{1,0:T(8,128)S(1)} fusion(f32[216,256]{1,0:T(8,128)S(1)} %fusion.79, f32[216,256]{1,0:T(8,128)} %fusion.95, bf16[216,1024]{1,0:T(8,128)(2,1)S(1)} %collective-permute-done.7, bf16[512,256]{1,0:T(8,128)(2,1)S(1)} %get-tuple-element.14, bf16[512,256]{1,0:T(8,128)(2,1)S(1)} %get-tuple-element.13), kind=kOutput, calls=%fused_computation.15 | convolution fusion | flops 114405376 | bytes 1630208 | tf_op jit(solution)/shard_map/dot_general | solution.py:22
  67.6 2.0 %collective-permute-start.9 = (bf16[216,256]{1,0:T(8,128)(2,1)S(1)}, bf16[216,256]{1,0:T(8,128)(2,1)S(1)}, u32[]{:S(2)}, u32[]{:S(2)}) collective-permute-start(bf16[216,256]{1,0:T(8,128)(2,1)S(1)} %fusion.7), channel_id=1, source_target_pairs={{0,4},{1,5},{2,6},{3,7},{4,0},{5,1},{6,2},{7,3},{8,12},{9,13},{10,... | collective-permute-start | bytes 331784 | tf_op jit(solution)/shard_map/ppermute | solution.py:98
  70.1 1.5 %collective-permute-start.10 = (bf16[216,256]{1,0:T(8,128)(2,1)S(1)}, bf16[216,256]{1,0:T(8,128)(2,1)S(1)}, u32[]{:S(2)}, u32[]{:S(2)}) collective-permute-start(bf16[216,256]{1,0:T(8,128)(2,1)S(1)} %fusion.8), channel_id=1, source_target_pairs={{0,2},{1,3},{2,0},{3,1},{4,6},{5,7},{6,4},{7,5},{8,10},{9,11},{10,... | collective-permute-start | bytes 331784 | tf_op jit(solution)/shard_map/ppermute | solution.py:98
  72.7 1.6 %collective-permute-done.9 = bf16[216,256]{1,0:T(8,128)(2,1)S(1)} collective-permute-done((bf16[216,256]{1,0:T(8,128)(2,1)S(1)}, bf16[216,256]{1,0:T(8,128)(2,1)S(1)}, u32[]{:S(2)}, u32[]{:S(2)}) %collective-permute-start.9) | collective-permute-done | bytes 110624 | tf_op jit(solution)/shard_map/ppermute | solution.py:98
  74.3 4.8 %collective-permute-done.10 = bf16[216,256]{1,0:T(8,128)(2,1)S(1)} collective-permute-done((bf16[216,256]{1,0:T(8,128)(2,1)S(1)}, bf16[216,256]{1,0:T(8,128)(2,1)S(1)}, u32[]{:S(2)}, u32[]{:S(2)}) %collective-permute-start.10) | collective-permute-done | bytes 110624 | tf_op jit(solution)/shard_map/ppermute | solution.py:98
  79.1 0.8 %add_convert_fusion = bf16[216,256]{1,0:T(8,128)(2,1)} fusion(bf16[216,256]{1,0:T(8,128)(2,1)S(1)} %collective-permute-done.14, bf16[216,256]{1,0:T(8,128)(2,1)S(1)} %collective-permute-done.10, bf16[216,256]{1,0:T(8,128)(2,1)S(1)} %collective-permute-done.9, f32[216,256]{1,0:T(8,128)S(1)} %fusion.3, bf16[128,256]{1,0:T(8,128)(2,1)S(1)} %get-tuple-element.38, ...), kind=kOutput, calls=%fused_computation.63 | convolution fusion | flops 14708736 | bytes 839680 | tf_op jit(solution)/shard_map/dot_general | solution.py:10
  80.0 0.6 slice_reduce_fusion
  80.7 0.6 copy-done.13
  (95 shorter events, 6.6 us)
Async XLA Ops:
  0.6 13.1 %copy-start = (bf16[216,256]{1,0:T(8,128)(2,1)S(1)}, bf16[216,256]{1,0:T(8,128)(2,1)}, u32[]{:S(2)}) copy-start(bf16[216,256]{1,0:T(8,128)(2,1)} %param.10) | copy-start | bytes 331780
  0.6 13.1 %copy-start.2 = (bf16[1,64,256]{2,1,0:T(8,128)(2,1)S(1)}, bf16[1,64,256]{2,1,0:T(8,128)(2,1)}, u32[]{:S(2)}) copy-start(bf16[1,64,256]{2,1,0:T(8,128)(2,1)} %param.9) | copy-start | bytes 98308
  2.3 18.5 %collective-permute-start.8 = (bf16[224,256]{1,0:T(8,128)(2,1)S(1)}, bf16[224,256]{1,0:T(8,128)(2,1)S(1)}, u32[]{:S(2)}, u32[]{:S(2)}) collective-permute-start(bf16[224,256]{1,0:T(8,128)(2,1)S(1)} %pad_maximum_fusion.13), channel_id=1, source_target_pairs={{0,4},{1,5},{2,6},{3,7},{4,0},{5,1},{6,2},{7,3},{8,12},{9,13},{10,... | collective-permute-start | bytes 344072 | tf_op jit(solution)/shard_map/ppermute | solution.py:98
  5.2 16.0 %collective-permute-start.13 = (bf16[224,256]{1,0:T(8,128)(2,1)S(1)}, bf16[224,256]{1,0:T(8,128)(2,1)S(1)}, u32[]{:S(2)}, u32[]{:S(2)}) collective-permute-start(bf16[224,256]{1,0:T(8,128)(2,1)S(1)} %pad_maximum_fusion.13), channel_id=1, source_target_pairs={{0,6},{1,7},{2,4},{3,5},{4,2},{5,3},{6,0},{7,1},{8,14},{9,15},{10,... | collective-permute-start | bytes 344072 | tf_op jit(solution)/shard_map/ppermute | solution.py:98
  7.7 22.3 %collective-permute-start = (bf16[512,256]{1,0:T(8,128)(2,1)S(1)}, bf16[512,256]{1,0:T(8,128)(2,1)S(1)}, u32[]{:S(2)}, u32[]{:S(2)}) collective-permute-start(bf16[512,256]{1,0:T(8,128)(2,1)S(1)} %constant_dynamic-slice_fusion.8), channel_id=1, source_target_pairs={{0,24},{1,25},{2,26},{3,27},{4,28},{5,29},{6,30},{7,31},{8,16},{9,... | collective-permute-start | bytes 786440 | tf_op jit(solution)/shard_map/ppermute | solution.py:98
  11.4 21.7 %collective-permute-start.1 = (bf16[512,256]{1,0:T(8,128)(2,1)S(1)}, bf16[512,256]{1,0:T(8,128)(2,1)S(1)}, u32[]{:S(2)}, u32[]{:S(2)}) collective-permute-start(bf16[512,256]{1,0:T(8,128)(2,1)S(1)} %constant_dynamic-slice_fusion.8), channel_id=1, source_target_pairs={{0,16},{1,17},{2,18},{3,19},{4,20},{5,21},{6,22},{7,23},{8,24},{9,... | collective-permute-start | bytes 786440 | tf_op jit(solution)/shard_map/ppermute | solution.py:98
  11.4 21.8 %collective-permute-start.2 = (bf16[512,256]{1,0:T(8,128)(2,1)S(1)}, bf16[512,256]{1,0:T(8,128)(2,1)S(1)}, u32[]{:S(2)}, u32[]{:S(2)}) collective-permute-start(bf16[512,256]{1,0:T(8,128)(2,1)S(1)} %constant_dynamic-slice_fusion.8), channel_id=1, source_target_pairs={{0,8},{1,9},{2,10},{3,11},{4,12},{5,13},{6,14},{7,15},{8,0},{9,1},... | collective-permute-start | bytes 786440 | tf_op jit(solution)/shard_map/ppermute | solution.py:98
  20.5 12.6 %copy-start.1 = (bf16[1024,256]{1,0:T(8,128)(2,1)S(1)}, bf16[1024,256]{1,0:T(8,128)(2,1)}, u32[]{:S(2)}) copy-start(bf16[1024,256]{1,0:T(8,128)(2,1)} %param.7) | copy-start | bytes 1572868
  20.8 5.2 %collective-permute-start.5 = (bf16[288,256]{1,0:T(8,128)(2,1)S(1)}, bf16[288,256]{1,0:T(8,128)(2,1)S(1)}, u32[]{:S(2)}, u32[]{:S(2)}) collective-permute-start(bf16[288,256]{1,0:T(8,128)(2,1)S(1)} %pad_maximum_fusion.9), channel_id=1, source_target_pairs={{0,2},{1,3},{2,0},{3,1},{4,6},{5,7},{6,4},{7,5},{8,10},{9,11},{10,... | collective-permute-start | bytes 442376 | tf_op jit(solution)/shard_map/ppermute | solution.py:98
  21.3 13.4 %collective-permute-start.6 = (bf16[216,1024]{1,0:T(8,128)(2,1)}, bf16[216,1024]{1,0:T(8,128)(2,1)S(1)}, u32[]{:S(2)}, u32[]{:S(2)}) collective-permute-start(bf16[216,1024]{1,0:T(8,128)(2,1)} %pad_maximum_fusion.4), channel_id=1, source_target_pairs={{0,4},{1,5},{2,6},{3,7},{4,0},{5,1},{6,2},{7,3},{8,12},{9,13},{10,... | collective-permute-start | bytes 1327112 | tf_op jit(solution)/shard_map/ppermute | solution.py:98
  26.0 16.6 %collective-permute-start.11 = (bf16[216,1024]{1,0:T(8,128)(2,1)}, bf16[216,1024]{1,0:T(8,128)(2,1)S(1)}, u32[]{:S(2)}, u32[]{:S(2)}) collective-permute-start(bf16[216,1024]{1,0:T(8,128)(2,1)} %pad_maximum_fusion.5), channel_id=1, source_target_pairs={{0,6},{1,7},{2,4},{3,5},{4,2},{5,3},{6,0},{7,1},{8,14},{9,15},{10,... | collective-permute-start | bytes 1327112 | tf_op jit(solution)/shard_map/ppermute | solution.py:98
  28.8 4.7 %copy-start.9 = (bf16[216,512]{1,0:T(8,128)(2,1)S(1)}, bf16[216,512]{1,0:T(8,128)(2,1)}, u32[]{:S(2)}) copy-start(bf16[216,512]{1,0:T(8,128)(2,1)} %get-tuple-element.3) | copy-start | bytes 663556
  28.8 4.7 %copy-start.10 = (bf16[216,512]{1,0:T(8,128)(2,1)S(1)}, bf16[216,512]{1,0:T(8,128)(2,1)}, u32[]{:S(2)}) copy-start(bf16[216,512]{1,0:T(8,128)(2,1)} %get-tuple-element.8) | copy-start | bytes 663556
  30.0 21.8 %collective-permute-start.3 = (bf16[280,1024]{1,0:T(8,128)(2,1)}, bf16[280,1024]{1,0:T(8,128)(2,1)S(1)}, u32[]{:S(2)}, u32[]{:S(2)}) collective-permute-start(bf16[280,1024]{1,0:T(8,128)(2,1)} %maximum_maximum_fusion), channel_id=1, source_target_pairs={{0,2},{1,3},{2,0},{3,1},{4,6},{5,7},{6,4},{7,5},{8,10},{9,11},{10,... | collective-permute-start | bytes 1720328 | tf_op jit(solution)/shard_map/ppermute | solution.py:98
  33.1 19.7 %collective-permute-start.15 = (bf16[1024,256]{1,0:T(8,128)(2,1)}, bf16[1024,256]{1,0:T(8,128)(2,1)S(1)}, u32[]{:S(2)}, u32[]{:S(2)}) collective-permute-start(bf16[1024,256]{1,0:T(8,128)(2,1)} %get-tuple-element.27), channel_id=1, source_target_pairs={{0,1},{1,0},{2,3},{3,2},{4,5},{5,4},{6,7},{7,6},{8,9},{9,8},{10,11... | collective-permute-start | bytes 1572872 | tf_op jit(solution)/shard_map/ppermute | solution.py:98
  33.4 18.4 %copy-start.3 = (bf16[512,256]{1,0:T(8,128)(2,1)}, bf16[512,256]{1,0:T(8,128)(2,1)S(1)}, u32[]{:S(2)}) copy-start(bf16[512,256]{1,0:T(8,128)(2,1)S(1)} %get-tuple-element.15) | copy-start | bytes 786436
  33.5 18.4 %copy-start.5 = (bf16[512,256]{1,0:T(8,128)(2,1)}, bf16[512,256]{1,0:T(8,128)(2,1)S(1)}, u32[]{:S(2)}) copy-start(bf16[512,256]{1,0:T(8,128)(2,1)S(1)} %get-tuple-element.16) | copy-start | bytes 786436
  34.7 21.2 %collective-permute-start.7 = (bf16[216,1024]{1,0:T(8,128)(2,1)S(1)}, bf16[216,1024]{1,0:T(8,128)(2,1)S(1)}, u32[]{:S(2)}, u32[]{:S(2)}) collective-permute-start(bf16[216,1024]{1,0:T(8,128)(2,1)S(1)} %collective-permute-done.6), channel_id=1, source_target_pairs={{0,1},{1,0},{2,3},{3,2},{4,5},{5,4},{6,7},{7,6},{8,9},{9,8},{10,11... | collective-permute-start | bytes 1327112 | tf_op jit(solution)/shard_map/ppermute | solution.py:98
  42.6 15.8 %collective-permute-start.12 = (bf16[216,1024]{1,0:T(8,128)(2,1)S(1)}, bf16[216,1024]{1,0:T(8,128)(2,1)S(1)}, u32[]{:S(2)}, u32[]{:S(2)}) collective-permute-start(bf16[216,1024]{1,0:T(8,128)(2,1)S(1)} %collective-permute-done.11), channel_id=1, source_target_pairs={{0,1},{1,0},{2,3},{3,2},{4,5},{5,4},{6,7},{7,6},{8,9},{9,8},{10,11... | collective-permute-start | bytes 1327112 | tf_op jit(solution)/shard_map/ppermute | solution.py:98
  51.8 3.1 %collective-permute-start.4 = (bf16[280,1024]{1,0:T(8,128)(2,1)S(1)}, bf16[280,1024]{1,0:T(8,128)(2,1)S(1)}, u32[]{:S(2)}, u32[]{:S(2)}) collective-permute-start(bf16[280,1024]{1,0:T(8,128)(2,1)S(1)} %collective-permute-done.3), channel_id=1, source_target_pairs={{0,1},{1,0},{2,3},{3,2},{4,5},{5,4},{6,7},{7,6},{8,9},{9,8},{10,11... | collective-permute-start | bytes 1720328 | tf_op jit(solution)/shard_map/ppermute | solution.py:98
  54.9 1.8 %copy-start.11 = (bf16[280,1024]{1,0:T(8,128)(2,1)}, bf16[280,1024]{1,0:T(8,128)(2,1)S(1)}, u32[]{:S(2)}) copy-start(bf16[280,1024]{1,0:T(8,128)(2,1)S(1)} %collective-permute-done.4) | copy-start | bytes 1720324
  60.2 19.7 %all-to-all-start = ((bf16[16,8,1280]{2,1,0:T(8,128)(2,1)}), bf16[16,8,1280]{2,1,0:T(8,128)(2,1)S(1)}, u32[]{:S(2)}, u32[]{:S(2)}) async-start(bf16[16,8,1280]{2,1,0:T(8,128)(2,1)} %pad_maximum_fusion.6), calls=%async_computation | async-start | bytes 655360 | tf_op jit(solution)/shard_map/all_to_all | solution.py:173
  66.0 3.5 %copy-start.8 = (f32[216,256]{1,0:T(8,128)S(1)}, f32[216,256]{1,0:T(8,128)}, u32[]{:S(2)}) copy-start(f32[216,256]{1,0:T(8,128)} %fusion.75) | copy-start | bytes 663556
  66.0 3.5 %copy-start.12 = (bf16[280,1024]{1,0:T(8,128)(2,1)S(1)}, bf16[280,1024]{1,0:T(8,128)(2,1)}, u32[]{:S(2)}) copy-start(bf16[280,1024]{1,0:T(8,128)(2,1)} %copy-done.11) | copy-start | bytes 1720324
  66.0 3.5 %copy-start.14 = (f32[216,256]{1,0:T(8,128)S(1)}, f32[216,256]{1,0:T(8,128)}, u32[]{:S(2)}) copy-start(f32[216,256]{1,0:T(8,128)} %fusion.28) | copy-start | bytes 663556
  67.5 4.0 %copy-start.7 = (f32[216,256]{1,0:T(8,128)S(1)}, f32[216,256]{1,0:T(8,128)}, u32[]{:S(2)}) copy-start(f32[216,256]{1,0:T(8,128)} %fusion.94) | copy-start | bytes 663556
  67.6 6.8 %collective-permute-start.9 = (bf16[216,256]{1,0:T(8,128)(2,1)S(1)}, bf16[216,256]{1,0:T(8,128)(2,1)S(1)}, u32[]{:S(2)}, u32[]{:S(2)}) collective-permute-start(bf16[216,256]{1,0:T(8,128)(2,1)S(1)} %fusion.7), channel_id=1, source_target_pairs={{0,4},{1,5},{2,6},{3,7},{4,0},{5,1},{6,2},{7,3},{8,12},{9,13},{10,... | collective-permute-start | bytes 331784 | tf_op jit(solution)/shard_map/ppermute | solution.py:98
  70.0 2.4 %copy-start.4 = (bf16[512,256]{1,0:T(8,128)(2,1)S(1)}, bf16[512,256]{1,0:T(8,128)(2,1)}, u32[]{:S(2)}) copy-start(bf16[512,256]{1,0:T(8,128)(2,1)} %copy-done.3) | copy-start | bytes 786436
  70.0 2.4 %copy-start.6 = (bf16[512,256]{1,0:T(8,128)(2,1)S(1)}, bf16[512,256]{1,0:T(8,128)(2,1)}, u32[]{:S(2)}) copy-start(bf16[512,256]{1,0:T(8,128)(2,1)} %copy-done.5) | copy-start | bytes 786436
  70.0 2.4 %copy-start.15 = (f32[216,256]{1,0:T(8,128)S(1)}, f32[216,256]{1,0:T(8,128)}, u32[]{:S(2)}) copy-start(f32[216,256]{1,0:T(8,128)} %fusion.30) | copy-start | bytes 663556
  70.1 9.0 %collective-permute-start.10 = (bf16[216,256]{1,0:T(8,128)(2,1)S(1)}, bf16[216,256]{1,0:T(8,128)(2,1)S(1)}, u32[]{:S(2)}, u32[]{:S(2)}) collective-permute-start(bf16[216,256]{1,0:T(8,128)(2,1)S(1)} %fusion.8), channel_id=1, source_target_pairs={{0,2},{1,3},{2,0},{3,1},{4,6},{5,7},{6,4},{7,5},{8,10},{9,11},{10,... | collective-permute-start | bytes 331784 | tf_op jit(solution)/shard_map/ppermute | solution.py:98
  72.1 7.0 %collective-permute-start.14 = (bf16[216,256]{1,0:T(8,128)(2,1)S(1)}, bf16[216,256]{1,0:T(8,128)(2,1)S(1)}, u32[]{:S(2)}, u32[]{:S(2)}) collective-permute-start(bf16[216,256]{1,0:T(8,128)(2,1)S(1)} %fusion.9), channel_id=1, source_target_pairs={{0,6},{1,7},{2,4},{3,5},{4,2},{5,3},{6,0},{7,1},{8,14},{9,15},{10,... | collective-permute-start | bytes 331784 | tf_op jit(solution)/shard_map/ppermute | solution.py:98
  80.7 0.7 copy-start.13

commit v2 on v1

v2 whole, which is shorter than its diff:
```python
import functools

import jax
import jax.numpy as jnp
from jax import lax
from jax.experimental import pallas as pl
from jax.experimental.pallas import tpu as pltpu
from jax.sharding import PartitionSpec as P

adapter_scale = 2.0


def reduce_over_rows(left, right):
    return lax.dot_general(
        left, right, (((0,), (0,)), ((), ())), preferred_element_type=jnp.float32
    )


def contract_cols(left, right):
    return lax.dot_general(
        left, right, (((1,), (1,)), ((), ())), preferred_element_type=jnp.float32
    )


def matmul(left, right):
    return jnp.dot(left, right, preferred_element_type=jnp.float32)


def by_owner(tokens, base_weight, adapter_a, adapter_b, cotangent, adapter_ids):
    owners = lax.axis_size("adapter")
    cores = lax.axis_size("mp")
    token_count, width = tokens.shape
    slot_rows = 4 * token_count // (3 * owners)
    column_part = width // cores
    member = lax.axis_index("mp")
    owner_ids = jnp.arange(owners, dtype=jnp.int32)
    onehot = (adapter_ids[:, None] == owner_ids[None, :]).astype(jnp.int32)
    ranking = jnp.sum((jnp.cumsum(onehot, axis=0) - 1) * onehot, axis=1)
    target = adapter_ids * slot_rows + ranking

    def exchange(rows):
        there = lax.all_to_all(
            rows.reshape(owners, slot_rows, rows.shape[1]),
            "adapter",
            split_axis=0,
            concat_axis=0,
            tiled=True,
        )
        return there.reshape(owners * slot_rows, rows.shape[1])

    def slotted(rows):
        return jnp.zeros((owners * slot_rows, rows.shape[1]), rows.dtype).at[target].set(rows)

    arrived = exchange(slotted(tokens))
    incoming_gradient = exchange(slotted(cotangent))
    own_a = adapter_a[0]
    own_b = adapter_b[0]
    feature_cols = lax.dynamic_slice_in_dim(arrived, member * column_part, column_part, 1)
    low = contract_cols(arrived, own_a).astype(jnp.bfloat16)
    value_update = (adapter_scale * matmul(low, own_b)).astype(jnp.bfloat16)
    delta_tokens = exchange(value_update)[target]
    base = matmul(tokens, lax.all_gather(base_weight, "dp", axis=0, tiled=True))
    projected = (base + delta_tokens.astype(jnp.float32)).astype(jnp.bfloat16)
    backward_total = lax.psum(contract_cols(incoming_gradient, own_b), "mp")
    backward_rows = (adapter_scale * backward_total).astype(jnp.bfloat16)
    up_term = adapter_scale * reduce_over_rows(low, incoming_gradient)
    term_a = reduce_over_rows(backward_rows, feature_cols)
    return (
        projected,
        lax.psum_scatter(term_a[None], "dp", scatter_dimension=1, tiled=True),
        lax.psum_scatter(up_term[None], "dp", scatter_dimension=1, tiled=True),
    )


AXES = ("dp", "adapter", "mp")
HBM = pl.BlockSpec(memory_space=pl.ANY)
VMEM = pl.BlockSpec(memory_space=pltpu.VMEM)


def like(shape, dtype):
    return jax.ShapeDtypeStruct(shape, dtype)


def call(kernel, outs, args, scratch=(), held=(), kept=None):
    return pl.pallas_call(
        kernel,
        out_shape=outs,
        in_specs=[VMEM if k in held else HBM for k in range(len(args))],
        out_specs=[VMEM if kept is None or k in kept else HBM for k in range(len(outs))],
        scratch_shapes=scratch,
        compiler_params=pltpu.CompilerParams(vmem_limit_bytes=61 << 20),
        cost_estimate=pl.CostEstimate(flops=1000, bytes_accessed=1000, transcendentals=0),
    )(*args)


def column_blocks(core, side, owner, half, block):
    first = ((core * half * 2 + side) * 2 + owner) * block
    return [pl.multiple_of(first + 4 * j * block, block) for j in range(half)]


def through(moves, stages, sems):
    ins, outs = [], []
    for k, (source, target) in enumerate(moves):
        ins.append(pltpu.make_async_copy(source, stages[k], sems.at[0, k]))
        outs.append(pltpu.make_async_copy(stages[k], target, sems.at[1, k]))
    return ins, outs


def coordinates():
    return lax.axis_index("dp") % 2, lax.axis_index("adapter"), lax.axis_index("mp")


def pack_first(block, tokens, ids, own_b, cotangent, out_x, out_grads, stage, grads, sems, last):
    x, y, c = coordinates()
    count, part = out_x.shape
    half = part // block
    padded = count + 8
    moves = [
        (tokens.at[:, pl.ds(start, block)], out_x.at[:, pl.ds(j * block, block)])
        for j, start in enumerate(column_blocks(c, 1 - x, y, half, block))
    ]
    copies = [
        pltpu.make_async_copy(cotangent, grads.at[pl.ds(0, count)], last.at[0]),
        pltpu.make_async_copy(own_b, grads.at[pl.ds(padded, own_b.shape[0])], last.at[1]),
    ]
    ins, outs = through(moves, [stage.at[j] for j in range(half)], sems)
    for copy in copies + ins:
        copy.start()
    grads[count:padded, :count] = (
        jnp.broadcast_to(ids[...], (8, count)).astype(jnp.float32).astype(grads.dtype)
    )
    grads[count:padded, count:] = jnp.zeros((8, grads.shape[1] - count), grads.dtype)
    for copy in copies:
        copy.wait()
    send = pltpu.make_async_copy(grads, out_grads, last.at[2])
    send.start()
    for arrive, leave in zip(ins, outs):
        arrive.wait()
        leave.start()
    for copy in outs + [send]:
        copy.wait()


def pack_rest(
    block, tokens, own_a, out_y, out_d, out_here, out_other, down_here, down_other, stage, small, sems
):
    x, y, c = coordinates()
    count, part = out_d.shape
    rank = own_a.shape[0]
    half = part // block
    moves, stages = [], []
    for target, place in (
        (out_y, (c, x, 1 - y)),
        (out_d, (c, 1 - x, 1 - y)),
        (out_here, (c, x, y)),
        (out_other, (1 - c, x, y)),
    ):
        for j, start in enumerate(column_blocks(*place, half, block)):
            columns = pl.ds(j * block, block)
            stages.append(stage.at[len(stages)])
            moves.append((tokens.at[:, pl.ds(start, block)], target.at[pl.ds(0, count), columns]))
    used = 0
    for target, offset, place in (
        (out_y, count, (c, x, 1 - y)),
        (down_here, 0, (c, x, y)),
        (down_other, 0, (1 - c, x, y)),
    ):
        for j, start in enumerate(column_blocks(*place, half, block)):
            columns = pl.ds(j * block, block)
            stages.append(small.at[used])
            used += 1
            moves.append((own_a.at[:, pl.ds(start, block)], target.at[pl.ds(offset, rank), columns]))
    ins, outs = through(moves, stages, sems)
    for copy in ins:
        copy.start()
    for arrive, leave in zip(ins, outs):
        arrive.wait()
        leave.start()
    for copy in outs:
        copy.wait()


def source_terms(down_here, down_other, here, other, back, mask, grads):
    low = mask * (contract_cols(down_here, here) + contract_cols(down_other, other))
    high = low.astype(jnp.bfloat16)
    rest = (low - high.astype(jnp.float32)).astype(jnp.bfloat16)
    return matmul(back, here), matmul(high, grads), high, rest


def value_of(here, other, weight, part, high, rest, up):
    c = lax.axis_index("mp")
    return (
        matmul(here, weight[pl.ds(pl.multiple_of(c * part, part), part)])
        + matmul(other, weight[pl.ds(pl.multiple_of((1 - c) * part, part), part)])
        + reduce_over_rows(high, up)
        + reduce_over_rows(rest, up)
    )


def fetch(sources, targets, sems):
    waits, k = [], 0
    for source, target in zip(sources, targets):
        columns = source.shape[1]
        pair = []
        for part in (pl.ds(0, columns // 2), pl.ds(columns // 2, columns // 2)):
            pair.append(pltpu.make_async_copy(source.at[:, part], target.at[:, part], sems.at[k]))
            k += 1
            pair[-1].start()
        waits.append(pair)
    return waits


def wait_all(waits):
    for pair in waits:
        for copy in pair:
            copy.wait()


def terms_kernel(count, rows, *refs):
    ins, refs = refs[:16], refs[16:]
    terms, highs, rests, up_map = refs[:4]
    held, sums, sems = refs[4:20], refs[20], refs[21]
    waits = fetch(ins, held, sems)
    own, over_y, over_x, own2, over_y2, over_x2 = held[:6]
    part = held[6].shape[1]
    rank = terms.shape[0] // 2
    padded = count + 8
    wait_all(waits[:6])
    grads = [own[:padded], over_x[:padded], over_y[:padded], over_x[padded:]]
    grads2 = [own2[:padded], over_x2[:padded], over_y2[:padded], over_x2[padded:]]
    up_map[...] = jnp.concatenate([own[padded:], over_y[padded:]], axis=0)
    up = up_map[...]
    up2 = jnp.concatenate([own2[padded:], over_y2[padded:]], axis=0)
    mine = lax.broadcasted_iota(jnp.int32, (2 * rank, count), 0) < rank
    owner = lax.axis_index("adapter").astype(jnp.float32)
    backs, masks = [], []
    for s in range(4):
        ids = grads[s][count:].astype(jnp.float32)[:1, :count]
        same = jnp.where(ids == owner, adapter_scale, 0.0)
        mask = jnp.where(mine, same, adapter_scale - same)
        both = contract_cols(up, grads[s]) + contract_cols(up2, grads2[s])
        backs.append((mask * both[:, :count]).astype(jnp.bfloat16))
        masks.append(mask)
    wait_all(waits[6:])
    here, other = held[6:14:2], held[7:14:2]
    down_here = jnp.concatenate([held[14][...], here[2][count:]], axis=0)
    down_other = jnp.concatenate([held[15][...], other[2][count:]], axis=0)
    for s in range(4):
        grad, gained, highs[s], rests[s] = source_terms(
            down_here,
            down_other,
            here[s][:count],
            other[s][:count],
            backs[s],
            masks[s],
            grads[s][:count],
        )
        if s == 0:
            sums[:, :part] = grad
            sums[:, part:] = gained
        else:
            sums[:, :part] += grad
            sums[:, part:] += gained
    first = lax.axis_index("adapter") == 0
    for m in range(rank // rows):
        mine, theirs = sums[m * rows : (m + 1) * rows], sums[rank + m * rows : rank + (m + 1) * rows]
        terms[2 * m * rows : 2 * (m + 1) * rows] = jnp.concatenate(
            [jnp.where(first, mine, theirs), jnp.where(first, theirs, mine)], axis=0
        ).astype(terms.dtype)


def values_kernel(count, *refs):
    ins, (highs, rests, up) = refs[:9], refs[9:12]
    values, held, sems = refs[12:16], refs[16:25], refs[25]
    waits = fetch(ins, held, sems)
    wait_all(waits[:1])
    weight = held[0]
    for s in (1, 2, 3, 0):
        wait_all(waits[1 + 2 * s : 3 + 2 * s])
        here, other = held[1 + 2 * s], held[2 + 2 * s]
        values[s][...] = value_of(
            here[:count], other[:count], weight, here.shape[1], highs[s], rests[s], up[...]
        ).astype(values[s].dtype)


def by_width(tokens, base_weight, adapter_a, adapter_b, cotangent, adapter_ids):
    members = lax.axis_size("dp")
    line = members // 2
    half = line // 2
    count, width = tokens.shape
    features = cotangent.shape[1]
    rank = adapter_a.shape[1]
    block = width // (4 * line)
    part = half * block
    rows = rank // members
    padded = count + 8
    bf16, f32 = jnp.bfloat16, jnp.float32
    y = lax.axis_index("adapter")

    def swap(array, dx=0, dy=0, dc=0):
        pairs = []
        for here in range(members * 4):
            at_z, at_x, at_y, at_c = here // 8, here // 4 % 2, here // 2 % 2, here % 2
            there = ((at_z * 2 + (at_x ^ dx)) * 2 + (at_y ^ dy)) * 2 + (at_c ^ dc)
            pairs.append((here, there))
        return lax.ppermute(array, AXES, pairs)

    own_a, own_b = adapter_a[0], adapter_b[0]
    send_x, grads_own = call(
        functools.partial(pack_first, block),
        (like((count, part), bf16), like((padded + rank, features), bf16)),
        (tokens, adapter_ids[None], own_b, cotangent),
        scratch=[
            pltpu.VMEM((half, count, block), bf16),
            pltpu.VMEM((padded + rank, features), bf16),
            pltpu.SemaphoreType.DMA((2, half)),
            pltpu.SemaphoreType.DMA((3,)),
        ],
        held=(1,),
        kept=(),
    )
    own_a, send_x = lax.optimization_barrier((own_a, send_x))
    send_y, send_d, here_own, other_own, down_here, down_other = call(
        functools.partial(pack_rest, block),
        (like((count + rank, part), bf16),)
        + (like((count, part), bf16),) * 3
        + (like((rank, part), bf16),) * 2,
        (tokens, own_a),
        scratch=[
            pltpu.VMEM((4 * half, count, block), bf16),
            pltpu.VMEM((3 * half, rank, block), bf16),
            pltpu.SemaphoreType.DMA((2, 7 * half)),
        ],
        kept=(),
    )
    grads_y = swap(grads_own, dy=1)
    grads_y, send_y = lax.optimization_barrier((grads_y, send_y))
    part_x, part_y = swap(send_x, dx=1), swap(send_y, dy=1)
    own_weight = lax.dynamic_slice_in_dim(base_weight, y * block, block, 0)
    part_x, send_d, grads_y = lax.optimization_barrier((part_x, send_d, grads_y))
    grads_x = swap(jnp.concatenate([grads_own[:padded], grads_y[:padded]], axis=0), dx=1)
    part_d = swap(send_d, dx=1, dy=1)
    part_x, part_y, grads_x = lax.optimization_barrier((part_x, part_y, grads_x))
    weight = lax.all_to_all(
        jnp.tile(own_weight, (line, 1)),
        "dp",
        split_axis=0,
        concat_axis=0,
        tiled=True,
        axis_index_groups=[[2 * k + side for k in range(line)] for side in range(2)],
    )
    grads_pairs = [grads_own, grads_y, grads_x]
    grads_pairs += [swap(array, dc=1) for array in grads_pairs]
    other_x, other_y = swap(part_x, dc=1), swap(part_y, dc=1)
    part_d, other_x, other_y, *grads_pairs = lax.optimization_barrier(
        (part_d, other_x, other_y, *grads_pairs)
    )
    parts = (here_own, other_own, part_x, other_x, part_y, other_y, part_d, swap(part_d, dc=1))
    args = (*grads_pairs, *parts, down_here, down_other)
    terms, highs, rests, up_map = call(
        functools.partial(terms_kernel, count, rows),
        (
            like((2 * rank, part + features), bf16),
            like((4, 2 * rank, count), bf16),
            like((4, 2 * rank, count), bf16),
            like((2 * rank, features), bf16),
        ),
        args,
        scratch=[pltpu.VMEM(arg.shape, arg.dtype) for arg in args]
        + [
            pltpu.VMEM((2 * rank, part + features), f32),
            pltpu.SemaphoreType.DMA((2 * len(args),)),
        ],
    )
    gathered = lax.all_to_all(terms, ("dp", "adapter"), split_axis=0, concat_axis=0, tiled=True)
    gathered = gathered.reshape(line, 2, 2, rows, part + features)
    sums = jnp.sum(gathered.astype(f32), axis=0)
    up_gradient = jnp.sum(sums[..., part:], axis=(0, 1))[None]
    grad_a = jnp.concatenate(
        [
            sums[side, owner, :, j * block : (j + 1) * block]
            for j in range(half)
            for side in range(2)
            for owner in range(2)
        ],
        axis=1,
    )[None]
    args = (weight, *parts)
    value, value_x, value_y, value_d = call(
        functools.partial(values_kernel, count),
        (like((count, features), f32),) + (like((count, features), bf16),) * 3,
        args + (highs, rests, up_map),
        scratch=[pltpu.VMEM(arg.shape, arg.dtype) for arg in args]
        + [pltpu.SemaphoreType.DMA((2 * len(args),))],
        held=(9, 10, 11),
    )
    projected = (
        value
        + swap(value_x, dx=1).astype(f32)
        + swap(value_y, dy=1).astype(f32)
        + swap(value_d, dx=1, dy=1).astype(f32)
    ).astype(bf16)
    return projected, grad_a, up_gradient


def solution(mesh):
    line = mesh.shape["dp"] // 2
    square = mesh.shape["adapter"] == 2 and mesh.shape["mp"] == 2 and mesh.shape["dp"] % 4 == 0
    return jax.shard_map(
        by_width if square and line & (line - 1) == 0 else by_owner,
        mesh=mesh,
        in_specs=(
            P(("dp", "adapter"), None),
            P("dp", "mp"),
            P("adapter", None, None),
            P("adapter", None, "mp"),
            P(("dp", "adapter"), "mp"),
            P(("dp", "adapter")),
        ),
        out_specs=(P(("dp", "adapter"), "mp"), P("adapter", "dp", "mp"), P("adapter", "dp", "mp")),
        check_vma=False,
    )
```

time: 81.7 us -> 73.4 us (0.90)
  Pallas kernels: 0 us -> 17.3 us
  matrix products: 13.9 us -> 0 us
  local copies, waits for them, and re-layouts: 11 us -> 3.39 us
  other arithmetic: 6.1 us -> 2.3 us
  starting transfers between devices: 23.8 us -> 26 us
  waiting for transfers between devices: 25.3 us -> 23.1 us
    pallas_call x0 -> x4, Pallas kernels: none -> 17.3 us  [call(): pl.pallas_call(kernel, out_shape=outs, in_specs=[VMEM if k in held else H...]
    dot_general x34 -> x0, matrix products: 13.9 us -> none  [the longest x16 8.28 us: matmul(): return jnp.dot(left, right, preferred_element_type=jnp.float32)]
    all_to_all x0 -> x1, starting transfers between devices: none -> 4.87 us  [by_width(): lax.all_to_all(jnp.tile(own_weight, (line, 1)), 'dp', split_axis=0, conca...]
    concatenate x6 -> x1, other arithmetic: 4.2 us -> 0.02 us  [by_width(): jnp.concatenate([grads_own[:padded], grads_y[:padded]], axis=0)]
    ppermute x16 -> x14, starting transfers between devices: 18 us -> 14.5 us  [swap(): return lax.ppermute(array, AXES, pairs)]
    dynamic_slice x1 -> x0, local copies, waits for them, and re-layouts: 2.62 us -> none  [columns(): lax.dynamic_slice_in_dim(array, (((core * half + j) * 2 + side) * 2 + own...]
    unnamed x44 -> x39, local copies, waits for them, and re-layouts: 4.81 us -> 2.31 us
    concatenate x4 -> x1, local copies, waits for them, and re-layouts: 2.29 us -> 0.01 us  [by_width(): jnp.concatenate([sums[side, owner, :, j * block:(j + 1) * block] for j in...]
  transfers between devices with their start and end apart: 17 -> 16, of which waited for: 7 -> 10; matrix products, arithmetic and copies ran while one was open for 32% -> 4% of each run, Pallas kernels for 0% -> 20%
where the time goes in v2:
time: 73.4 us; the launch traced here: 73 us
  starting transfers between devices  26 us (35%)
  waiting for transfers between devices  23.1 us (31%)
  Pallas kernels  17.3 us (24%)
  local copies, waits for them, and re-layouts  3.39 us (5%)
  other arithmetic  2.3 us (3%)
  between operations  0.86 us (1%)
    ppermute x14, waiting for transfers between devices, swap(): return lax.ppermute(array, AXES, pairs)  23.1 us
    pallas_call x4, Pallas kernels, call(): pl.pallas_call(kernel, out_shape=outs, in_specs=[VMEM if k in held else H...  17.3 us
    ppermute x14, starting transfers between devices, swap(): return lax.ppermute(array, AXES, pairs)  14.5 us
    all_to_all x1, starting transfers between devices, by_width(): lax.all_to_all(terms, ('dp', 'adapter'), split_axis=0, concat_axis=0, til...  6.64 us
    all_to_all x1, starting transfers between devices, by_width(): lax.all_to_all(jnp.tile(own_weight, (line, 1)), 'dp', split_axis=0, conca...  4.87 us
    unnamed x39, local copies, waits for them, and re-layouts  2.31 us
    convert_element_type x1, other arithmetic, by_width(): projected = (value + swap(value_x, dx=1).astype(f32) + swap(value_y, dy=1...  1.64 us
  transfers between devices with their start and end apart: 16, of which 10 were waited for; matrix products, arithmetic and copies ran while one was open for 4% of the time, Pallas kernels for 20%

profile of v2, /device:TPU:0, one launch (start us, length us, event | category | flops | bytes accessed | tf_op | source)
XLA Modules:
  0.0 73.0 jit_solution(1032728482538055222)
XLA Ops:
  0.6 0.0 copy-start
  0.6 2.6 %shard_map.85 = (bf16[216,1024]{1,0:T(8,128)(2,1)}, bf16[288,256]{1,0:T(8,128)(2,1)}) custom-call(bf16[216,8192]{1,0:T(8,128)(2,1)} %tokens.3, s32[1,216]{1,0:T(1,128)} %bitcast.48, bf16[64,256]{1,0:T(8,128)(2,1)} %bitcast.45, bf16[216,256]{1,0:T(8,128)(2,1)} %cotangent.1), custom_call_target="tpu_custom_call" | custom-call | flops 1000 | bytes 1000 | tf_op jit(solution)/shard_map/pallas_call | solution.py:85
  3.3 3.0 %collective-permute-start.1 = (bf16[288,256]{1,0:T(8,128)(2,1)}, bf16[288,256]{1,0:T(8,128)(2,1)S(1)}, u32[]{:S(2)}, u32[]{:S(2)}) collective-permute-start(bf16[288,256]{1,0:T(8,128)(2,1)} %get-tuple-element.57.refs_0_), channel_id=1, source_target_pairs={{0,2},{1,3},{2,0},{3,1},{4,6},{5,7},{6,4},{7,5},{8,10},{9,11},{10,... | collective-permute-start | bytes 442376 | tf_op jit(solution)/shard_map/ppermute | solution.py:306
  6.3 1.5 %collective-permute-start = (bf16[216,1024]{1,0:T(8,128)(2,1)}, bf16[216,1024]{1,0:T(8,128)(2,1)S(1)}, u32[]{:S(2)}, u32[]{:S(2)}) collective-permute-start(bf16[216,1024]{1,0:T(8,128)(2,1)} %get-tuple-element.42), channel_id=1, source_target_pairs={{0,4},{1,5},{2,6},{3,7},{4,0},{5,1},{6,2},{7,3},{8,12},{9,13},{10,... | collective-permute-start | bytes 1327112 | tf_op jit(solution)/shard_map/ppermute | solution.py:306
  7.8 2.6 %shard_map.86 = (bf16[280,1024]{1,0:T(8,128)(2,1)}, bf16[216,1024]{1,0:T(8,128)(2,1)}, bf16[216,1024]{1,0:T(8,128)(2,1)}, bf16[216,1024]{1,0:T(8,128)(2,1)}, bf1...) custom-call(bf16[216,8192]{1,0:T(8,128)(2,1)} %tokens.3, bf16[64,8192]{1,0:T(8,128)(2,1)} %bitcast.43), custom_call_target="tpu_custom_call" | custom-call | flops 1000 | bytes 1000 | tf_op jit(solution)/shard_map/pallas_call | solution.py:85
  10.4 0.0 copy-start.15
  10.5 0.0 collective-permute-done.1.refs_1_
  10.5 0.0 copy-start.9
  10.5 1.7 %collective-permute-start.2 = (bf16[280,1024]{1,0:T(8,128)(2,1)}, bf16[280,1024]{1,0:T(8,128)(2,1)S(1)}, u32[]{:S(2)}, u32[]{:S(2)}) collective-permute-start(bf16[280,1024]{1,0:T(8,128)(2,1)} %get-tuple-element.48), channel_id=1, source_target_pairs={{0,2},{1,3},{2,0},{3,1},{4,6},{5,7},{6,4},{7,5},{8,10},{9,11},{10,... | collective-permute-start | bytes 1720328 | tf_op jit(solution)/shard_map/ppermute | solution.py:306
  12.1 1.0 %tile.2 = bf16[4,512,256]{2,1,0:T(8,128)(2,1)} broadcast(bf16[512,256]{1,0:T(8,128)(2,1)S(1)} %constant_dynamic-slice_fusion), dimensions={1,2} | broadcast | bytes 1310720 | tf_op jit(solution)/shard_map/tile | solution.py:345
  13.2 4.9 %all-to-all-start = ((bf16[4,512,256]{2,1,0:T(8,128)(2,1)}), bf16[4,512,256]{2,1,0:T(8,128)(2,1)S(1)}, u32[]{:S(2)}, u32[]{:S(2)}) async-start(bf16[4,512,256]{2,1,0:T(8,128)(2,1)} %tile.2), calls=%async_computation | async-start | bytes 2097152 | tf_op jit(solution)/shard_map/all_to_all | solution.py:344
  18.1 0.1 collective-permute-done.refs_8_.refs_3_
  18.2 1.6 %collective-permute-start.3 = (bf16[448,256]{1,0:T(8,128)(2,1)S(1)}, bf16[448,256]{1,0:T(8,128)(2,1)S(1)}, u32[]{:S(2)}, u32[]{:S(2)}) collective-permute-start(bf16[448,256]{1,0:T(8,128)(2,1)S(1)} %pad_maximum_fusion), channel_id=1, source_target_pairs={{0,4},{1,5},{2,6},{3,7},{4,0},{5,1},{6,2},{7,3},{8,12},{9,13},{10,... | collective-permute-start | bytes 688136 | tf_op jit(solution)/shard_map/ppermute | solution.py:306
  19.8 4.7 %collective-permute-done.3.refs_2_ = bf16[448,256]{1,0:T(8,128)(2,1)S(1)} collective-permute-done((bf16[448,256]{1,0:T(8,128)(2,1)S(1)}, bf16[448,256]{1,0:T(8,128)(2,1)S(1)}, u32[]{:S(2)}, u32[]{:S(2)}) %collective-permute-start.3) | collective-permute-done | bytes 229408 | tf_op jit(solution)/shard_map/ppermute | solution.py:306
  24.4 0.5 collective-permute-done.2.refs_10_.refs_5_
  24.9 0.0 collective-permute-start.6
  24.9 2.3 %collective-permute-start.4 = (bf16[216,1024]{1,0:T(8,128)(2,1)S(1)}, bf16[216,1024]{1,0:T(8,128)(2,1)S(1)}, u32[]{:S(2)}, u32[]{:S(2)}) collective-permute-start(bf16[216,1024]{1,0:T(8,128)(2,1)S(1)} %copy-done.15), channel_id=1, source_target_pairs={{0,6},{1,7},{2,4},{3,5},{4,2},{5,3},{6,0},{7,1},{8,14},{9,15},{10,... | collective-permute-start | bytes 1327112 | tf_op jit(solution)/shard_map/ppermute | solution.py:306
  27.2 0.2 collective-permute-start.5
  27.3 0.4 collective-permute-start.7
  27.7 0.2 collective-permute-start.9
  27.9 1.3 %collective-permute-done.7.refs_3_ = bf16[288,256]{1,0:T(8,128)(2,1)S(1)} collective-permute-done((bf16[288,256]{1,0:T(8,128)(2,1)S(1)}, bf16[288,256]{1,0:T(8,128)(2,1)S(1)}, u32[]{:S(2)}, u32[]{:S(2)}) %collective-permute-start.7) | collective-permute-done | bytes 147488 | tf_op jit(solution)/shard_map/ppermute | solution.py:306
  29.2 0.2 collective-permute-start.8
  29.4 1.2 %collective-permute-done.8.refs_4_ = bf16[288,256]{1,0:T(8,128)(2,1)S(1)} collective-permute-done((bf16[288,256]{1,0:T(8,128)(2,1)S(1)}, bf16[288,256]{1,0:T(8,128)(2,1)S(1)}, u32[]{:S(2)}, u32[]{:S(2)}) %collective-permute-start.8) | collective-permute-done | bytes 147488 | tf_op jit(solution)/shard_map/ppermute | solution.py:306
  30.6 7.8 %collective-permute-done.4.refs_12_.refs_7_ = bf16[216,1024]{1,0:T(8,128)(2,1)S(1)} collective-permute-done((bf16[216,1024]{1,0:T(8,128)(2,1)S(1)}, bf16[216,1024]{1,0:T(8,128)(2,1)S(1)}, u32[]{:S(2)}, u32[]{:S(2)}) %collective-permute-start.4) | collective-permute-done | bytes 442400 | tf_op jit(solution)/shard_map/ppermute | solution.py:306
  38.4 0.0 collective-permute-done.9.refs_5_
  38.4 0.0 collective-permute-done.5.refs_9_.refs_4_
  38.4 0.8 %copy-done.11 = bf16[448,256]{1,0:T(8,128)(2,1)} copy-done((bf16[448,256]{1,0:T(8,128)(2,1)}, bf16[448,256]{1,0:T(8,128)(2,1)S(1)}, u32[]{:S(2)}) %copy-start.11) | copy-done | bytes 229400
  39.2 0.0 collective-permute-done.6.refs_11_.refs_6_
  39.2 0.0 copy-done.5
  39.3 0.1 collective-permute-start.10
  39.3 1.8 %collective-permute-done.10.refs_13_.refs_8_ = bf16[216,1024]{1,0:T(8,128)(2,1)S(1)} collective-permute-done((bf16[216,1024]{1,0:T(8,128)(2,1)S(1)}, bf16[216,1024]{1,0:T(8,128)(2,1)S(1)}, u32[]{:S(2)}, u32[]{:S(2)}) %collective-permute-start.10) | collective-permute-done | bytes 442400 | tf_op jit(solution)/shard_map/ppermute | solution.py:306
  41.1 0.8 %copy-done.7 = bf16[216,1024]{1,0:T(8,128)(2,1)} copy-done((bf16[216,1024]{1,0:T(8,128)(2,1)}, bf16[216,1024]{1,0:T(8,128)(2,1)S(1)}, u32[]{:S(2)}) %copy-start.7) | copy-done | bytes 442392
  41.9 0.0 copy-done.9
  41.9 5.5 %shard_map.87 = (bf16[128,1280]{1,0:T(8,128)(2,1)}, bf16[4,128,216]{2,1,0:T(8,128)(2,1)}, bf16[4,128,216]{2,1,0:T(8,128)(2,1)}, bf16[128,256]{1,0:T(8,128)(2,1)}) custom-call(bf16[288,256]{1,0:T(8,128)(2,1)} %get-tuple-element.57.refs_0_, bf16[288,256]{1,0:T(8,128)(2,1)} %copy-done.9, bf16[448,256]{1,0:T(8,128)(2,1)} %copy-done.10, ...), custom_call_target="tpu_custom_call" | custom-call | flops 1000 | bytes 1000 | tf_op jit(solution)/shard_map/pallas_call | solution.py:85
  47.4 0.0 all-to-all-done
  47.4 6.6 %all-to-all-start.1 = ((bf16[16,8,1280]{2,1,0:T(8,128)(2,1)}), bf16[16,8,1280]{2,1,0:T(8,128)(2,1)S(1)}, u32[]{:S(2)}, u32[]{:S(2)}) async-start(bf16[16,8,1280]{2,1,0:T(8,128)(2,1)} %bitcast.44), calls=%async_computation.1 | async-start | bytes 655360 | tf_op jit(solution)/shard_map/all_to_all | solution.py:375
  54.0 6.6 %shard_map.88 = (f32[216,256]{1,0:T(8,128)}, bf16[216,256]{1,0:T(8,128)(2,1)}, bf16[216,256]{1,0:T(8,128)(2,1)}, bf16[216,256]{1,0:T(8,128)(2,1)}) custom-call(bf16[2048,256]{1,0:T(8,128)(2,1)} %bitcast.41, bf16[216,1024]{1,0:T(8,128)(2,1)} %get-tuple-element.40.refs_6_.refs_1_, bf16[216,1024]{1,0:T(8,128)(2,1)} %get-tuple-element.41.refs_7_.refs_2_, ...), custom_call_target="tpu_custom_call" | custom-call | flops 1000 | bytes 1000 | tf_op jit(solution)/shard_map/pallas_call | solution.py:85
  60.6 2.0 %collective-permute-start.11 = (bf16[216,256]{1,0:T(8,128)(2,1)}, bf16[216,256]{1,0:T(8,128)(2,1)S(1)}, u32[]{:S(2)}, u32[]{:S(2)}) collective-permute-start(bf16[216,256]{1,0:T(8,128)(2,1)} %get-tuple-element.69), channel_id=1, source_target_pairs={{0,4},{1,5},{2,6},{3,7},{4,0},{5,1},{6,2},{7,3},{8,12},{9,13},{10,... | collective-permute-start | bytes 331784 | tf_op jit(solution)/shard_map/ppermute | solution.py:306
  62.6 1.5 %collective-permute-start.12 = (bf16[216,256]{1,0:T(8,128)(2,1)}, bf16[216,256]{1,0:T(8,128)(2,1)S(1)}, u32[]{:S(2)}, u32[]{:S(2)}) collective-permute-start(bf16[216,256]{1,0:T(8,128)(2,1)} %get-tuple-element.70), channel_id=1, source_target_pairs={{0,2},{1,3},{2,0},{3,1},{4,6},{5,7},{6,4},{7,5},{8,10},{9,11},{10,... | collective-permute-start | bytes 331784 | tf_op jit(solution)/shard_map/ppermute | solution.py:306
  64.1 0.1 collective-permute-start.13
  64.2 2.4 %collective-permute-done.11 = bf16[216,256]{1,0:T(8,128)(2,1)S(1)} collective-permute-done((bf16[216,256]{1,0:T(8,128)(2,1)}, bf16[216,256]{1,0:T(8,128)(2,1)S(1)}, u32[]{:S(2)}, u32[]{:S(2)}) %collective-permute-start.11) | collective-permute-done | bytes 110624 | tf_op jit(solution)/shard_map/ppermute | solution.py:306
  66.6 2.3 %collective-permute-done.12 = bf16[216,256]{1,0:T(8,128)(2,1)S(1)} collective-permute-done((bf16[216,256]{1,0:T(8,128)(2,1)}, bf16[216,256]{1,0:T(8,128)(2,1)S(1)}, u32[]{:S(2)}, u32[]{:S(2)}) %collective-permute-start.12) | collective-permute-done | bytes 110624 | tf_op jit(solution)/shard_map/ppermute | solution.py:306
  68.8 1.1 %collective-permute-done.13 = bf16[216,256]{1,0:T(8,128)(2,1)S(1)} collective-permute-done((bf16[216,256]{1,0:T(8,128)(2,1)}, bf16[216,256]{1,0:T(8,128)(2,1)S(1)}, u32[]{:S(2)}, u32[]{:S(2)}) %collective-permute-start.13) | collective-permute-done | bytes 110624 | tf_op jit(solution)/shard_map/ppermute | solution.py:306
  70.0 1.6 %add_convert_fusion = bf16[216,256]{1,0:T(8,128)(2,1)} fusion(bf16[216,256]{1,0:T(8,128)(2,1)S(1)} %collective-permute-done.13, bf16[216,256]{1,0:T(8,128)(2,1)S(1)} %collective-permute-done.12, f32[216,256]{1,0:T(8,128)} %get-tuple-element.68, bf16[216,256]{1,0:T(8,128)(2,1)S(1)} %collective-permute-done.11), kind=kLoop, calls=%fused_computation.2 | loop fusion | flops 387072 | bytes 663552 | tf_op jit(solution)/shard_map/convert_element_type | solution.py:402
  71.6 0.0 all-to-all-done.1
  71.6 0.6 slice_reduce_fusion
  72.3 0.0 copy-start.14
  72.3 0.6 copy-done.14
  (36 shorter events, 0.2 us)
Async XLA Ops:
  0.6 11.5 %copy-start = (bf16[1024,256]{1,0:T(8,128)(2,1)S(1)}, bf16[1024,256]{1,0:T(8,128)(2,1)}, u32[]{:S(2)}) copy-start(bf16[1024,256]{1,0:T(8,128)(2,1)} %param.7) | copy-start | bytes 1572868
  3.3 7.2 %collective-permute-start.1 = (bf16[288,256]{1,0:T(8,128)(2,1)}, bf16[288,256]{1,0:T(8,128)(2,1)S(1)}, u32[]{:S(2)}, u32[]{:S(2)}) collective-permute-start(bf16[288,256]{1,0:T(8,128)(2,1)} %get-tuple-element.57.refs_0_), channel_id=1, source_target_pairs={{0,2},{1,3},{2,0},{3,1},{4,6},{5,7},{6,4},{7,5},{8,10},{9,11},{10,... | collective-permute-start | bytes 442376 | tf_op jit(solution)/shard_map/ppermute | solution.py:306
  6.3 11.7 %copy-start.8 = (bf16[288,256]{1,0:T(8,128)(2,1)S(1)}, bf16[288,256]{1,0:T(8,128)(2,1)}, u32[]{:S(2)}) copy-start(bf16[288,256]{1,0:T(8,128)(2,1)} %get-tuple-element.57.refs_0_) | copy-start | bytes 442372
  6.3 11.8 %collective-permute-start = (bf16[216,1024]{1,0:T(8,128)(2,1)}, bf16[216,1024]{1,0:T(8,128)(2,1)S(1)}, u32[]{:S(2)}, u32[]{:S(2)}) collective-permute-start(bf16[216,1024]{1,0:T(8,128)(2,1)} %get-tuple-element.42), channel_id=1, source_target_pairs={{0,4},{1,5},{2,6},{3,7},{4,0},{5,1},{6,2},{7,3},{8,12},{9,13},{10,... | collective-permute-start | bytes 1327112 | tf_op jit(solution)/shard_map/ppermute | solution.py:306
  10.4 14.5 %copy-start.15 = (bf16[216,1024]{1,0:T(8,128)(2,1)S(1)}, bf16[216,1024]{1,0:T(8,128)(2,1)}, u32[]{:S(2)}) copy-start(bf16[216,1024]{1,0:T(8,128)(2,1)} %get-tuple-element.51) | copy-start | bytes 1327108
  10.5 31.4 %copy-start.9 = (bf16[288,256]{1,0:T(8,128)(2,1)}, bf16[288,256]{1,0:T(8,128)(2,1)S(1)}, u32[]{:S(2)}) copy-start(bf16[288,256]{1,0:T(8,128)(2,1)S(1)} %collective-permute-done.1.refs_1_) | copy-start | bytes 442372
  10.5 14.4 %collective-permute-start.2 = (bf16[280,1024]{1,0:T(8,128)(2,1)}, bf16[280,1024]{1,0:T(8,128)(2,1)S(1)}, u32[]{:S(2)}, u32[]{:S(2)}) collective-permute-start(bf16[280,1024]{1,0:T(8,128)(2,1)} %get-tuple-element.48), channel_id=1, source_target_pairs={{0,2},{1,3},{2,0},{3,1},{4,6},{5,7},{6,4},{7,5},{8,10},{9,11},{10,... | collective-permute-start | bytes 1720328 | tf_op jit(solution)/shard_map/ppermute | solution.py:306
  13.2 34.2 %all-to-all-start = ((bf16[4,512,256]{2,1,0:T(8,128)(2,1)}), bf16[4,512,256]{2,1,0:T(8,128)(2,1)S(1)}, u32[]{:S(2)}, u32[]{:S(2)}) async-start(bf16[4,512,256]{2,1,0:T(8,128)(2,1)} %tile.2), calls=%async_computation | async-start | bytes 2097152 | tf_op jit(solution)/shard_map/all_to_all | solution.py:344
  18.2 6.3 %copy-start.4 = (bf16[216,1024]{1,0:T(8,128)(2,1)}, bf16[216,1024]{1,0:T(8,128)(2,1)S(1)}, u32[]{:S(2)}) copy-start(bf16[216,1024]{1,0:T(8,128)(2,1)S(1)} %collective-permute-done.refs_8_.refs_3_) | copy-start | bytes 1327108
  18.2 6.2 %collective-permute-start.3 = (bf16[448,256]{1,0:T(8,128)(2,1)S(1)}, bf16[448,256]{1,0:T(8,128)(2,1)S(1)}, u32[]{:S(2)}, u32[]{:S(2)}) collective-permute-start(bf16[448,256]{1,0:T(8,128)(2,1)S(1)} %pad_maximum_fusion), channel_id=1, source_target_pairs={{0,4},{1,5},{2,6},{3,7},{4,0},{5,1},{6,2},{7,3},{8,12},{9,13},{10,... | collective-permute-start | bytes 688136 | tf_op jit(solution)/shard_map/ppermute | solution.py:306
  24.4 14.0 %copy-start.10 = (bf16[448,256]{1,0:T(8,128)(2,1)}, bf16[448,256]{1,0:T(8,128)(2,1)S(1)}, u32[]{:S(2)}) copy-start(bf16[448,256]{1,0:T(8,128)(2,1)S(1)} %collective-permute-done.3.refs_2_) | copy-start | bytes 688132
  24.9 17.0 %copy-start.2 = (bf16[280,1024]{1,0:T(8,128)(2,1)}, bf16[280,1024]{1,0:T(8,128)(2,1)S(1)}, u32[]{:S(2)}) copy-start(bf16[280,1024]{1,0:T(8,128)(2,1)S(1)} %collective-permute-done.2.refs_10_.refs_5_) | copy-start | bytes 1720324
  24.9 14.3 %collective-permute-start.6 = (bf16[280,1024]{1,0:T(8,128)(2,1)S(1)}, bf16[280,1024]{1,0:T(8,128)(2,1)S(1)}, u32[]{:S(2)}, u32[]{:S(2)}) collective-permute-start(bf16[280,1024]{1,0:T(8,128)(2,1)S(1)} %collective-permute-done.2.refs_10_.refs_5_), channel_id=1, source_target_pairs={{0,1},{1,0},{2,3},{3,2},{4,5},{5,4},{6,7},{7,6},{8,9},{9,8},{10,11... | collective-permute-start | bytes 1720328 | tf_op jit(solution)/shard_map/ppermute | solution.py:306
  24.9 13.5 %collective-permute-start.4 = (bf16[216,1024]{1,0:T(8,128)(2,1)S(1)}, bf16[216,1024]{1,0:T(8,128)(2,1)S(1)}, u32[]{:S(2)}, u32[]{:S(2)}) collective-permute-start(bf16[216,1024]{1,0:T(8,128)(2,1)S(1)} %copy-done.15), channel_id=1, source_target_pairs={{0,6},{1,7},{2,4},{3,5},{4,2},{5,3},{6,0},{7,1},{8,14},{9,15},{10,... | collective-permute-start | bytes 1327112 | tf_op jit(solution)/shard_map/ppermute | solution.py:306
  27.2 11.2 %collective-permute-start.5 = (bf16[216,1024]{1,0:T(8,128)(2,1)}, bf16[216,1024]{1,0:T(8,128)(2,1)S(1)}, u32[]{:S(2)}, u32[]{:S(2)}) collective-permute-start(bf16[216,1024]{1,0:T(8,128)(2,1)} %copy-done.4), channel_id=1, source_target_pairs={{0,1},{1,0},{2,3},{3,2},{4,5},{5,4},{6,7},{7,6},{8,9},{9,8},{10,11... | collective-permute-start | bytes 1327112 | tf_op jit(solution)/shard_map/ppermute | solution.py:306
  27.3 1.8 %collective-permute-start.7 = (bf16[288,256]{1,0:T(8,128)(2,1)S(1)}, bf16[288,256]{1,0:T(8,128)(2,1)S(1)}, u32[]{:S(2)}, u32[]{:S(2)}) collective-permute-start(bf16[288,256]{1,0:T(8,128)(2,1)S(1)} %copy-done.8), channel_id=1, source_target_pairs={{0,1},{1,0},{2,3},{3,2},{4,5},{5,4},{6,7},{7,6},{8,9},{9,8},{10,11... | collective-permute-start | bytes 442376 | tf_op jit(solution)/shard_map/ppermute | solution.py:306
  27.7 10.7 %collective-permute-start.9 = (bf16[448,256]{1,0:T(8,128)(2,1)S(1)}, bf16[448,256]{1,0:T(8,128)(2,1)S(1)}, u32[]{:S(2)}, u32[]{:S(2)}) collective-permute-start(bf16[448,256]{1,0:T(8,128)(2,1)S(1)} %collective-permute-done.3.refs_2_), channel_id=1, source_target_pairs={{0,1},{1,0},{2,3},{3,2},{4,5},{5,4},{6,7},{7,6},{8,9},{9,8},{10,11... | collective-permute-start | bytes 688136 | tf_op jit(solution)/shard_map/ppermute | solution.py:306
  29.2 12.7 %copy-start.12 = (bf16[288,256]{1,0:T(8,128)(2,1)}, bf16[288,256]{1,0:T(8,128)(2,1)S(1)}, u32[]{:S(2)}) copy-start(bf16[288,256]{1,0:T(8,128)(2,1)S(1)} %collective-permute-done.7.refs_3_) | copy-start | bytes 442372
  29.2 1.4 %collective-permute-start.8 = (bf16[288,256]{1,0:T(8,128)(2,1)S(1)}, bf16[288,256]{1,0:T(8,128)(2,1)S(1)}, u32[]{:S(2)}, u32[]{:S(2)}) collective-permute-start(bf16[288,256]{1,0:T(8,128)(2,1)S(1)} %collective-permute-done.1.refs_1_), channel_id=1, source_target_pairs={{0,1},{1,0},{2,3},{3,2},{4,5},{5,4},{6,7},{7,6},{8,9},{9,8},{10,11... | collective-permute-start | bytes 442376 | tf_op jit(solution)/shard_map/ppermute | solution.py:306
  30.6 11.3 %copy-start.13 = (bf16[288,256]{1,0:T(8,128)(2,1)}, bf16[288,256]{1,0:T(8,128)(2,1)S(1)}, u32[]{:S(2)}) copy-start(bf16[288,256]{1,0:T(8,128)(2,1)S(1)} %collective-permute-done.8.refs_4_) | copy-start | bytes 442372
  38.4 0.9 %copy-start.5 = (bf16[216,1024]{1,0:T(8,128)(2,1)}, bf16[216,1024]{1,0:T(8,128)(2,1)S(1)}, u32[]{:S(2)}) copy-start(bf16[216,1024]{1,0:T(8,128)(2,1)S(1)} %collective-permute-done.4.refs_12_.refs_7_) | copy-start | bytes 1327108
  38.4 0.8 %copy-start.11 = (bf16[448,256]{1,0:T(8,128)(2,1)}, bf16[448,256]{1,0:T(8,128)(2,1)S(1)}, u32[]{:S(2)}) copy-start(bf16[448,256]{1,0:T(8,128)(2,1)S(1)} %collective-permute-done.9.refs_5_) | copy-start | bytes 688132
  39.2 1.9 %copy-start.6 = (bf16[216,1024]{1,0:T(8,128)(2,1)}, bf16[216,1024]{1,0:T(8,128)(2,1)S(1)}, u32[]{:S(2)}) copy-start(bf16[216,1024]{1,0:T(8,128)(2,1)S(1)} %collective-permute-done.5.refs_9_.refs_4_) | copy-start | bytes 1327108
  39.2 2.6 %copy-start.3 = (bf16[280,1024]{1,0:T(8,128)(2,1)}, bf16[280,1024]{1,0:T(8,128)(2,1)S(1)}, u32[]{:S(2)}) copy-start(bf16[280,1024]{1,0:T(8,128)(2,1)S(1)} %collective-permute-done.6.refs_11_.refs_6_) | copy-start | bytes 1720324
  39.3 1.9 %collective-permute-start.10 = (bf16[216,1024]{1,0:T(8,128)(2,1)S(1)}, bf16[216,1024]{1,0:T(8,128)(2,1)S(1)}, u32[]{:S(2)}, u32[]{:S(2)}) collective-permute-start(bf16[216,1024]{1,0:T(8,128)(2,1)S(1)} %collective-permute-done.4.refs_12_.refs_7_), channel_id=1, source_target_pairs={{0,1},{1,0},{2,3},{3,2},{4,5},{5,4},{6,7},{7,6},{8,9},{9,8},{10,11... | collective-permute-start | bytes 1327112 | tf_op jit(solution)/shard_map/ppermute | solution.py:306
  41.1 0.8 %copy-start.7 = (bf16[216,1024]{1,0:T(8,128)(2,1)}, bf16[216,1024]{1,0:T(8,128)(2,1)S(1)}, u32[]{:S(2)}) copy-start(bf16[216,1024]{1,0:T(8,128)(2,1)S(1)} %collective-permute-done.10.refs_13_.refs_8_) | copy-start | bytes 1327108
  47.4 6.7 %copy-start.1 = (bf16[4,512,256]{2,1,0:T(8,128)(2,1)}, bf16[4,512,256]{2,1,0:T(8,128)(2,1)S(1)}, u32[]{:S(2)}) copy-start(bf16[4,512,256]{2,1,0:T(8,128)(2,1)S(1)} %all-to-all-done) | copy-start | bytes 3145732
  47.4 24.2 %all-to-all-start.1 = ((bf16[16,8,1280]{2,1,0:T(8,128)(2,1)}), bf16[16,8,1280]{2,1,0:T(8,128)(2,1)S(1)}, u32[]{:S(2)}, u32[]{:S(2)}) async-start(bf16[16,8,1280]{2,1,0:T(8,128)(2,1)} %bitcast.44), calls=%async_computation.1 | async-start | bytes 655360 | tf_op jit(solution)/shard_map/all_to_all | solution.py:375
  60.6 5.9 %collective-permute-start.11 = (bf16[216,256]{1,0:T(8,128)(2,1)}, bf16[216,256]{1,0:T(8,128)(2,1)S(1)}, u32[]{:S(2)}, u32[]{:S(2)}) collective-permute-start(bf16[216,256]{1,0:T(8,128)(2,1)} %get-tuple-element.69), channel_id=1, source_target_pairs={{0,4},{1,5},{2,6},{3,7},{4,0},{5,1},{6,2},{7,3},{8,12},{9,13},{10,... | collective-permute-start | bytes 331784 | tf_op jit(solution)/shard_map/ppermute | solution.py:306
  62.6 6.2 %collective-permute-start.12 = (bf16[216,256]{1,0:T(8,128)(2,1)}, bf16[216,256]{1,0:T(8,128)(2,1)S(1)}, u32[]{:S(2)}, u32[]{:S(2)}) collective-permute-start(bf16[216,256]{1,0:T(8,128)(2,1)} %get-tuple-element.70), channel_id=1, source_target_pairs={{0,2},{1,3},{2,0},{3,1},{4,6},{5,7},{6,4},{7,5},{8,10},{9,11},{10,... | collective-permute-start | bytes 331784 | tf_op jit(solution)/shard_map/ppermute | solution.py:306
  64.1 5.9 %collective-permute-start.13 = (bf16[216,256]{1,0:T(8,128)(2,1)}, bf16[216,256]{1,0:T(8,128)(2,1)S(1)}, u32[]{:S(2)}, u32[]{:S(2)}) collective-permute-start(bf16[216,256]{1,0:T(8,128)(2,1)} %get-tuple-element.71), channel_id=1, source_target_pairs={{0,6},{1,7},{2,4},{3,5},{4,2},{5,3},{6,0},{7,1},{8,14},{9,15},{10,... | collective-permute-start | bytes 331784 | tf_op jit(solution)/shard_map/ppermute | solution.py:306
  72.3 0.7 copy-start.14

commit v3 on v2

--- a/solution.py
+++ b/solution.py
@@ -88,7 +88,7 @@
         in_specs=[VMEM if k in held else HBM for k in range(len(args))],
         out_specs=[VMEM if kept is None or k in kept else HBM for k in range(len(outs))],
         scratch_shapes=scratch,
-        compiler_params=pltpu.CompilerParams(vmem_limit_bytes=61 << 20),
+        compiler_params=pltpu.CompilerParams(vmem_limit_bytes=56 << 20),
         cost_estimate=pl.CostEstimate(flops=1000, bytes_accessed=1000, transcendentals=0),
     )(*args)
 
@@ -198,32 +198,29 @@
 
 
 def fetch(sources, targets, sems):
-    waits, k = [], 0
-    for source, target in zip(sources, targets):
-        columns = source.shape[1]
-        pair = []
-        for part in (pl.ds(0, columns // 2), pl.ds(columns // 2, columns // 2)):
-            pair.append(pltpu.make_async_copy(source.at[:, part], target.at[:, part], sems.at[k]))
-            k += 1
-            pair[-1].start()
-        waits.append(pair)
-    return waits
-
-
-def wait_all(waits):
-    for pair in waits:
-        for copy in pair:
-            copy.wait()
-
-
-def terms_kernel(count, rows, *refs):
-    ins, refs = refs[:16], refs[16:]
-    terms, highs, rests, up_map = refs[:4]
-    held, sums, sems = refs[4:20], refs[20], refs[21]
+    copies = [
+        pltpu.make_async_copy(source, target, sems.at[k])
+        for k, (source, target) in enumerate(zip(sources, targets))
+    ]
+    for copy in copies:
+        copy.start()
+    return copies
+
+
+def wait_all(copies):
+    for copy in copies:
+        copy.wait()
+
+
+def early_kernel(count, *refs):
+    ins, refs = refs[:14], refs[14:]
+    total, highs, rests, up_map, back_d, mask_d, down_here, down_other = refs[:8]
+    held, sems = refs[8:22], refs[22]
     waits = fetch(ins, held, sems)
-    own, over_y, over_x, own2, over_y2, over_x2 = held[:6]
-    part = held[6].shape[1]
-    rank = terms.shape[0] // 2
+    parts, others = held[6:12], held[:6] + held[12:]
+    own, over_y, over_x, own2, over_y2, over_x2 = others[:6]
+    part = parts[0].shape[1]
+    rank = total.shape[0] // 2
     padded = count + 8
     wait_all(waits[:6])
     grads = [own[:padded], over_x[:padded], over_y[:padded], over_x[padded:]]
@@ -241,14 +238,16 @@
         both = contract_cols(up, grads[s]) + contract_cols(up2, grads2[s])
         backs.append((mask * both[:, :count]).astype(jnp.bfloat16))
         masks.append(mask)
+    back_d[...] = backs[3]
+    mask_d[...] = masks[3]
     wait_all(waits[6:])
-    here, other = held[6:14:2], held[7:14:2]
-    down_here = jnp.concatenate([held[14][...], here[2][count:]], axis=0)
-    down_other = jnp.concatenate([held[15][...], other[2][count:]], axis=0)
-    for s in range(4):
+    here, other = parts[::2], parts[1::2]
+    down_here[...] = jnp.concatenate([others[6][...], here[2][count:]], axis=0)
+    down_other[...] = jnp.concatenate([others[7][...], other[2][count:]], axis=0)
+    for s in range(3):
         grad, gained, highs[s], rests[s] = source_terms(
-            down_here,
-            down_other,
+            down_here[...],
+            down_other[...],
             here[s][:count],
             other[s][:count],
             backs[s],
@@ -256,11 +255,26 @@
             grads[s][:count],
         )
         if s == 0:
-            sums[:, :part] = grad
-            sums[:, part:] = gained
+            total[:, :part] = grad
+            total[:, part:] = gained
         else:
-            sums[:, :part] += grad
-            sums[:, part:] += gained
+            total[:, :part] += grad
+            total[:, part:] += gained
+
+
+def late_kernel(rows, *refs):
+    ins, (terms, high, rest), held, (sums, sems) = refs[:8], refs[8:11], refs[11:19], refs[19:]
+    grads, back, mask, down_here, down_other, here, other, total = held
+    count, part = here.shape
+    wait_all(
+        fetch((ins[0].at[pl.ds(grads.shape[0], grads.shape[0])],) + ins[1:], held, sems)
+    )
+    grad, up, high[...], rest[...] = source_terms(
+        down_here[...], down_other[...], here[...], other[...], back[...], mask[...], grads[:count]
+    )
+    sums[:, :part] = total[:, :part] + grad
+    sums[:, part:] = total[:, part:] + up
+    rank = sums.shape[0] // 2
     first = lax.axis_index("adapter") == 0
     for m in range(rank // rows):
         mine, theirs = sums[m * rows : (m + 1) * rows], sums[rank + m * rows : rank + (m + 1) * rows]
@@ -270,16 +284,22 @@
 
 
 def values_kernel(count, *refs):
-    ins, (highs, rests, up) = refs[:9], refs[9:12]
-    values, held, sems = refs[12:16], refs[16:25], refs[25]
-    waits = fetch(ins, held, sems)
-    wait_all(waits[:1])
-    weight = held[0]
-    for s in (1, 2, 3, 0):
-        wait_all(waits[1 + 2 * s : 3 + 2 * s])
-        here, other = held[1 + 2 * s], held[2 + 2 * s]
+    ins, values, held, sems = refs[:14], refs[14:18], refs[18:32], refs[32]
+    copies = fetch(ins, held, sems)
+    weight, up, highs, rests, high_d, rest_d = held[:6]
+    parts = held[6:]
+    wait_all(copies[:6])
+    for k, s in enumerate((3, 1, 2, 0)):
+        wait_all(copies[6 + 2 * k : 8 + 2 * k])
+        here, other = parts[2 * k], parts[1 + 2 * k]
         values[s][...] = value_of(
-            here[:count], other[:count], weight, here.shape[1], highs[s], rests[s], up[...]
+            here[:count],
+            other[:count],
+            weight,
+            here.shape[1],
+            high_d[...] if s == 3 else highs[s],
+            rest_d[...] if s == 3 else rests[s],
+            up[...],
         ).astype(values[s].dtype)
 
 
@@ -349,30 +369,50 @@
         tiled=True,
         axis_index_groups=[[2 * k + side for k in range(line)] for side in range(2)],
     )
-    grads_pairs = [grads_own, grads_y, grads_x]
-    grads_pairs += [swap(array, dc=1) for array in grads_pairs]
-    other_x, other_y = swap(part_x, dc=1), swap(part_y, dc=1)
-    part_d, other_x, other_y, *grads_pairs = lax.optimization_barrier(
-        (part_d, other_x, other_y, *grads_pairs)
-    )
-    parts = (here_own, other_own, part_x, other_x, part_y, other_y, part_d, swap(part_d, dc=1))
-    args = (*grads_pairs, *parts, down_here, down_other)
-    terms, highs, rests, up_map = call(
-        functools.partial(terms_kernel, count, rows),
+    grads = (grads_own, grads_y, grads_x)
+    parts = (here_own, other_own, part_x, swap(part_x, dc=1), part_y, swap(part_y, dc=1))
+    args = (*grads, *(swap(array, dc=1) for array in grads), *parts, down_here, down_other)
+    total, highs, rests, up_map, back_d, mask_d, down_here, down_other = call(
+        functools.partial(early_kernel, count),
+        (
+            like((2 * rank, part + features), f32),
+            like((3, 2 * rank, count), bf16),
+            like((3, 2 * rank, count), bf16),
+            like((2 * rank, features), bf16),
+            like((2 * rank, count), bf16),
+            like((2 * rank, count), f32),
+            like((2 * rank, part), bf16),
+            like((2 * rank, part), bf16),
+        ),
+        args,
+        scratch=[pltpu.VMEM(array.shape, array.dtype) for array in args]
+        + [pltpu.SemaphoreType.DMA((len(args),))],
+    )
+    part_d, total = lax.optimization_barrier((part_d, total))
+    parts_d = (part_d, swap(part_d, dc=1))
+    args = (grads_x, back_d, mask_d, down_here, down_other, *parts_d, total)
+    terms, high_d, rest_d = call(
+        functools.partial(late_kernel, rows),
         (
             like((2 * rank, part + features), bf16),
-            like((4, 2 * rank, count), bf16),
-            like((4, 2 * rank, count), bf16),
-            like((2 * rank, features), bf16),
+            like((2 * rank, count), bf16),
+            like((2 * rank, count), bf16),
         ),
         args,
-        scratch=[pltpu.VMEM(arg.shape, arg.dtype) for arg in args]
-        + [
-            pltpu.VMEM((2 * rank, part + features), f32),
-            pltpu.SemaphoreType.DMA((2 * len(args),)),
-        ],
+        scratch=[pltpu.VMEM((padded, features), bf16)]
+        + [pltpu.VMEM(array.shape, array.dtype) for array in args[1:]]
+        + [pltpu.VMEM(total.shape, f32), pltpu.SemaphoreType.DMA((len(args),))],
     )
     gathered = lax.all_to_all(terms, ("dp", "adapter"), split_axis=0, concat_axis=0, tiled=True)
+    args = (weight, up_map, highs, rests, high_d, rest_d, *parts_d, *parts[2:], *parts[:2])
+    value, value_x, value_y, value_d = call(
+        functools.partial(values_kernel, count),
+        (like((count, features), f32),) + (like((count, features), bf16),) * 3,
+        args,
+        scratch=[pltpu.VMEM(array.shape, array.dtype) for array in args]
+        + [pltpu.SemaphoreType.DMA((len(args),))],
+    )
+    value_x, value_y, value_d = swap(value_x, dx=1), swap(value_y, dy=1), swap(value_d, dx=1, dy=1)
     gathered = gathered.reshape(line, 2, 2, rows, part + features)
     sums = jnp.sum(gathered.astype(f32), axis=0)
     up_gradient = jnp.sum(sums[..., part:], axis=(0, 1))[None]
@@ -385,20 +425,9 @@
         ],
         axis=1,
     )[None]
-    args = (weight, *parts)
-    value, value_x, value_y, value_d = call(
-        functools.partial(values_kernel, count),
-        (like((count, features), f32),) + (like((count, features), bf16),) * 3,
-        args + (highs, rests, up_map),
-        scratch=[pltpu.VMEM(arg.shape, arg.dtype) for arg in args]
-        + [pltpu.SemaphoreType.DMA((2 * len(args),))],
-        held=(9, 10, 11),
-    )
+    value_x, value_y, value_d, grad_a = lax.optimization_barrier((value_x, value_y, value_d, grad_a))
     projected = (
-        value
-        + swap(value_x, dx=1).astype(f32)
-        + swap(value_y, dy=1).astype(f32)
-        + swap(value_d, dx=1, dy=1).astype(f32)
+        value + value_x.astype(f32) + value_y.astype(f32) + value_d.astype(f32)
     ).astype(bf16)
     return projected, grad_a, up_gradient
 

time: 73.4 us -> 67.8 us (0.924)
  waiting for transfers between devices: 23.1 us -> 16.3 us
  Pallas kernels: 17.3 us -> 18.7 us
    ppermute x14, waiting for transfers between devices: 23.1 us -> 13.6 us  [swap(): return lax.ppermute(array, AXES, pairs)]
    all_to_all x1, waiting for transfers between devices: 0.01 us -> 2.73 us  [by_width(): lax.all_to_all(terms, ('dp', 'adapter'), split_axis=0, concat_axis=0, til...]
    pallas_call x4 -> x5, Pallas kernels: 17.3 us -> 18.7 us  [call(): pl.pallas_call(kernel, out_shape=outs, in_specs=[VMEM if k in held else H...]
  transfers between devices with their start and end apart: 16 -> 16, of which waited for: 10 -> 9; matrix products, arithmetic and copies ran while one was open for 4% -> 3% of each run, Pallas kernels for 20% -> 24%
where the time goes in v3:
time: 67.8 us; the launch traced here: 67.4 us
  starting transfers between devices  26.1 us (38%)
  Pallas kernels  18.7 us (28%)
  waiting for transfers between devices  16.3 us (24%)
  local copies, waits for them, and re-layouts  2.97 us (4%)
  other arithmetic  2.33 us (3%)
  between operations  0.92 us (1%)
    pallas_call x5, Pallas kernels, call(): pl.pallas_call(kernel, out_shape=outs, in_specs=[VMEM if k in held else H...  18.7 us
    ppermute x14, starting transfers between devices, swap(): return lax.ppermute(array, AXES, pairs)  14.6 us
    ppermute x14, waiting for transfers between devices, swap(): return lax.ppermute(array, AXES, pairs)  13.6 us
    all_to_all x1, starting transfers between devices, by_width(): lax.all_to_all(terms, ('dp', 'adapter'), split_axis=0, concat_axis=0, til...  6.62 us
    all_to_all x1, starting transfers between devices, by_width(): lax.all_to_all(jnp.tile(own_weight, (line, 1)), 'dp', split_axis=0, conca...  4.87 us
    all_to_all x1, waiting for transfers between devices, by_width(): lax.all_to_all(terms, ('dp', 'adapter'), split_axis=0, concat_axis=0, til...  2.73 us
    unnamed x39, local copies, waits for them, and re-layouts  1.89 us
    convert_element_type x1, other arithmetic, by_width(): projected = (value + value_x.astype(f32) + value_y.astype(f32) + value_d....  1.64 us
  transfers between devices with their start and end apart: 16, of which 9 were waited for; matrix products, arithmetic and copies ran while one was open for 3% of the time, Pallas kernels for 24%

profile of v3, /device:TPU:0, one launch (start us, length us, event | category | flops | bytes accessed | tf_op | source)
XLA Modules:
  0.0 67.4 jit_solution(6461732541712344070)
XLA Ops:
  0.6 0.0 copy-start
  0.6 2.6 %shard_map.85 = (bf16[216,1024]{1,0:T(8,128)(2,1)}, bf16[288,256]{1,0:T(8,128)(2,1)}) custom-call(bf16[216,8192]{1,0:T(8,128)(2,1)} %tokens.3, s32[1,216]{1,0:T(1,128)} %bitcast.48, bf16[64,256]{1,0:T(8,128)(2,1)} %bitcast.45, bf16[216,256]{1,0:T(8,128)(2,1)} %cotangent.1), custom_call_target="tpu_custom_call" | custom-call | flops 1000 | bytes 1000 | tf_op jit(solution)/shard_map/pallas_call | solution.py:85
  3.3 3.0 %collective-permute-start.1 = (bf16[288,256]{1,0:T(8,128)(2,1)}, bf16[288,256]{1,0:T(8,128)(2,1)S(1)}, u32[]{:S(2)}, u32[]{:S(2)}) collective-permute-start(bf16[288,256]{1,0:T(8,128)(2,1)} %get-tuple-element.42.refs_0_), channel_id=1, source_target_pairs={{0,2},{1,3},{2,0},{3,1},{4,6},{5,7},{6,4},{7,5},{8,10},{9,11},{10,... | collective-permute-start | bytes 442376 | tf_op jit(solution)/shard_map/ppermute | solution.py:326
  6.3 1.5 %collective-permute-start = (bf16[216,1024]{1,0:T(8,128)(2,1)}, bf16[216,1024]{1,0:T(8,128)(2,1)S(1)}, u32[]{:S(2)}, u32[]{:S(2)}) collective-permute-start(bf16[216,1024]{1,0:T(8,128)(2,1)} %get-tuple-element.44), channel_id=1, source_target_pairs={{0,4},{1,5},{2,6},{3,7},{4,0},{5,1},{6,2},{7,3},{8,12},{9,13},{10,... | collective-permute-start | bytes 1327112 | tf_op jit(solution)/shard_map/ppermute | solution.py:326
  7.8 2.6 %shard_map.86 = (bf16[280,1024]{1,0:T(8,128)(2,1)}, bf16[216,1024]{1,0:T(8,128)(2,1)}, bf16[216,1024]{1,0:T(8,128)(2,1)}, bf16[216,1024]{1,0:T(8,128)(2,1)}, bf1...) custom-call(bf16[216,8192]{1,0:T(8,128)(2,1)} %tokens.3, bf16[64,8192]{1,0:T(8,128)(2,1)} %bitcast.43), custom_call_target="tpu_custom_call" | custom-call | flops 1000 | bytes 1000 | tf_op jit(solution)/shard_map/pallas_call | solution.py:85
  10.4 0.0 collective-permute-done.1.refs_1_
  10.5 0.0 copy-start.10
  10.5 1.6 %collective-permute-start.2 = (bf16[280,1024]{1,0:T(8,128)(2,1)}, bf16[280,1024]{1,0:T(8,128)(2,1)S(1)}, u32[]{:S(2)}, u32[]{:S(2)}) collective-permute-start(bf16[280,1024]{1,0:T(8,128)(2,1)} %get-tuple-element.51), channel_id=1, source_target_pairs={{0,2},{1,3},{2,0},{3,1},{4,6},{5,7},{6,4},{7,5},{8,10},{9,11},{10,... | collective-permute-start | bytes 1720328 | tf_op jit(solution)/shard_map/ppermute | solution.py:326
  12.1 1.0 %tile.2 = bf16[4,512,256]{2,1,0:T(8,128)(2,1)} broadcast(bf16[512,256]{1,0:T(8,128)(2,1)S(1)} %constant_dynamic-slice_fusion), dimensions={1,2} | broadcast | bytes 1310720 | tf_op jit(solution)/shard_map/tile | solution.py:365
  13.2 4.9 %all-to-all-start = ((bf16[4,512,256]{2,1,0:T(8,128)(2,1)}), bf16[4,512,256]{2,1,0:T(8,128)(2,1)S(1)}, u32[]{:S(2)}, u32[]{:S(2)}) async-start(bf16[4,512,256]{2,1,0:T(8,128)(2,1)} %tile.2), calls=%async_computation | async-start | bytes 2097152 | tf_op jit(solution)/shard_map/all_to_all | solution.py:364
  18.1 0.1 collective-permute-done.refs_8_
  18.2 1.6 %collective-permute-start.3 = (bf16[448,256]{1,0:T(8,128)(2,1)S(1)}, bf16[448,256]{1,0:T(8,128)(2,1)S(1)}, u32[]{:S(2)}, u32[]{:S(2)}) collective-permute-start(bf16[448,256]{1,0:T(8,128)(2,1)S(1)} %pad_maximum_fusion), channel_id=1, source_target_pairs={{0,4},{1,5},{2,6},{3,7},{4,0},{5,1},{6,2},{7,3},{8,12},{9,13},{10,... | collective-permute-start | bytes 688136 | tf_op jit(solution)/shard_map/ppermute | solution.py:326
  19.7 4.7 %collective-permute-done.3.refs_2_.refs_0_ = bf16[448,256]{1,0:T(8,128)(2,1)S(1)} collective-permute-done((bf16[448,256]{1,0:T(8,128)(2,1)S(1)}, bf16[448,256]{1,0:T(8,128)(2,1)S(1)}, u32[]{:S(2)}, u32[]{:S(2)}) %collective-permute-start.3) | collective-permute-done | bytes 229408 | tf_op jit(solution)/shard_map/ppermute | solution.py:326
  24.4 0.5 collective-permute-done.2.refs_10_
  24.9 0.0 collective-permute-start.8
  24.9 0.5 collective-permute-start.7
  25.4 2.2 %collective-permute-start.9 = (bf16[216,1024]{1,0:T(8,128)(2,1)S(1)}, bf16[216,1024]{1,0:T(8,128)(2,1)S(1)}, u32[]{:S(2)}, u32[]{:S(2)}) collective-permute-start(bf16[216,1024]{1,0:T(8,128)(2,1)S(1)} %copy-done.15), channel_id=1, source_target_pairs={{0,6},{1,7},{2,4},{3,5},{4,2},{5,3},{6,0},{7,1},{8,14},{9,15},{10,... | collective-permute-start | bytes 1327112 | tf_op jit(solution)/shard_map/ppermute | solution.py:326
  27.6 0.0 collective-permute-start.4
  27.6 0.5 collective-permute-start.6
  28.1 0.9 %collective-permute-done.4.refs_3_ = bf16[288,256]{1,0:T(8,128)(2,1)S(1)} collective-permute-done((bf16[288,256]{1,0:T(8,128)(2,1)S(1)}, bf16[288,256]{1,0:T(8,128)(2,1)S(1)}, u32[]{:S(2)}, u32[]{:S(2)}) %collective-permute-start.4) | collective-permute-done | bytes 147488 | tf_op jit(solution)/shard_map/ppermute | solution.py:326
  29.0 0.1 collective-permute-start.5
  29.1 1.2 %collective-permute-done.5.refs_4_ = bf16[288,256]{1,0:T(8,128)(2,1)S(1)} collective-permute-done((bf16[288,256]{1,0:T(8,128)(2,1)S(1)}, bf16[288,256]{1,0:T(8,128)(2,1)S(1)}, u32[]{:S(2)}, u32[]{:S(2)}) %collective-permute-start.5) | collective-permute-done | bytes 147488 | tf_op jit(solution)/shard_map/ppermute | solution.py:326
  30.4 0.0 collective-permute-done.6.refs_5_
  30.4 0.0 collective-permute-done.7.refs_9_
  30.4 0.0 collective-permute-done.8.refs_11_
  30.4 0.6 copy-done.13
  31.0 0.1 copy-done.11
  31.1 0.2 copy-done.5
  31.3 0.2 copy-done.3
  31.5 4.9 %shard_map.87 = (f32[128,1280]{1,0:T(8,128)}, bf16[3,128,216]{2,1,0:T(8,128)(2,1)}, bf16[3,128,216]{2,1,0:T(8,128)(2,1)}, bf16[128,256]{1,0:T(8,128)(2,1)}, bf16...) custom-call(bf16[288,256]{1,0:T(8,128)(2,1)} %get-tuple-element.42.refs_0_, ...), custom_call_target="tpu_custom_call" | custom-call | flops 1000 | bytes 1000 | tf_op jit(solution)/shard_map/pallas_call | solution.py:85
  36.4 2.0 %collective-permute-done.9.refs_5_.refs_6_ = bf16[216,1024]{1,0:T(8,128)(2,1)S(1)} collective-permute-done((bf16[216,1024]{1,0:T(8,128)(2,1)S(1)}, bf16[216,1024]{1,0:T(8,128)(2,1)S(1)}, u32[]{:S(2)}, u32[]{:S(2)}) %collective-permute-start.9) | collective-permute-done | bytes 442400 | tf_op jit(solution)/shard_map/ppermute | solution.py:326
  38.4 0.0 collective-permute-start.10
  38.4 1.8 %collective-permute-done.10.refs_6_.refs_7_ = bf16[216,1024]{1,0:T(8,128)(2,1)S(1)} collective-permute-done((bf16[216,1024]{1,0:T(8,128)(2,1)S(1)}, bf16[216,1024]{1,0:T(8,128)(2,1)S(1)}, u32[]{:S(2)}, u32[]{:S(2)}) %collective-permute-start.10) | collective-permute-done | bytes 442400 | tf_op jit(solution)/shard_map/ppermute | solution.py:326
  40.2 0.8 %copy-done.7 = bf16[216,1024]{1,0:T(8,128)(2,1)} copy-done((bf16[216,1024]{1,0:T(8,128)(2,1)}, bf16[216,1024]{1,0:T(8,128)(2,1)S(1)}, u32[]{:S(2)}) %copy-start.7) | copy-done | bytes 442392
  41.0 3.1 %shard_map.88 = (bf16[128,1280]{1,0:T(8,128)(2,1)}, bf16[128,216]{1,0:T(8,128)(2,1)}, bf16[128,216]{1,0:T(8,128)(2,1)}) custom-call(bf16[448,256]{1,0:T(8,128)(2,1)} %copy-done.8, bf16[128,216]{1,0:T(8,128)(2,1)} %get-tuple-element.62.refs_1_, f32[128,216]{1,0:T(8,128)} %get-tuple-element.63.refs_2_, bf16[128,1024]{1,0:T(8,128)(2,1)} %get-tuple-element.64.refs_3_, ...), custom_call_target="tpu_custom_call" | custom-call | flops 1000 | bytes 1000 | tf_op jit(solution)/shard_map/pallas_call | solution.py:85
  44.1 0.0 all-to-all-done
  44.1 6.6 %all-to-all-start.1 = ((bf16[16,8,1280]{2,1,0:T(8,128)(2,1)}), bf16[16,8,1280]{2,1,0:T(8,128)(2,1)S(1)}, u32[]{:S(2)}, u32[]{:S(2)}) async-start(bf16[16,8,1280]{2,1,0:T(8,128)(2,1)} %bitcast.44), calls=%async_computation.1 | async-start | bytes 655360 | tf_op jit(solution)/shard_map/all_to_all | solution.py:406
  50.8 5.4 %shard_map.89 = (f32[216,256]{1,0:T(8,128)}, bf16[216,256]{1,0:T(8,128)(2,1)}, bf16[216,256]{1,0:T(8,128)(2,1)}, bf16[216,256]{1,0:T(8,128)(2,1)}) custom-call(bf16[2048,256]{1,0:T(8,128)(2,1)} %bitcast.41, bf16[128,256]{1,0:T(8,128)(2,1)} %get-tuple-element.59.refs_1_, bf16[3,128,216]{2,1,0:T(8,128)(2,1)} %get-tuple-element.60.refs_2_, ...), custom_call_target="tpu_custom_call" | custom-call | flops 1000 | bytes 1000 | tf_op jit(solution)/shard_map/pallas_call | solution.py:85
  56.2 2.0 %collective-permute-start.11 = (bf16[216,256]{1,0:T(8,128)(2,1)}, bf16[216,256]{1,0:T(8,128)(2,1)S(1)}, u32[]{:S(2)}, u32[]{:S(2)}) collective-permute-start(bf16[216,256]{1,0:T(8,128)(2,1)} %get-tuple-element.73), channel_id=1, source_target_pairs={{0,4},{1,5},{2,6},{3,7},{4,0},{5,1},{6,2},{7,3},{8,12},{9,13},{10,... | collective-permute-start | bytes 331784 | tf_op jit(solution)/shard_map/ppermute | solution.py:326
  58.2 1.5 %collective-permute-start.12 = (bf16[216,256]{1,0:T(8,128)(2,1)}, bf16[216,256]{1,0:T(8,128)(2,1)S(1)}, u32[]{:S(2)}, u32[]{:S(2)}) collective-permute-start(bf16[216,256]{1,0:T(8,128)(2,1)} %get-tuple-element.74), channel_id=1, source_target_pairs={{0,2},{1,3},{2,0},{3,1},{4,6},{5,7},{6,4},{7,5},{8,10},{9,11},{10,... | collective-permute-start | bytes 331784 | tf_op jit(solution)/shard_map/ppermute | solution.py:326
  59.7 0.1 collective-permute-start.13
  59.8 2.7 %all-to-all-done.1 = bf16[16,8,1280]{2,1,0:T(8,128)(2,1)S(1)} async-done(((bf16[16,8,1280]{2,1,0:T(8,128)(2,1)}), bf16[16,8,1280]{2,1,0:T(8,128)(2,1)S(1)}, u32[]{:S(2)}, u32[]{:S(2)}) %all-to-all-start.1) | async-done | bytes 327712 | tf_op jit(solution)/shard_map/all_to_all | solution.py:406
  62.6 0.0 copy-start.14
  62.6 0.6 slice_reduce_fusion
  63.3 0.0 collective-permute-done.11
  63.3 2.5 %collective-permute-done.12 = bf16[216,256]{1,0:T(8,128)(2,1)S(1)} collective-permute-done((bf16[216,256]{1,0:T(8,128)(2,1)}, bf16[216,256]{1,0:T(8,128)(2,1)S(1)}, u32[]{:S(2)}, u32[]{:S(2)}) %collective-permute-start.12) | collective-permute-done | bytes 110624 | tf_op jit(solution)/shard_map/ppermute | solution.py:326
  65.7 0.0 collective-permute-done.13
  65.7 1.6 %add_convert_fusion = bf16[216,256]{1,0:T(8,128)(2,1)} fusion(bf16[216,256]{1,0:T(8,128)(2,1)S(1)} %collective-permute-done.13, bf16[216,256]{1,0:T(8,128)(2,1)S(1)} %collective-permute-done.12, f32[216,256]{1,0:T(8,128)} %get-tuple-element.72, bf16[216,256]{1,0:T(8,128)(2,1)S(1)} %collective-permute-done.11), kind=kLoop, calls=%fused_computation.2 | loop fusion | flops 387072 | bytes 663552 | tf_op jit(solution)/shard_map/convert_element_type | solution.py:431
  (37 shorter events, 0.2 us)
Async XLA Ops:
  0.6 11.5 %copy-start = (bf16[1024,256]{1,0:T(8,128)(2,1)S(1)}, bf16[1024,256]{1,0:T(8,128)(2,1)}, u32[]{:S(2)}) copy-start(bf16[1024,256]{1,0:T(8,128)(2,1)} %param.7) | copy-start | bytes 1572868
  3.3 7.2 %collective-permute-start.1 = (bf16[288,256]{1,0:T(8,128)(2,1)}, bf16[288,256]{1,0:T(8,128)(2,1)S(1)}, u32[]{:S(2)}, u32[]{:S(2)}) collective-permute-start(bf16[288,256]{1,0:T(8,128)(2,1)} %get-tuple-element.42.refs_0_), channel_id=1, source_target_pairs={{0,2},{1,3},{2,0},{3,1},{4,6},{5,7},{6,4},{7,5},{8,10},{9,11},{10,... | collective-permute-start | bytes 442376 | tf_op jit(solution)/shard_map/ppermute | solution.py:326
  6.3 11.7 %copy-start.9 = (bf16[288,256]{1,0:T(8,128)(2,1)S(1)}, bf16[288,256]{1,0:T(8,128)(2,1)}, u32[]{:S(2)}) copy-start(bf16[288,256]{1,0:T(8,128)(2,1)} %get-tuple-element.42.refs_0_) | copy-start | bytes 442372
  6.3 11.8 %collective-permute-start = (bf16[216,1024]{1,0:T(8,128)(2,1)}, bf16[216,1024]{1,0:T(8,128)(2,1)S(1)}, u32[]{:S(2)}, u32[]{:S(2)}) collective-permute-start(bf16[216,1024]{1,0:T(8,128)(2,1)} %get-tuple-element.44), channel_id=1, source_target_pairs={{0,4},{1,5},{2,6},{3,7},{4,0},{5,1},{6,2},{7,3},{8,12},{9,13},{10,... | collective-permute-start | bytes 1327112 | tf_op jit(solution)/shard_map/ppermute | solution.py:326
  10.4 15.0 %copy-start.15 = (bf16[216,1024]{1,0:T(8,128)(2,1)S(1)}, bf16[216,1024]{1,0:T(8,128)(2,1)}, u32[]{:S(2)}) copy-start(bf16[216,1024]{1,0:T(8,128)(2,1)} %get-tuple-element.66) | copy-start | bytes 1327108
  10.5 19.9 %copy-start.10 = (bf16[288,256]{1,0:T(8,128)(2,1)}, bf16[288,256]{1,0:T(8,128)(2,1)S(1)}, u32[]{:S(2)}) copy-start(bf16[288,256]{1,0:T(8,128)(2,1)S(1)} %collective-permute-done.1.refs_1_) | copy-start | bytes 442372
  10.5 14.4 %collective-permute-start.2 = (bf16[280,1024]{1,0:T(8,128)(2,1)}, bf16[280,1024]{1,0:T(8,128)(2,1)S(1)}, u32[]{:S(2)}, u32[]{:S(2)}) collective-permute-start(bf16[280,1024]{1,0:T(8,128)(2,1)} %get-tuple-element.51), channel_id=1, source_target_pairs={{0,2},{1,3},{2,0},{3,1},{4,6},{5,7},{6,4},{7,5},{8,10},{9,11},{10,... | collective-permute-start | bytes 1720328 | tf_op jit(solution)/shard_map/ppermute | solution.py:326
  13.2 30.9 %all-to-all-start = ((bf16[4,512,256]{2,1,0:T(8,128)(2,1)}), bf16[4,512,256]{2,1,0:T(8,128)(2,1)S(1)}, u32[]{:S(2)}, u32[]{:S(2)}) async-start(bf16[4,512,256]{2,1,0:T(8,128)(2,1)} %tile.2), calls=%async_computation | async-start | bytes 2097152 | tf_op jit(solution)/shard_map/all_to_all | solution.py:364
  18.1 12.3 %copy-start.4 = (bf16[216,1024]{1,0:T(8,128)(2,1)}, bf16[216,1024]{1,0:T(8,128)(2,1)S(1)}, u32[]{:S(2)}) copy-start(bf16[216,1024]{1,0:T(8,128)(2,1)S(1)} %collective-permute-done.refs_8_) | copy-start | bytes 1327108
  18.2 6.2 %collective-permute-start.3 = (bf16[448,256]{1,0:T(8,128)(2,1)S(1)}, bf16[448,256]{1,0:T(8,128)(2,1)S(1)}, u32[]{:S(2)}, u32[]{:S(2)}) collective-permute-start(bf16[448,256]{1,0:T(8,128)(2,1)S(1)} %pad_maximum_fusion), channel_id=1, source_target_pairs={{0,4},{1,5},{2,6},{3,7},{4,0},{5,1},{6,2},{7,3},{8,12},{9,13},{10,... | collective-permute-start | bytes 688136 | tf_op jit(solution)/shard_map/ppermute | solution.py:326
  24.4 6.0 %copy-start.8 = (bf16[448,256]{1,0:T(8,128)(2,1)}, bf16[448,256]{1,0:T(8,128)(2,1)S(1)}, u32[]{:S(2)}) copy-start(bf16[448,256]{1,0:T(8,128)(2,1)S(1)} %collective-permute-done.3.refs_2_.refs_0_) | copy-start | bytes 688132
  24.9 5.5 %copy-start.2 = (bf16[280,1024]{1,0:T(8,128)(2,1)}, bf16[280,1024]{1,0:T(8,128)(2,1)S(1)}, u32[]{:S(2)}) copy-start(bf16[280,1024]{1,0:T(8,128)(2,1)S(1)} %collective-permute-done.2.refs_10_) | copy-start | bytes 1720324
  24.9 5.5 %collective-permute-start.8 = (bf16[280,1024]{1,0:T(8,128)(2,1)S(1)}, bf16[280,1024]{1,0:T(8,128)(2,1)S(1)}, u32[]{:S(2)}, u32[]{:S(2)}) collective-permute-start(bf16[280,1024]{1,0:T(8,128)(2,1)S(1)} %collective-permute-done.2.refs_10_), channel_id=1, source_target_pairs={{0,1},{1,0},{2,3},{3,2},{4,5},{5,4},{6,7},{7,6},{8,9},{9,8},{10,11... | collective-permute-start | bytes 1720328 | tf_op jit(solution)/shard_map/ppermute | solution.py:326
  24.9 5.5 %collective-permute-start.7 = (bf16[216,1024]{1,0:T(8,128)(2,1)S(1)}, bf16[216,1024]{1,0:T(8,128)(2,1)S(1)}, u32[]{:S(2)}, u32[]{:S(2)}) collective-permute-start(bf16[216,1024]{1,0:T(8,128)(2,1)S(1)} %collective-permute-done.refs_8_), channel_id=1, source_target_pairs={{0,1},{1,0},{2,3},{3,2},{4,5},{5,4},{6,7},{7,6},{8,9},{9,8},{10,11... | collective-permute-start | bytes 1327112 | tf_op jit(solution)/shard_map/ppermute | solution.py:326
  25.4 13.0 %collective-permute-start.9 = (bf16[216,1024]{1,0:T(8,128)(2,1)S(1)}, bf16[216,1024]{1,0:T(8,128)(2,1)S(1)}, u32[]{:S(2)}, u32[]{:S(2)}) collective-permute-start(bf16[216,1024]{1,0:T(8,128)(2,1)S(1)} %copy-done.15), channel_id=1, source_target_pairs={{0,6},{1,7},{2,4},{3,5},{4,2},{5,3},{6,0},{7,1},{8,14},{9,15},{10,... | collective-permute-start | bytes 1327112 | tf_op jit(solution)/shard_map/ppermute | solution.py:326
  27.6 1.4 %collective-permute-start.4 = (bf16[288,256]{1,0:T(8,128)(2,1)S(1)}, bf16[288,256]{1,0:T(8,128)(2,1)S(1)}, u32[]{:S(2)}, u32[]{:S(2)}) collective-permute-start(bf16[288,256]{1,0:T(8,128)(2,1)S(1)} %copy-done.9), channel_id=1, source_target_pairs={{0,1},{1,0},{2,3},{3,2},{4,5},{5,4},{6,7},{7,6},{8,9},{9,8},{10,11... | collective-permute-start | bytes 442376 | tf_op jit(solution)/shard_map/ppermute | solution.py:326
  27.6 2.7 %collective-permute-start.6 = (bf16[448,256]{1,0:T(8,128)(2,1)S(1)}, bf16[448,256]{1,0:T(8,128)(2,1)S(1)}, u32[]{:S(2)}, u32[]{:S(2)}) collective-permute-start(bf16[448,256]{1,0:T(8,128)(2,1)S(1)} %collective-permute-done.3.refs_2_.refs_0_), channel_id=1, source_target_pairs={{0,1},{1,0},{2,3},{3,2},{4,5},{5,4},{6,7},{7,6},{8,9},{9,8},{10,11... | collective-permute-start | bytes 688136 | tf_op jit(solution)/shard_map/ppermute | solution.py:326
  29.0 1.5 %copy-start.12 = (bf16[288,256]{1,0:T(8,128)(2,1)}, bf16[288,256]{1,0:T(8,128)(2,1)S(1)}, u32[]{:S(2)}) copy-start(bf16[288,256]{1,0:T(8,128)(2,1)S(1)} %collective-permute-done.4.refs_3_) | copy-start | bytes 442372
  29.0 1.4 %collective-permute-start.5 = (bf16[288,256]{1,0:T(8,128)(2,1)S(1)}, bf16[288,256]{1,0:T(8,128)(2,1)S(1)}, u32[]{:S(2)}, u32[]{:S(2)}) collective-permute-start(bf16[288,256]{1,0:T(8,128)(2,1)S(1)} %collective-permute-done.1.refs_1_), channel_id=1, source_target_pairs={{0,1},{1,0},{2,3},{3,2},{4,5},{5,4},{6,7},{7,6},{8,9},{9,8},{10,11... | collective-permute-start | bytes 442376 | tf_op jit(solution)/shard_map/ppermute | solution.py:326
  30.4 0.7 copy-start.13
  30.4 0.7 %copy-start.11 = (bf16[448,256]{1,0:T(8,128)(2,1)}, bf16[448,256]{1,0:T(8,128)(2,1)S(1)}, u32[]{:S(2)}) copy-start(bf16[448,256]{1,0:T(8,128)(2,1)S(1)} %collective-permute-done.6.refs_5_) | copy-start | bytes 688132
  30.4 0.9 %copy-start.5 = (bf16[216,1024]{1,0:T(8,128)(2,1)}, bf16[216,1024]{1,0:T(8,128)(2,1)S(1)}, u32[]{:S(2)}) copy-start(bf16[216,1024]{1,0:T(8,128)(2,1)S(1)} %collective-permute-done.7.refs_9_) | copy-start | bytes 1327108
  30.4 1.1 %copy-start.3 = (bf16[280,1024]{1,0:T(8,128)(2,1)}, bf16[280,1024]{1,0:T(8,128)(2,1)S(1)}, u32[]{:S(2)}) copy-start(bf16[280,1024]{1,0:T(8,128)(2,1)S(1)} %collective-permute-done.8.refs_11_) | copy-start | bytes 1720324
  38.4 1.8 %copy-start.6 = (bf16[216,1024]{1,0:T(8,128)(2,1)}, bf16[216,1024]{1,0:T(8,128)(2,1)S(1)}, u32[]{:S(2)}) copy-start(bf16[216,1024]{1,0:T(8,128)(2,1)S(1)} %collective-permute-done.9.refs_5_.refs_6_) | copy-start | bytes 1327108
  38.4 1.8 %collective-permute-start.10 = (bf16[216,1024]{1,0:T(8,128)(2,1)S(1)}, bf16[216,1024]{1,0:T(8,128)(2,1)S(1)}, u32[]{:S(2)}, u32[]{:S(2)}) collective-permute-start(bf16[216,1024]{1,0:T(8,128)(2,1)S(1)} %collective-permute-done.9.refs_5_.refs_6_), channel_id=1, source_target_pairs={{0,1},{1,0},{2,3},{3,2},{4,5},{5,4},{6,7},{7,6},{8,9},{9,8},{10,11... | collective-permute-start | bytes 1327112 | tf_op jit(solution)/shard_map/ppermute | solution.py:326
  40.2 0.8 %copy-start.7 = (bf16[216,1024]{1,0:T(8,128)(2,1)}, bf16[216,1024]{1,0:T(8,128)(2,1)S(1)}, u32[]{:S(2)}) copy-start(bf16[216,1024]{1,0:T(8,128)(2,1)S(1)} %collective-permute-done.10.refs_6_.refs_7_) | copy-start | bytes 1327108
  44.1 6.6 %copy-start.1 = (bf16[4,512,256]{2,1,0:T(8,128)(2,1)}, bf16[4,512,256]{2,1,0:T(8,128)(2,1)S(1)}, u32[]{:S(2)}) copy-start(bf16[4,512,256]{2,1,0:T(8,128)(2,1)S(1)} %all-to-all-done) | copy-start | bytes 3145732
  44.1 18.4 %all-to-all-start.1 = ((bf16[16,8,1280]{2,1,0:T(8,128)(2,1)}), bf16[16,8,1280]{2,1,0:T(8,128)(2,1)S(1)}, u32[]{:S(2)}, u32[]{:S(2)}) async-start(bf16[16,8,1280]{2,1,0:T(8,128)(2,1)} %bitcast.44), calls=%async_computation.1 | async-start | bytes 655360 | tf_op jit(solution)/shard_map/all_to_all | solution.py:406
  56.2 7.1 %collective-permute-start.11 = (bf16[216,256]{1,0:T(8,128)(2,1)}, bf16[216,256]{1,0:T(8,128)(2,1)S(1)}, u32[]{:S(2)}, u32[]{:S(2)}) collective-permute-start(bf16[216,256]{1,0:T(8,128)(2,1)} %get-tuple-element.73), channel_id=1, source_target_pairs={{0,4},{1,5},{2,6},{3,7},{4,0},{5,1},{6,2},{7,3},{8,12},{9,13},{10,... | collective-permute-start | bytes 331784 | tf_op jit(solution)/shard_map/ppermute | solution.py:326
  58.2 7.5 %collective-permute-start.12 = (bf16[216,256]{1,0:T(8,128)(2,1)}, bf16[216,256]{1,0:T(8,128)(2,1)S(1)}, u32[]{:S(2)}, u32[]{:S(2)}) collective-permute-start(bf16[216,256]{1,0:T(8,128)(2,1)} %get-tuple-element.74), channel_id=1, source_target_pairs={{0,2},{1,3},{2,0},{3,1},{4,6},{5,7},{6,4},{7,5},{8,10},{9,11},{10,... | collective-permute-start | bytes 331784 | tf_op jit(solution)/shard_map/ppermute | solution.py:326
  59.7 6.1 %collective-permute-start.13 = (bf16[216,256]{1,0:T(8,128)(2,1)}, bf16[216,256]{1,0:T(8,128)(2,1)S(1)}, u32[]{:S(2)}, u32[]{:S(2)}) collective-permute-start(bf16[216,256]{1,0:T(8,128)(2,1)} %get-tuple-element.75), channel_id=1, source_target_pairs={{0,6},{1,7},{2,4},{3,5},{4,2},{5,3},{6,0},{7,1},{8,14},{9,15},{10,... | collective-permute-start | bytes 331784 | tf_op jit(solution)/shard_map/ppermute | solution.py:326
  62.6 4.7 %copy-start.14 = (f32[8,4096]{1,0:T(8,128)}, f32[8,4096]{1,0:T(8,128)S(1)}, u32[]{:S(2)}) copy-start(f32[8,4096]{1,0:T(8,128)S(1)} %constant_dynamic-update-slice_fusion) | copy-start | bytes 393220

commit v4 on v3

--- a/solution.py
+++ b/solution.py
@@ -360,7 +360,11 @@
     part_x, send_d, grads_y = lax.optimization_barrier((part_x, send_d, grads_y))
     grads_x = swap(jnp.concatenate([grads_own[:padded], grads_y[:padded]], axis=0), dx=1)
     part_d = swap(send_d, dx=1, dy=1)
-    part_x, part_y, grads_x = lax.optimization_barrier((part_x, part_y, grads_x))
+    part_x, own_again, y_again = lax.optimization_barrier((part_x, grads_own, grads_y))
+    grads_own2, grads_y2 = swap(own_again, dc=1), swap(y_again, dc=1)
+    part_x, part_y, grads_x, grads_own2, grads_y2 = lax.optimization_barrier(
+        (part_x, part_y, grads_x, grads_own2, grads_y2)
+    )
     weight = lax.all_to_all(
         jnp.tile(own_weight, (line, 1)),
         "dp",
@@ -371,7 +375,8 @@
     )
     grads = (grads_own, grads_y, grads_x)
     parts = (here_own, other_own, part_x, swap(part_x, dc=1), part_y, swap(part_y, dc=1))
-    args = (*grads, *(swap(array, dc=1) for array in grads), *parts, down_here, down_other)
+    grads += (grads_own2, grads_y2, swap(grads_x, dc=1))
+    args = (*grads, *parts, down_here, down_other)
     total, highs, rests, up_map, back_d, mask_d, down_here, down_other = call(
         functools.partial(early_kernel, count),
         (

time: 67.8 us -> 67.8 us (level)
  transfers between devices with their start and end apart: 16 -> 16, of which waited for: 9 -> 10; matrix products, arithmetic and copies ran while one was open for 3% -> 3% of each run, Pallas kernels for 24% -> 24%
where the time goes in v4:
time: 67.8 us; the launch traced here: 67.4 us
  starting transfers between devices  26 us (38%)
  Pallas kernels  18.7 us (28%)
  waiting for transfers between devices  16.5 us (24%)
  local copies, waits for them, and re-layouts  2.93 us (4%)
  other arithmetic  2.33 us (3%)
  between operations  0.92 us (1%)
    pallas_call x5, Pallas kernels, call(): pl.pallas_call(kernel, out_shape=outs, in_specs=[VMEM if k in held else H...  18.7 us
    ppermute x14, starting transfers between devices, swap(): return lax.ppermute(array, AXES, pairs)  14.5 us
    ppermute x14, waiting for transfers between devices, swap(): return lax.ppermute(array, AXES, pairs)  13.8 us
    all_to_all x1, starting transfers between devices, by_width(): lax.all_to_all(terms, ('dp', 'adapter'), split_axis=0, concat_axis=0, til...  6.62 us
    all_to_all x1, starting transfers between devices, by_width(): lax.all_to_all(jnp.tile(own_weight, (line, 1)), 'dp', split_axis=0, conca...  4.87 us
    all_to_all x1, waiting for transfers between devices, by_width(): lax.all_to_all(terms, ('dp', 'adapter'), split_axis=0, concat_axis=0, til...  2.73 us
    unnamed x39, local copies, waits for them, and re-layouts  1.85 us
    convert_element_type x1, other arithmetic, by_width(): projected = (value + value_x.astype(f32) + value_y.astype(f32) + value_d....  1.64 us
  transfers between devices with their start and end apart: 16, of which 10 were waited for; matrix products, arithmetic and copies ran while one was open for 3% of the time, Pallas kernels for 24%

profile of v4, /device:TPU:0, one launch (start us, length us, event | category | flops | bytes accessed | tf_op | source)
XLA Modules:
  0.0 67.4 jit_solution(8876408659977163704)
XLA Ops:
  0.6 0.0 copy-start
  0.6 2.6 %shard_map.85 = (bf16[216,1024]{1,0:T(8,128)(2,1)}, bf16[288,256]{1,0:T(8,128)(2,1)}) custom-call(bf16[216,8192]{1,0:T(8,128)(2,1)} %tokens.3, s32[1,216]{1,0:T(1,128)} %bitcast.48, bf16[64,256]{1,0:T(8,128)(2,1)} %bitcast.45, bf16[216,256]{1,0:T(8,128)(2,1)} %cotangent.1), custom_call_target="tpu_custom_call" | custom-call | flops 1000 | bytes 1000 | tf_op jit(solution)/shard_map/pallas_call | solution.py:85
  3.3 3.0 %collective-permute-start.1 = (bf16[288,256]{1,0:T(8,128)(2,1)}, bf16[288,256]{1,0:T(8,128)(2,1)S(1)}, u32[]{:S(2)}, u32[]{:S(2)}) collective-permute-start(bf16[288,256]{1,0:T(8,128)(2,1)} %get-tuple-element.58.refs_0_), channel_id=1, source_target_pairs={{0,2},{1,3},{2,0},{3,1},{4,6},{5,7},{6,4},{7,5},{8,10},{9,11},{10,... | collective-permute-start | bytes 442376 | tf_op jit(solution)/shard_map/ppermute | solution.py:326
  6.3 1.5 %collective-permute-start = (bf16[216,1024]{1,0:T(8,128)(2,1)}, bf16[216,1024]{1,0:T(8,128)(2,1)S(1)}, u32[]{:S(2)}, u32[]{:S(2)}) collective-permute-start(bf16[216,1024]{1,0:T(8,128)(2,1)} %get-tuple-element.49), channel_id=1, source_target_pairs={{0,4},{1,5},{2,6},{3,7},{4,0},{5,1},{6,2},{7,3},{8,12},{9,13},{10,... | collective-permute-start | bytes 1327112 | tf_op jit(solution)/shard_map/ppermute | solution.py:326
  7.8 2.6 %shard_map.86 = (bf16[280,1024]{1,0:T(8,128)(2,1)}, bf16[216,1024]{1,0:T(8,128)(2,1)}, bf16[216,1024]{1,0:T(8,128)(2,1)}, bf16[216,1024]{1,0:T(8,128)(2,1)}, bf1...) custom-call(bf16[216,8192]{1,0:T(8,128)(2,1)} %tokens.3, bf16[64,8192]{1,0:T(8,128)(2,1)} %bitcast.43), custom_call_target="tpu_custom_call" | custom-call | flops 1000 | bytes 1000 | tf_op jit(solution)/shard_map/pallas_call | solution.py:85
  10.4 0.0 collective-permute-done.1.refs_1_
  10.5 0.0 copy-start.10
  10.5 1.6 %collective-permute-start.2 = (bf16[280,1024]{1,0:T(8,128)(2,1)}, bf16[280,1024]{1,0:T(8,128)(2,1)S(1)}, u32[]{:S(2)}, u32[]{:S(2)}) collective-permute-start(bf16[280,1024]{1,0:T(8,128)(2,1)} %get-tuple-element.57), channel_id=1, source_target_pairs={{0,2},{1,3},{2,0},{3,1},{4,6},{5,7},{6,4},{7,5},{8,10},{9,11},{10,... | collective-permute-start | bytes 1720328 | tf_op jit(solution)/shard_map/ppermute | solution.py:326
  12.1 0.0 copy-done
  12.1 1.0 %tile.2 = bf16[4,512,256]{2,1,0:T(8,128)(2,1)} broadcast(bf16[512,256]{1,0:T(8,128)(2,1)S(1)} %constant_dynamic-slice_fusion), dimensions={1,2} | broadcast | bytes 1310720 | tf_op jit(solution)/shard_map/tile | solution.py:369
  13.2 4.9 %all-to-all-start = ((bf16[4,512,256]{2,1,0:T(8,128)(2,1)}), bf16[4,512,256]{2,1,0:T(8,128)(2,1)S(1)}, u32[]{:S(2)}, u32[]{:S(2)}) async-start(bf16[4,512,256]{2,1,0:T(8,128)(2,1)} %tile.2), calls=%async_computation | async-start | bytes 2097152 | tf_op jit(solution)/shard_map/all_to_all | solution.py:368
  18.1 0.1 collective-permute-done.refs_8_
  18.2 1.6 %collective-permute-start.3 = (bf16[448,256]{1,0:T(8,128)(2,1)S(1)}, bf16[448,256]{1,0:T(8,128)(2,1)S(1)}, u32[]{:S(2)}, u32[]{:S(2)}) collective-permute-start(bf16[448,256]{1,0:T(8,128)(2,1)S(1)} %pad_maximum_fusion), channel_id=1, source_target_pairs={{0,4},{1,5},{2,6},{3,7},{4,0},{5,1},{6,2},{7,3},{8,12},{9,13},{10,... | collective-permute-start | bytes 688136 | tf_op jit(solution)/shard_map/ppermute | solution.py:326
  19.7 0.0 collective-permute-start.4
  19.7 0.5 collective-permute-start.5
  20.3 0.9 %collective-permute-done.4.refs_3_ = bf16[288,256]{1,0:T(8,128)(2,1)S(1)} collective-permute-done((bf16[288,256]{1,0:T(8,128)(2,1)S(1)}, bf16[288,256]{1,0:T(8,128)(2,1)S(1)}, u32[]{:S(2)}, u32[]{:S(2)}) %collective-permute-start.4) | collective-permute-done | bytes 147488 | tf_op jit(solution)/shard_map/ppermute | solution.py:326
  21.1 0.2 collective-permute-done.5.refs_4_
  21.3 3.1 %collective-permute-done.3.refs_2_.refs_0_ = bf16[448,256]{1,0:T(8,128)(2,1)S(1)} collective-permute-done((bf16[448,256]{1,0:T(8,128)(2,1)S(1)}, bf16[448,256]{1,0:T(8,128)(2,1)S(1)}, u32[]{:S(2)}, u32[]{:S(2)}) %collective-permute-start.3) | collective-permute-done | bytes 229408 | tf_op jit(solution)/shard_map/ppermute | solution.py:326
  24.4 0.5 collective-permute-done.2.refs_10_
  24.9 0.0 collective-permute-start.8
  24.9 0.5 collective-permute-start.7
  25.4 2.2 %collective-permute-start.9 = (bf16[216,1024]{1,0:T(8,128)(2,1)S(1)}, bf16[216,1024]{1,0:T(8,128)(2,1)S(1)}, u32[]{:S(2)}, u32[]{:S(2)}) collective-permute-start(bf16[216,1024]{1,0:T(8,128)(2,1)S(1)} %copy-done.15), channel_id=1, source_target_pairs={{0,6},{1,7},{2,4},{3,5},{4,2},{5,3},{6,0},{7,1},{8,14},{9,15},{10,... | collective-permute-start | bytes 1327112 | tf_op jit(solution)/shard_map/ppermute | solution.py:326
  27.6 0.0 collective-permute-start.6
  27.6 1.5 %collective-permute-done.6.refs_5_ = bf16[448,256]{1,0:T(8,128)(2,1)S(1)} collective-permute-done((bf16[448,256]{1,0:T(8,128)(2,1)S(1)}, bf16[448,256]{1,0:T(8,128)(2,1)S(1)}, u32[]{:S(2)}, u32[]{:S(2)}) %collective-permute-start.6) | collective-permute-done | bytes 229408 | tf_op jit(solution)/shard_map/ppermute | solution.py:326
  29.1 0.0 collective-permute-done.7.refs_9_
  29.1 0.0 collective-permute-done.8.refs_11_
  29.2 0.6 copy-done.11
  29.8 0.2 copy-done.5
  30.0 0.2 copy-done.3
  30.2 4.9 %shard_map.87 = (f32[128,1280]{1,0:T(8,128)}, bf16[3,128,216]{2,1,0:T(8,128)(2,1)}, bf16[3,128,216]{2,1,0:T(8,128)(2,1)}, bf16[128,256]{1,0:T(8,128)(2,1)}, bf16...) custom-call(bf16[288,256]{1,0:T(8,128)(2,1)} %get-tuple-element.58.refs_0_, ...), custom_call_target="tpu_custom_call" | custom-call | flops 1000 | bytes 1000 | tf_op jit(solution)/shard_map/pallas_call | solution.py:85
  35.1 3.3 %collective-permute-done.9.refs_5_.refs_6_ = bf16[216,1024]{1,0:T(8,128)(2,1)S(1)} collective-permute-done((bf16[216,1024]{1,0:T(8,128)(2,1)S(1)}, bf16[216,1024]{1,0:T(8,128)(2,1)S(1)}, u32[]{:S(2)}, u32[]{:S(2)}) %collective-permute-start.9) | collective-permute-done | bytes 442400 | tf_op jit(solution)/shard_map/ppermute | solution.py:326
  38.4 0.0 collective-permute-start.10
  38.4 1.8 %collective-permute-done.10.refs_6_.refs_7_ = bf16[216,1024]{1,0:T(8,128)(2,1)S(1)} collective-permute-done((bf16[216,1024]{1,0:T(8,128)(2,1)S(1)}, bf16[216,1024]{1,0:T(8,128)(2,1)S(1)}, u32[]{:S(2)}, u32[]{:S(2)}) %collective-permute-start.10) | collective-permute-done | bytes 442400 | tf_op jit(solution)/shard_map/ppermute | solution.py:326
  40.2 0.8 %copy-done.7 = bf16[216,1024]{1,0:T(8,128)(2,1)} copy-done((bf16[216,1024]{1,0:T(8,128)(2,1)}, bf16[216,1024]{1,0:T(8,128)(2,1)S(1)}, u32[]{:S(2)}) %copy-start.7) | copy-done | bytes 442392
  41.0 3.1 %shard_map.88 = (bf16[128,1280]{1,0:T(8,128)(2,1)}, bf16[128,216]{1,0:T(8,128)(2,1)}, bf16[128,216]{1,0:T(8,128)(2,1)}) custom-call(bf16[448,256]{1,0:T(8,128)(2,1)} %copy-done.8, bf16[128,216]{1,0:T(8,128)(2,1)} %get-tuple-element.72.refs_1_, f32[128,216]{1,0:T(8,128)} %get-tuple-element.73.refs_2_, bf16[128,1024]{1,0:T(8,128)(2,1)} %get-tuple-element.74.refs_3_, ...), custom_call_target="tpu_custom_call" | custom-call | flops 1000 | bytes 1000 | tf_op jit(solution)/shard_map/pallas_call | solution.py:85
  44.1 0.0 all-to-all-done
  44.1 6.6 %all-to-all-start.1 = ((bf16[16,8,1280]{2,1,0:T(8,128)(2,1)}), bf16[16,8,1280]{2,1,0:T(8,128)(2,1)S(1)}, u32[]{:S(2)}, u32[]{:S(2)}) async-start(bf16[16,8,1280]{2,1,0:T(8,128)(2,1)} %bitcast.44), calls=%async_computation.1 | async-start | bytes 655360 | tf_op jit(solution)/shard_map/all_to_all | solution.py:411
  50.8 5.4 %shard_map.89 = (f32[216,256]{1,0:T(8,128)}, bf16[216,256]{1,0:T(8,128)(2,1)}, bf16[216,256]{1,0:T(8,128)(2,1)}, bf16[216,256]{1,0:T(8,128)(2,1)}) custom-call(bf16[2048,256]{1,0:T(8,128)(2,1)} %bitcast.41, bf16[128,256]{1,0:T(8,128)(2,1)} %get-tuple-element.69.refs_1_, bf16[3,128,216]{2,1,0:T(8,128)(2,1)} %get-tuple-element.70.refs_2_, ...), custom_call_target="tpu_custom_call" | custom-call | flops 1000 | bytes 1000 | tf_op jit(solution)/shard_map/pallas_call | solution.py:85
  56.2 2.0 %collective-permute-start.11 = (bf16[216,256]{1,0:T(8,128)(2,1)}, bf16[216,256]{1,0:T(8,128)(2,1)S(1)}, u32[]{:S(2)}, u32[]{:S(2)}) collective-permute-start(bf16[216,256]{1,0:T(8,128)(2,1)} %get-tuple-element.83), channel_id=1, source_target_pairs={{0,4},{1,5},{2,6},{3,7},{4,0},{5,1},{6,2},{7,3},{8,12},{9,13},{10,... | collective-permute-start | bytes 331784 | tf_op jit(solution)/shard_map/ppermute | solution.py:326
  58.2 1.5 %collective-permute-start.12 = (bf16[216,256]{1,0:T(8,128)(2,1)}, bf16[216,256]{1,0:T(8,128)(2,1)S(1)}, u32[]{:S(2)}, u32[]{:S(2)}) collective-permute-start(bf16[216,256]{1,0:T(8,128)(2,1)} %get-tuple-element.84), channel_id=1, source_target_pairs={{0,2},{1,3},{2,0},{3,1},{4,6},{5,7},{6,4},{7,5},{8,10},{9,11},{10,... | collective-permute-start | bytes 331784 | tf_op jit(solution)/shard_map/ppermute | solution.py:326
  59.7 0.1 collective-permute-start.13
  59.8 2.7 %all-to-all-done.1 = bf16[16,8,1280]{2,1,0:T(8,128)(2,1)S(1)} async-done(((bf16[16,8,1280]{2,1,0:T(8,128)(2,1)}), bf16[16,8,1280]{2,1,0:T(8,128)(2,1)S(1)}, u32[]{:S(2)}, u32[]{:S(2)}) %all-to-all-start.1) | async-done | bytes 327712 | tf_op jit(solution)/shard_map/all_to_all | solution.py:411
  62.6 0.0 copy-start.14
  62.6 0.6 slice_reduce_fusion
  63.3 0.0 collective-permute-done.11
  63.3 2.5 %collective-permute-done.12 = bf16[216,256]{1,0:T(8,128)(2,1)S(1)} collective-permute-done((bf16[216,256]{1,0:T(8,128)(2,1)}, bf16[216,256]{1,0:T(8,128)(2,1)S(1)}, u32[]{:S(2)}, u32[]{:S(2)}) %collective-permute-start.12) | collective-permute-done | bytes 110624 | tf_op jit(solution)/shard_map/ppermute | solution.py:326
  65.7 0.0 collective-permute-done.13
  65.7 1.6 %add_convert_fusion = bf16[216,256]{1,0:T(8,128)(2,1)} fusion(bf16[216,256]{1,0:T(8,128)(2,1)S(1)} %collective-permute-done.13, bf16[216,256]{1,0:T(8,128)(2,1)S(1)} %collective-permute-done.12, f32[216,256]{1,0:T(8,128)} %get-tuple-element.82, bf16[216,256]{1,0:T(8,128)(2,1)S(1)} %collective-permute-done.11), kind=kLoop, calls=%fused_computation.2 | loop fusion | flops 387072 | bytes 663552 | tf_op jit(solution)/shard_map/convert_element_type | solution.py:436
  (37 shorter events, 0.2 us)
Async XLA Ops:
  0.6 11.5 %copy-start = (bf16[1024,256]{1,0:T(8,128)(2,1)S(1)}, bf16[1024,256]{1,0:T(8,128)(2,1)}, u32[]{:S(2)}) copy-start(bf16[1024,256]{1,0:T(8,128)(2,1)} %param.7) | copy-start | bytes 1572868
  3.3 7.2 %collective-permute-start.1 = (bf16[288,256]{1,0:T(8,128)(2,1)}, bf16[288,256]{1,0:T(8,128)(2,1)S(1)}, u32[]{:S(2)}, u32[]{:S(2)}) collective-permute-start(bf16[288,256]{1,0:T(8,128)(2,1)} %get-tuple-element.58.refs_0_), channel_id=1, source_target_pairs={{0,2},{1,3},{2,0},{3,1},{4,6},{5,7},{6,4},{7,5},{8,10},{9,11},{10,... | collective-permute-start | bytes 442376 | tf_op jit(solution)/shard_map/ppermute | solution.py:326
  6.3 11.7 %copy-start.9 = (bf16[288,256]{1,0:T(8,128)(2,1)S(1)}, bf16[288,256]{1,0:T(8,128)(2,1)}, u32[]{:S(2)}) copy-start(bf16[288,256]{1,0:T(8,128)(2,1)} %get-tuple-element.58.refs_0_) | copy-start | bytes 442372
  6.3 11.8 %collective-permute-start = (bf16[216,1024]{1,0:T(8,128)(2,1)}, bf16[216,1024]{1,0:T(8,128)(2,1)S(1)}, u32[]{:S(2)}, u32[]{:S(2)}) collective-permute-start(bf16[216,1024]{1,0:T(8,128)(2,1)} %get-tuple-element.49), channel_id=1, source_target_pairs={{0,4},{1,5},{2,6},{3,7},{4,0},{5,1},{6,2},{7,3},{8,12},{9,13},{10,... | collective-permute-start | bytes 1327112 | tf_op jit(solution)/shard_map/ppermute | solution.py:326
  10.4 15.0 %copy-start.15 = (bf16[216,1024]{1,0:T(8,128)(2,1)S(1)}, bf16[216,1024]{1,0:T(8,128)(2,1)}, u32[]{:S(2)}) copy-start(bf16[216,1024]{1,0:T(8,128)(2,1)} %get-tuple-element.76) | copy-start | bytes 1327108
  10.5 18.7 %copy-start.10 = (bf16[288,256]{1,0:T(8,128)(2,1)}, bf16[288,256]{1,0:T(8,128)(2,1)S(1)}, u32[]{:S(2)}) copy-start(bf16[288,256]{1,0:T(8,128)(2,1)S(1)} %collective-permute-done.1.refs_1_) | copy-start | bytes 442372
  10.5 14.4 %collective-permute-start.2 = (bf16[280,1024]{1,0:T(8,128)(2,1)}, bf16[280,1024]{1,0:T(8,128)(2,1)S(1)}, u32[]{:S(2)}, u32[]{:S(2)}) collective-permute-start(bf16[280,1024]{1,0:T(8,128)(2,1)} %get-tuple-element.57), channel_id=1, source_target_pairs={{0,2},{1,3},{2,0},{3,1},{4,6},{5,7},{6,4},{7,5},{8,10},{9,11},{10,... | collective-permute-start | bytes 1720328 | tf_op jit(solution)/shard_map/ppermute | solution.py:326
  13.2 30.9 %all-to-all-start = ((bf16[4,512,256]{2,1,0:T(8,128)(2,1)}), bf16[4,512,256]{2,1,0:T(8,128)(2,1)S(1)}, u32[]{:S(2)}, u32[]{:S(2)}) async-start(bf16[4,512,256]{2,1,0:T(8,128)(2,1)} %tile.2), calls=%async_computation | async-start | bytes 2097152 | tf_op jit(solution)/shard_map/all_to_all | solution.py:368
  18.1 11.0 %copy-start.4 = (bf16[216,1024]{1,0:T(8,128)(2,1)}, bf16[216,1024]{1,0:T(8,128)(2,1)S(1)}, u32[]{:S(2)}) copy-start(bf16[216,1024]{1,0:T(8,128)(2,1)S(1)} %collective-permute-done.refs_8_) | copy-start | bytes 1327108
  18.2 6.2 %collective-permute-start.3 = (bf16[448,256]{1,0:T(8,128)(2,1)S(1)}, bf16[448,256]{1,0:T(8,128)(2,1)S(1)}, u32[]{:S(2)}, u32[]{:S(2)}) collective-permute-start(bf16[448,256]{1,0:T(8,128)(2,1)S(1)} %pad_maximum_fusion), channel_id=1, source_target_pairs={{0,4},{1,5},{2,6},{3,7},{4,0},{5,1},{6,2},{7,3},{8,12},{9,13},{10,... | collective-permute-start | bytes 688136 | tf_op jit(solution)/shard_map/ppermute | solution.py:326
  19.7 1.4 %collective-permute-start.4 = (bf16[288,256]{1,0:T(8,128)(2,1)S(1)}, bf16[288,256]{1,0:T(8,128)(2,1)S(1)}, u32[]{:S(2)}, u32[]{:S(2)}) collective-permute-start(bf16[288,256]{1,0:T(8,128)(2,1)S(1)} %copy-done.9), channel_id=1, source_target_pairs={{0,1},{1,0},{2,3},{3,2},{4,5},{5,4},{6,7},{7,6},{8,9},{9,8},{10,11... | collective-permute-start | bytes 442376 | tf_op jit(solution)/shard_map/ppermute | solution.py:326
  19.7 1.6 %collective-permute-start.5 = (bf16[288,256]{1,0:T(8,128)(2,1)S(1)}, bf16[288,256]{1,0:T(8,128)(2,1)S(1)}, u32[]{:S(2)}, u32[]{:S(2)}) collective-permute-start(bf16[288,256]{1,0:T(8,128)(2,1)S(1)} %collective-permute-done.1.refs_1_), channel_id=1, source_target_pairs={{0,1},{1,0},{2,3},{3,2},{4,5},{5,4},{6,7},{7,6},{8,9},{9,8},{10,11... | collective-permute-start | bytes 442376 | tf_op jit(solution)/shard_map/ppermute | solution.py:326
  21.1 8.0 %copy-start.12 = (bf16[288,256]{1,0:T(8,128)(2,1)}, bf16[288,256]{1,0:T(8,128)(2,1)S(1)}, u32[]{:S(2)}) copy-start(bf16[288,256]{1,0:T(8,128)(2,1)S(1)} %collective-permute-done.4.refs_3_) | copy-start | bytes 442372
  21.3 7.8 %copy-start.13 = (bf16[288,256]{1,0:T(8,128)(2,1)}, bf16[288,256]{1,0:T(8,128)(2,1)S(1)}, u32[]{:S(2)}) copy-start(bf16[288,256]{1,0:T(8,128)(2,1)S(1)} %collective-permute-done.5.refs_4_) | copy-start | bytes 442372
  24.4 4.8 %copy-start.8 = (bf16[448,256]{1,0:T(8,128)(2,1)}, bf16[448,256]{1,0:T(8,128)(2,1)S(1)}, u32[]{:S(2)}) copy-start(bf16[448,256]{1,0:T(8,128)(2,1)S(1)} %collective-permute-done.3.refs_2_.refs_0_) | copy-start | bytes 688132
  24.9 4.3 %copy-start.2 = (bf16[280,1024]{1,0:T(8,128)(2,1)}, bf16[280,1024]{1,0:T(8,128)(2,1)S(1)}, u32[]{:S(2)}) copy-start(bf16[280,1024]{1,0:T(8,128)(2,1)S(1)} %collective-permute-done.2.refs_10_) | copy-start | bytes 1720324
  24.9 4.2 %collective-permute-start.8 = (bf16[280,1024]{1,0:T(8,128)(2,1)S(1)}, bf16[280,1024]{1,0:T(8,128)(2,1)S(1)}, u32[]{:S(2)}, u32[]{:S(2)}) collective-permute-start(bf16[280,1024]{1,0:T(8,128)(2,1)S(1)} %collective-permute-done.2.refs_10_), channel_id=1, source_target_pairs={{0,1},{1,0},{2,3},{3,2},{4,5},{5,4},{6,7},{7,6},{8,9},{9,8},{10,11... | collective-permute-start | bytes 1720328 | tf_op jit(solution)/shard_map/ppermute | solution.py:326
  24.9 4.2 %collective-permute-start.7 = (bf16[216,1024]{1,0:T(8,128)(2,1)S(1)}, bf16[216,1024]{1,0:T(8,128)(2,1)S(1)}, u32[]{:S(2)}, u32[]{:S(2)}) collective-permute-start(bf16[216,1024]{1,0:T(8,128)(2,1)S(1)} %collective-permute-done.refs_8_), channel_id=1, source_target_pairs={{0,1},{1,0},{2,3},{3,2},{4,5},{5,4},{6,7},{7,6},{8,9},{9,8},{10,11... | collective-permute-start | bytes 1327112 | tf_op jit(solution)/shard_map/ppermute | solution.py:326
  25.4 13.0 %collective-permute-start.9 = (bf16[216,1024]{1,0:T(8,128)(2,1)S(1)}, bf16[216,1024]{1,0:T(8,128)(2,1)S(1)}, u32[]{:S(2)}, u32[]{:S(2)}) collective-permute-start(bf16[216,1024]{1,0:T(8,128)(2,1)S(1)} %copy-done.15), channel_id=1, source_target_pairs={{0,6},{1,7},{2,4},{3,5},{4,2},{5,3},{6,0},{7,1},{8,14},{9,15},{10,... | collective-permute-start | bytes 1327112 | tf_op jit(solution)/shard_map/ppermute | solution.py:326
  27.6 1.5 %collective-permute-start.6 = (bf16[448,256]{1,0:T(8,128)(2,1)S(1)}, bf16[448,256]{1,0:T(8,128)(2,1)S(1)}, u32[]{:S(2)}, u32[]{:S(2)}) collective-permute-start(bf16[448,256]{1,0:T(8,128)(2,1)S(1)} %collective-permute-done.3.refs_2_.refs_0_), channel_id=1, source_target_pairs={{0,1},{1,0},{2,3},{3,2},{4,5},{5,4},{6,7},{7,6},{8,9},{9,8},{10,11... | collective-permute-start | bytes 688136 | tf_op jit(solution)/shard_map/ppermute | solution.py:326
  29.1 0.7 %copy-start.11 = (bf16[448,256]{1,0:T(8,128)(2,1)}, bf16[448,256]{1,0:T(8,128)(2,1)S(1)}, u32[]{:S(2)}) copy-start(bf16[448,256]{1,0:T(8,128)(2,1)S(1)} %collective-permute-done.6.refs_5_) | copy-start | bytes 688132
  29.1 0.9 %copy-start.5 = (bf16[216,1024]{1,0:T(8,128)(2,1)}, bf16[216,1024]{1,0:T(8,128)(2,1)S(1)}, u32[]{:S(2)}) copy-start(bf16[216,1024]{1,0:T(8,128)(2,1)S(1)} %collective-permute-done.7.refs_9_) | copy-start | bytes 1327108
  29.1 1.1 %copy-start.3 = (bf16[280,1024]{1,0:T(8,128)(2,1)}, bf16[280,1024]{1,0:T(8,128)(2,1)S(1)}, u32[]{:S(2)}) copy-start(bf16[280,1024]{1,0:T(8,128)(2,1)S(1)} %collective-permute-done.8.refs_11_) | copy-start | bytes 1720324
  38.4 1.8 %copy-start.6 = (bf16[216,1024]{1,0:T(8,128)(2,1)}, bf16[216,1024]{1,0:T(8,128)(2,1)S(1)}, u32[]{:S(2)}) copy-start(bf16[216,1024]{1,0:T(8,128)(2,1)S(1)} %collective-permute-done.9.refs_5_.refs_6_) | copy-start | bytes 1327108
  38.4 1.8 %collective-permute-start.10 = (bf16[216,1024]{1,0:T(8,128)(2,1)S(1)}, bf16[216,1024]{1,0:T(8,128)(2,1)S(1)}, u32[]{:S(2)}, u32[]{:S(2)}) collective-permute-start(bf16[216,1024]{1,0:T(8,128)(2,1)S(1)} %collective-permute-done.9.refs_5_.refs_6_), channel_id=1, source_target_pairs={{0,1},{1,0},{2,3},{3,2},{4,5},{5,4},{6,7},{7,6},{8,9},{9,8},{10,11... | collective-permute-start | bytes 1327112 | tf_op jit(solution)/shard_map/ppermute | solution.py:326
  40.2 0.8 %copy-start.7 = (bf16[216,1024]{1,0:T(8,128)(2,1)}, bf16[216,1024]{1,0:T(8,128)(2,1)S(1)}, u32[]{:S(2)}) copy-start(bf16[216,1024]{1,0:T(8,128)(2,1)S(1)} %collective-permute-done.10.refs_6_.refs_7_) | copy-start | bytes 1327108
  44.1 6.6 %copy-start.1 = (bf16[4,512,256]{2,1,0:T(8,128)(2,1)}, bf16[4,512,256]{2,1,0:T(8,128)(2,1)S(1)}, u32[]{:S(2)}) copy-start(bf16[4,512,256]{2,1,0:T(8,128)(2,1)S(1)} %all-to-all-done) | copy-start | bytes 3145732
  44.1 18.4 %all-to-all-start.1 = ((bf16[16,8,1280]{2,1,0:T(8,128)(2,1)}), bf16[16,8,1280]{2,1,0:T(8,128)(2,1)S(1)}, u32[]{:S(2)}, u32[]{:S(2)}) async-start(bf16[16,8,1280]{2,1,0:T(8,128)(2,1)} %bitcast.44), calls=%async_computation.1 | async-start | bytes 655360 | tf_op jit(solution)/shard_map/all_to_all | solution.py:411
  56.2 7.1 %collective-permute-start.11 = (bf16[216,256]{1,0:T(8,128)(2,1)}, bf16[216,256]{1,0:T(8,128)(2,1)S(1)}, u32[]{:S(2)}, u32[]{:S(2)}) collective-permute-start(bf16[216,256]{1,0:T(8,128)(2,1)} %get-tuple-element.83), channel_id=1, source_target_pairs={{0,4},{1,5},{2,6},{3,7},{4,0},{5,1},{6,2},{7,3},{8,12},{9,13},{10,... | collective-permute-start | bytes 331784 | tf_op jit(solution)/shard_map/ppermute | solution.py:326
  58.2 7.5 %collective-permute-start.12 = (bf16[216,256]{1,0:T(8,128)(2,1)}, bf16[216,256]{1,0:T(8,128)(2,1)S(1)}, u32[]{:S(2)}, u32[]{:S(2)}) collective-permute-start(bf16[216,256]{1,0:T(8,128)(2,1)} %get-tuple-element.84), channel_id=1, source_target_pairs={{0,2},{1,3},{2,0},{3,1},{4,6},{5,7},{6,4},{7,5},{8,10},{9,11},{10,... | collective-permute-start | bytes 331784 | tf_op jit(solution)/shard_map/ppermute | solution.py:326
  59.7 6.1 %collective-permute-start.13 = (bf16[216,256]{1,0:T(8,128)(2,1)}, bf16[216,256]{1,0:T(8,128)(2,1)S(1)}, u32[]{:S(2)}, u32[]{:S(2)}) collective-permute-start(bf16[216,256]{1,0:T(8,128)(2,1)} %get-tuple-element.85), channel_id=1, source_target_pairs={{0,6},{1,7},{2,4},{3,5},{4,2},{5,3},{6,0},{7,1},{8,14},{9,15},{10,... | collective-permute-start | bytes 331784 | tf_op jit(solution)/shard_map/ppermute | solution.py:326
  62.6 4.7 %copy-start.14 = (f32[8,4096]{1,0:T(8,128)}, f32[8,4096]{1,0:T(8,128)S(1)}, u32[]{:S(2)}) copy-start(f32[8,4096]{1,0:T(8,128)S(1)} %constant_dynamic-update-slice_fusion) | copy-start | bytes 393220

commit v5 on v3

--- a/solution.py
+++ b/solution.py
@@ -426,9 +426,8 @@
         axis=1,
     )[None]
     value_x, value_y, value_d, grad_a = lax.optimization_barrier((value_x, value_y, value_d, grad_a))
-    projected = (
-        value + value_x.astype(f32) + value_y.astype(f32) + value_d.astype(f32)
-    ).astype(bf16)
+    partial = lax.optimization_barrier(value + value_x.astype(f32))
+    projected = (partial + value_y.astype(f32) + value_d.astype(f32)).astype(bf16)
     return projected, grad_a, up_gradient
 
 

time: 67.8 us -> 67.8 us (level)
    add x0 -> x1, other arithmetic: none -> 0.96 us  [by_width(): partial = lax.optimization_barrier(value + value_x.astype(f32))]
    convert_element_type x1, other arithmetic: 1.64 us -> 0.69 us  [by_width(): (partial + value_y.astype(f32) + value_d.astype(f32)).astype(bf16)]
where the time goes in v5:
time: 67.8 us; the launch traced here: 67.4 us
  starting transfers between devices  26.1 us (38%)
  Pallas kernels  18.7 us (28%)
  waiting for transfers between devices  16.3 us (24%)
  local copies, waits for them, and re-layouts  2.97 us (4%)
  other arithmetic  2.34 us (3%)
  between operations  0.93 us (1%)
    pallas_call x5, Pallas kernels, call(): pl.pallas_call(kernel, out_shape=outs, in_specs=[VMEM if k in held else H...  18.7 us
    ppermute x14, starting transfers between devices, swap(): return lax.ppermute(array, AXES, pairs)  14.6 us
    ppermute x14, waiting for transfers between devices, swap(): return lax.ppermute(array, AXES, pairs)  13.6 us
    all_to_all x1, starting transfers between devices, by_width(): lax.all_to_all(terms, ('dp', 'adapter'), split_axis=0, concat_axis=0, til...  6.62 us
    all_to_all x1, starting transfers between devices, by_width(): lax.all_to_all(jnp.tile(own_weight, (line, 1)), 'dp', split_axis=0, conca...  4.87 us
    all_to_all x1, waiting for transfers between devices, by_width(): lax.all_to_all(terms, ('dp', 'adapter'), split_axis=0, concat_axis=0, til...  2.73 us
    unnamed x39, local copies, waits for them, and re-layouts  1.89 us
  transfers between devices with their start and end apart: 16, of which 9 were waited for; matrix products, arithmetic and copies ran while one was open for 3% of the time, Pallas kernels for 24%

profile of v5, /device:TPU:0, one launch (start us, length us, event | category | flops | bytes accessed | tf_op | source)
XLA Modules:
  0.0 67.4 jit_solution(16707570772414892885)
XLA Ops:
  0.6 0.0 copy-start
  0.6 2.6 %shard_map.85 = (bf16[216,1024]{1,0:T(8,128)(2,1)}, bf16[288,256]{1,0:T(8,128)(2,1)}) custom-call(bf16[216,8192]{1,0:T(8,128)(2,1)} %tokens.3, s32[1,216]{1,0:T(1,128)} %bitcast.48, bf16[64,256]{1,0:T(8,128)(2,1)} %bitcast.45, bf16[216,256]{1,0:T(8,128)(2,1)} %cotangent.1), custom_call_target="tpu_custom_call" | custom-call | flops 1000 | bytes 1000 | tf_op jit(solution)/shard_map/pallas_call | solution.py:85
  3.3 3.0 %collective-permute-start.1 = (bf16[288,256]{1,0:T(8,128)(2,1)}, bf16[288,256]{1,0:T(8,128)(2,1)S(1)}, u32[]{:S(2)}, u32[]{:S(2)}) collective-permute-start(bf16[288,256]{1,0:T(8,128)(2,1)} %get-tuple-element.42.refs_0_), channel_id=1, source_target_pairs={{0,2},{1,3},{2,0},{3,1},{4,6},{5,7},{6,4},{7,5},{8,10},{9,11},{10,... | collective-permute-start | bytes 442376 | tf_op jit(solution)/shard_map/ppermute | solution.py:326
  6.3 1.5 %collective-permute-start = (bf16[216,1024]{1,0:T(8,128)(2,1)}, bf16[216,1024]{1,0:T(8,128)(2,1)S(1)}, u32[]{:S(2)}, u32[]{:S(2)}) collective-permute-start(bf16[216,1024]{1,0:T(8,128)(2,1)} %get-tuple-element.44), channel_id=1, source_target_pairs={{0,4},{1,5},{2,6},{3,7},{4,0},{5,1},{6,2},{7,3},{8,12},{9,13},{10,... | collective-permute-start | bytes 1327112 | tf_op jit(solution)/shard_map/ppermute | solution.py:326
  7.8 2.6 %shard_map.86 = (bf16[280,1024]{1,0:T(8,128)(2,1)}, bf16[216,1024]{1,0:T(8,128)(2,1)}, bf16[216,1024]{1,0:T(8,128)(2,1)}, bf16[216,1024]{1,0:T(8,128)(2,1)}, bf1...) custom-call(bf16[216,8192]{1,0:T(8,128)(2,1)} %tokens.3, bf16[64,8192]{1,0:T(8,128)(2,1)} %bitcast.43), custom_call_target="tpu_custom_call" | custom-call | flops 1000 | bytes 1000 | tf_op jit(solution)/shard_map/pallas_call | solution.py:85
  10.4 0.0 collective-permute-done.1.refs_1_
  10.5 1.6 %collective-permute-start.2 = (bf16[280,1024]{1,0:T(8,128)(2,1)}, bf16[280,1024]{1,0:T(8,128)(2,1)S(1)}, u32[]{:S(2)}, u32[]{:S(2)}) collective-permute-start(bf16[280,1024]{1,0:T(8,128)(2,1)} %get-tuple-element.51), channel_id=1, source_target_pairs={{0,2},{1,3},{2,0},{3,1},{4,6},{5,7},{6,4},{7,5},{8,10},{9,11},{10,... | collective-permute-start | bytes 1720328 | tf_op jit(solution)/shard_map/ppermute | solution.py:326
  12.1 1.0 %tile.2 = bf16[4,512,256]{2,1,0:T(8,128)(2,1)} broadcast(bf16[512,256]{1,0:T(8,128)(2,1)S(1)} %constant_dynamic-slice_fusion), dimensions={1,2} | broadcast | bytes 1310720 | tf_op jit(solution)/shard_map/tile | solution.py:365
  13.2 4.9 %all-to-all-start = ((bf16[4,512,256]{2,1,0:T(8,128)(2,1)}), bf16[4,512,256]{2,1,0:T(8,128)(2,1)S(1)}, u32[]{:S(2)}, u32[]{:S(2)}) async-start(bf16[4,512,256]{2,1,0:T(8,128)(2,1)} %tile.2), calls=%async_computation | async-start | bytes 2097152 | tf_op jit(solution)/shard_map/all_to_all | solution.py:364
  18.1 0.1 collective-permute-done.refs_8_
  18.2 1.6 %collective-permute-start.3 = (bf16[448,256]{1,0:T(8,128)(2,1)S(1)}, bf16[448,256]{1,0:T(8,128)(2,1)S(1)}, u32[]{:S(2)}, u32[]{:S(2)}) collective-permute-start(bf16[448,256]{1,0:T(8,128)(2,1)S(1)} %pad_maximum_fusion), channel_id=1, source_target_pairs={{0,4},{1,5},{2,6},{3,7},{4,0},{5,1},{6,2},{7,3},{8,12},{9,13},{10,... | collective-permute-start | bytes 688136 | tf_op jit(solution)/shard_map/ppermute | solution.py:326
  19.7 4.7 %collective-permute-done.3.refs_2_.refs_0_ = bf16[448,256]{1,0:T(8,128)(2,1)S(1)} collective-permute-done((bf16[448,256]{1,0:T(8,128)(2,1)S(1)}, bf16[448,256]{1,0:T(8,128)(2,1)S(1)}, u32[]{:S(2)}, u32[]{:S(2)}) %collective-permute-start.3) | collective-permute-done | bytes 229408 | tf_op jit(solution)/shard_map/ppermute | solution.py:326
  24.4 0.5 collective-permute-done.2.refs_10_
  24.9 0.0 collective-permute-start.8
  24.9 0.5 collective-permute-start.7
  25.4 2.2 %collective-permute-start.9 = (bf16[216,1024]{1,0:T(8,128)(2,1)S(1)}, bf16[216,1024]{1,0:T(8,128)(2,1)S(1)}, u32[]{:S(2)}, u32[]{:S(2)}) collective-permute-start(bf16[216,1024]{1,0:T(8,128)(2,1)S(1)} %copy-done.15), channel_id=1, source_target_pairs={{0,6},{1,7},{2,4},{3,5},{4,2},{5,3},{6,0},{7,1},{8,14},{9,15},{10,... | collective-permute-start | bytes 1327112 | tf_op jit(solution)/shard_map/ppermute | solution.py:326
  27.6 0.0 collective-permute-start.4
  27.6 0.5 collective-permute-start.6
  28.1 0.9 %collective-permute-done.4.refs_3_ = bf16[288,256]{1,0:T(8,128)(2,1)S(1)} collective-permute-done((bf16[288,256]{1,0:T(8,128)(2,1)S(1)}, bf16[288,256]{1,0:T(8,128)(2,1)S(1)}, u32[]{:S(2)}, u32[]{:S(2)}) %collective-permute-start.4) | collective-permute-done | bytes 147488 | tf_op jit(solution)/shard_map/ppermute | solution.py:326
  29.0 0.1 collective-permute-start.5
  29.1 1.2 %collective-permute-done.5.refs_4_ = bf16[288,256]{1,0:T(8,128)(2,1)S(1)} collective-permute-done((bf16[288,256]{1,0:T(8,128)(2,1)S(1)}, bf16[288,256]{1,0:T(8,128)(2,1)S(1)}, u32[]{:S(2)}, u32[]{:S(2)}) %collective-permute-start.5) | collective-permute-done | bytes 147488 | tf_op jit(solution)/shard_map/ppermute | solution.py:326
  30.4 0.0 collective-permute-done.6.refs_5_
  30.4 0.0 collective-permute-done.7.refs_9_
  30.4 0.0 collective-permute-done.8.refs_11_
  30.4 0.6 copy-done.13
  31.0 0.1 copy-done.11
  31.1 0.2 copy-done.5
  31.3 0.2 copy-done.3
  31.5 4.9 %shard_map.87 = (f32[128,1280]{1,0:T(8,128)}, bf16[3,128,216]{2,1,0:T(8,128)(2,1)}, bf16[3,128,216]{2,1,0:T(8,128)(2,1)}, bf16[128,256]{1,0:T(8,128)(2,1)}, bf16...) custom-call(bf16[288,256]{1,0:T(8,128)(2,1)} %get-tuple-element.42.refs_0_, ...), custom_call_target="tpu_custom_call" | custom-call | flops 1000 | bytes 1000 | tf_op jit(solution)/shard_map/pallas_call | solution.py:85
  36.4 2.0 %collective-permute-done.9.refs_5_.refs_6_ = bf16[216,1024]{1,0:T(8,128)(2,1)S(1)} collective-permute-done((bf16[216,1024]{1,0:T(8,128)(2,1)S(1)}, bf16[216,1024]{1,0:T(8,128)(2,1)S(1)}, u32[]{:S(2)}, u32[]{:S(2)}) %collective-permute-start.9) | collective-permute-done | bytes 442400 | tf_op jit(solution)/shard_map/ppermute | solution.py:326
  38.4 0.0 collective-permute-start.10
  38.4 1.8 %collective-permute-done.10.refs_6_.refs_7_ = bf16[216,1024]{1,0:T(8,128)(2,1)S(1)} collective-permute-done((bf16[216,1024]{1,0:T(8,128)(2,1)S(1)}, bf16[216,1024]{1,0:T(8,128)(2,1)S(1)}, u32[]{:S(2)}, u32[]{:S(2)}) %collective-permute-start.10) | collective-permute-done | bytes 442400 | tf_op jit(solution)/shard_map/ppermute | solution.py:326
  40.2 0.8 %copy-done.7 = bf16[216,1024]{1,0:T(8,128)(2,1)} copy-done((bf16[216,1024]{1,0:T(8,128)(2,1)}, bf16[216,1024]{1,0:T(8,128)(2,1)S(1)}, u32[]{:S(2)}) %copy-start.7) | copy-done | bytes 442392
  41.0 3.1 %shard_map.88 = (bf16[128,1280]{1,0:T(8,128)(2,1)}, bf16[128,216]{1,0:T(8,128)(2,1)}, bf16[128,216]{1,0:T(8,128)(2,1)}) custom-call(bf16[448,256]{1,0:T(8,128)(2,1)} %copy-done.8, bf16[128,216]{1,0:T(8,128)(2,1)} %get-tuple-element.62.refs_1_, f32[128,216]{1,0:T(8,128)} %get-tuple-element.63.refs_2_, bf16[128,1024]{1,0:T(8,128)(2,1)} %get-tuple-element.64.refs_3_, ...), custom_call_target="tpu_custom_call" | custom-call | flops 1000 | bytes 1000 | tf_op jit(solution)/shard_map/pallas_call | solution.py:85
  44.1 0.0 all-to-all-done
  44.1 6.6 %all-to-all-start.1 = ((bf16[16,8,1280]{2,1,0:T(8,128)(2,1)}), bf16[16,8,1280]{2,1,0:T(8,128)(2,1)S(1)}, u32[]{:S(2)}, u32[]{:S(2)}) async-start(bf16[16,8,1280]{2,1,0:T(8,128)(2,1)} %bitcast.44), calls=%async_computation.1 | async-start | bytes 655360 | tf_op jit(solution)/shard_map/all_to_all | solution.py:406
  50.8 5.4 %shard_map.89 = (f32[216,256]{1,0:T(8,128)}, bf16[216,256]{1,0:T(8,128)(2,1)}, bf16[216,256]{1,0:T(8,128)(2,1)}, bf16[216,256]{1,0:T(8,128)(2,1)}) custom-call(bf16[2048,256]{1,0:T(8,128)(2,1)} %bitcast.41, bf16[128,256]{1,0:T(8,128)(2,1)} %get-tuple-element.59.refs_1_, bf16[3,128,216]{2,1,0:T(8,128)(2,1)} %get-tuple-element.60.refs_2_, ...), custom_call_target="tpu_custom_call" | custom-call | flops 1000 | bytes 1000 | tf_op jit(solution)/shard_map/pallas_call | solution.py:85
  56.2 2.0 %collective-permute-start.11 = (bf16[216,256]{1,0:T(8,128)(2,1)}, bf16[216,256]{1,0:T(8,128)(2,1)S(1)}, u32[]{:S(2)}, u32[]{:S(2)}) collective-permute-start(bf16[216,256]{1,0:T(8,128)(2,1)} %get-tuple-element.73), channel_id=1, source_target_pairs={{0,4},{1,5},{2,6},{3,7},{4,0},{5,1},{6,2},{7,3},{8,12},{9,13},{10,... | collective-permute-start | bytes 331784 | tf_op jit(solution)/shard_map/ppermute | solution.py:326
  58.2 1.5 %collective-permute-start.12 = (bf16[216,256]{1,0:T(8,128)(2,1)}, bf16[216,256]{1,0:T(8,128)(2,1)S(1)}, u32[]{:S(2)}, u32[]{:S(2)}) collective-permute-start(bf16[216,256]{1,0:T(8,128)(2,1)} %get-tuple-element.74), channel_id=1, source_target_pairs={{0,2},{1,3},{2,0},{3,1},{4,6},{5,7},{6,4},{7,5},{8,10},{9,11},{10,... | collective-permute-start | bytes 331784 | tf_op jit(solution)/shard_map/ppermute | solution.py:326
  59.7 0.1 collective-permute-start.13
  59.8 2.7 %all-to-all-done.1 = bf16[16,8,1280]{2,1,0:T(8,128)(2,1)S(1)} async-done(((bf16[16,8,1280]{2,1,0:T(8,128)(2,1)}), bf16[16,8,1280]{2,1,0:T(8,128)(2,1)S(1)}, u32[]{:S(2)}, u32[]{:S(2)}) %all-to-all-start.1) | async-done | bytes 327712 | tf_op jit(solution)/shard_map/all_to_all | solution.py:406
  62.6 0.0 copy-start.14
  62.6 0.6 slice_reduce_fusion
  63.3 0.0 collective-permute-done.11
  63.3 2.5 %collective-permute-done.12 = bf16[216,256]{1,0:T(8,128)(2,1)S(1)} collective-permute-done((bf16[216,256]{1,0:T(8,128)(2,1)}, bf16[216,256]{1,0:T(8,128)(2,1)S(1)}, u32[]{:S(2)}, u32[]{:S(2)}) %collective-permute-start.12) | collective-permute-done | bytes 110624 | tf_op jit(solution)/shard_map/ppermute | solution.py:326
  65.7 0.0 collective-permute-done.13
  65.7 1.0 %convert_add_fusion = f32[216,256]{1,0:T(8,128)S(1)} fusion(f32[216,256]{1,0:T(8,128)} %get-tuple-element.72, bf16[216,256]{1,0:T(8,128)(2,1)S(1)} %collective-permute-done.11), kind=kLoop, calls=%fused_computation.3 | loop fusion | flops 110592 | bytes 552960 | tf_op jit(solution)/shard_map/add | solution.py:429
  66.7 0.7 %add_convert_fusion = bf16[216,256]{1,0:T(8,128)(2,1)} fusion(bf16[216,256]{1,0:T(8,128)(2,1)S(1)} %collective-permute-done.13, f32[216,256]{1,0:T(8,128)S(1)} %convert_add_fusion, bf16[216,256]{1,0:T(8,128)(2,1)S(1)} %collective-permute-done.12), kind=kLoop, calls=%fused_computation.2 | loop fusion | flops 276480 | bytes 552960 | tf_op jit(solution)/shard_map/convert_element_type | solution.py:430
  (38 shorter events, 0.2 us)
Async XLA Ops:
  0.6 11.5 %copy-start = (bf16[1024,256]{1,0:T(8,128)(2,1)S(1)}, bf16[1024,256]{1,0:T(8,128)(2,1)}, u32[]{:S(2)}) copy-start(bf16[1024,256]{1,0:T(8,128)(2,1)} %param.7) | copy-start | bytes 1572868
  3.3 7.2 %collective-permute-start.1 = (bf16[288,256]{1,0:T(8,128)(2,1)}, bf16[288,256]{1,0:T(8,128)(2,1)S(1)}, u32[]{:S(2)}, u32[]{:S(2)}) collective-permute-start(bf16[288,256]{1,0:T(8,128)(2,1)} %get-tuple-element.42.refs_0_), channel_id=1, source_target_pairs={{0,2},{1,3},{2,0},{3,1},{4,6},{5,7},{6,4},{7,5},{8,10},{9,11},{10,... | collective-permute-start | bytes 442376 | tf_op jit(solution)/shard_map/ppermute | solution.py:326
  6.3 11.7 %copy-start.9 = (bf16[288,256]{1,0:T(8,128)(2,1)S(1)}, bf16[288,256]{1,0:T(8,128)(2,1)}, u32[]{:S(2)}) copy-start(bf16[288,256]{1,0:T(8,128)(2,1)} %get-tuple-element.42.refs_0_) | copy-start | bytes 442372
  6.3 11.8 %collective-permute-start = (bf16[216,1024]{1,0:T(8,128)(2,1)}, bf16[216,1024]{1,0:T(8,128)(2,1)S(1)}, u32[]{:S(2)}, u32[]{:S(2)}) collective-permute-start(bf16[216,1024]{1,0:T(8,128)(2,1)} %get-tuple-element.44), channel_id=1, source_target_pairs={{0,4},{1,5},{2,6},{3,7},{4,0},{5,1},{6,2},{7,3},{8,12},{9,13},{10,... | collective-permute-start | bytes 1327112 | tf_op jit(solution)/shard_map/ppermute | solution.py:326
  10.4 15.0 %copy-start.15 = (bf16[216,1024]{1,0:T(8,128)(2,1)S(1)}, bf16[216,1024]{1,0:T(8,128)(2,1)}, u32[]{:S(2)}) copy-start(bf16[216,1024]{1,0:T(8,128)(2,1)} %get-tuple-element.66) | copy-start | bytes 1327108
  10.5 19.9 %copy-start.10 = (bf16[288,256]{1,0:T(8,128)(2,1)}, bf16[288,256]{1,0:T(8,128)(2,1)S(1)}, u32[]{:S(2)}) copy-start(bf16[288,256]{1,0:T(8,128)(2,1)S(1)} %collective-permute-done.1.refs_1_) | copy-start | bytes 442372
  10.5 14.4 %collective-permute-start.2 = (bf16[280,1024]{1,0:T(8,128)(2,1)}, bf16[280,1024]{1,0:T(8,128)(2,1)S(1)}, u32[]{:S(2)}, u32[]{:S(2)}) collective-permute-start(bf16[280,1024]{1,0:T(8,128)(2,1)} %get-tuple-element.51), channel_id=1, source_target_pairs={{0,2},{1,3},{2,0},{3,1},{4,6},{5,7},{6,4},{7,5},{8,10},{9,11},{10,... | collective-permute-start | bytes 1720328 | tf_op jit(solution)/shard_map/ppermute | solution.py:326
  13.2 30.9 %all-to-all-start = ((bf16[4,512,256]{2,1,0:T(8,128)(2,1)}), bf16[4,512,256]{2,1,0:T(8,128)(2,1)S(1)}, u32[]{:S(2)}, u32[]{:S(2)}) async-start(bf16[4,512,256]{2,1,0:T(8,128)(2,1)} %tile.2), calls=%async_computation | async-start | bytes 2097152 | tf_op jit(solution)/shard_map/all_to_all | solution.py:364
  18.1 12.3 %copy-start.4 = (bf16[216,1024]{1,0:T(8,128)(2,1)}, bf16[216,1024]{1,0:T(8,128)(2,1)S(1)}, u32[]{:S(2)}) copy-start(bf16[216,1024]{1,0:T(8,128)(2,1)S(1)} %collective-permute-done.refs_8_) | copy-start | bytes 1327108
  18.2 6.2 %collective-permute-start.3 = (bf16[448,256]{1,0:T(8,128)(2,1)S(1)}, bf16[448,256]{1,0:T(8,128)(2,1)S(1)}, u32[]{:S(2)}, u32[]{:S(2)}) collective-permute-start(bf16[448,256]{1,0:T(8,128)(2,1)S(1)} %pad_maximum_fusion), channel_id=1, source_target_pairs={{0,4},{1,5},{2,6},{3,7},{4,0},{5,1},{6,2},{7,3},{8,12},{9,13},{10,... | collective-permute-start | bytes 688136 | tf_op jit(solution)/shard_map/ppermute | solution.py:326
  24.4 6.0 %copy-start.8 = (bf16[448,256]{1,0:T(8,128)(2,1)}, bf16[448,256]{1,0:T(8,128)(2,1)S(1)}, u32[]{:S(2)}) copy-start(bf16[448,256]{1,0:T(8,128)(2,1)S(1)} %collective-permute-done.3.refs_2_.refs_0_) | copy-start | bytes 688132
  24.9 5.5 %copy-start.2 = (bf16[280,1024]{1,0:T(8,128)(2,1)}, bf16[280,1024]{1,0:T(8,128)(2,1)S(1)}, u32[]{:S(2)}) copy-start(bf16[280,1024]{1,0:T(8,128)(2,1)S(1)} %collective-permute-done.2.refs_10_) | copy-start | bytes 1720324
  24.9 5.5 %collective-permute-start.8 = (bf16[280,1024]{1,0:T(8,128)(2,1)S(1)}, bf16[280,1024]{1,0:T(8,128)(2,1)S(1)}, u32[]{:S(2)}, u32[]{:S(2)}) collective-permute-start(bf16[280,1024]{1,0:T(8,128)(2,1)S(1)} %collective-permute-done.2.refs_10_), channel_id=1, source_target_pairs={{0,1},{1,0},{2,3},{3,2},{4,5},{5,4},{6,7},{7,6},{8,9},{9,8},{10,11... | collective-permute-start | bytes 1720328 | tf_op jit(solution)/shard_map/ppermute | solution.py:326
  24.9 5.5 %collective-permute-start.7 = (bf16[216,1024]{1,0:T(8,128)(2,1)S(1)}, bf16[216,1024]{1,0:T(8,128)(2,1)S(1)}, u32[]{:S(2)}, u32[]{:S(2)}) collective-permute-start(bf16[216,1024]{1,0:T(8,128)(2,1)S(1)} %collective-permute-done.refs_8_), channel_id=1, source_target_pairs={{0,1},{1,0},{2,3},{3,2},{4,5},{5,4},{6,7},{7,6},{8,9},{9,8},{10,11... | collective-permute-start | bytes 1327112 | tf_op jit(solution)/shard_map/ppermute | solution.py:326
  25.4 13.0 %collective-permute-start.9 = (bf16[216,1024]{1,0:T(8,128)(2,1)S(1)}, bf16[216,1024]{1,0:T(8,128)(2,1)S(1)}, u32[]{:S(2)}, u32[]{:S(2)}) collective-permute-start(bf16[216,1024]{1,0:T(8,128)(2,1)S(1)} %copy-done.15), channel_id=1, source_target_pairs={{0,6},{1,7},{2,4},{3,5},{4,2},{5,3},{6,0},{7,1},{8,14},{9,15},{10,... | collective-permute-start | bytes 1327112 | tf_op jit(solution)/shard_map/ppermute | solution.py:326
  27.6 1.4 %collective-permute-start.4 = (bf16[288,256]{1,0:T(8,128)(2,1)S(1)}, bf16[288,256]{1,0:T(8,128)(2,1)S(1)}, u32[]{:S(2)}, u32[]{:S(2)}) collective-permute-start(bf16[288,256]{1,0:T(8,128)(2,1)S(1)} %copy-done.9), channel_id=1, source_target_pairs={{0,1},{1,0},{2,3},{3,2},{4,5},{5,4},{6,7},{7,6},{8,9},{9,8},{10,11... | collective-permute-start | bytes 442376 | tf_op jit(solution)/shard_map/ppermute | solution.py:326
  27.6 2.7 %collective-permute-start.6 = (bf16[448,256]{1,0:T(8,128)(2,1)S(1)}, bf16[448,256]{1,0:T(8,128)(2,1)S(1)}, u32[]{:S(2)}, u32[]{:S(2)}) collective-permute-start(bf16[448,256]{1,0:T(8,128)(2,1)S(1)} %collective-permute-done.3.refs_2_.refs_0_), channel_id=1, source_target_pairs={{0,1},{1,0},{2,3},{3,2},{4,5},{5,4},{6,7},{7,6},{8,9},{9,8},{10,11... | collective-permute-start | bytes 688136 | tf_op jit(solution)/shard_map/ppermute | solution.py:326
  29.0 1.5 %copy-start.12 = (bf16[288,256]{1,0:T(8,128)(2,1)}, bf16[288,256]{1,0:T(8,128)(2,1)S(1)}, u32[]{:S(2)}) copy-start(bf16[288,256]{1,0:T(8,128)(2,1)S(1)} %collective-permute-done.4.refs_3_) | copy-start | bytes 442372
  29.0 1.4 %collective-permute-start.5 = (bf16[288,256]{1,0:T(8,128)(2,1)S(1)}, bf16[288,256]{1,0:T(8,128)(2,1)S(1)}, u32[]{:S(2)}, u32[]{:S(2)}) collective-permute-start(bf16[288,256]{1,0:T(8,128)(2,1)S(1)} %collective-permute-done.1.refs_1_), channel_id=1, source_target_pairs={{0,1},{1,0},{2,3},{3,2},{4,5},{5,4},{6,7},{7,6},{8,9},{9,8},{10,11... | collective-permute-start | bytes 442376 | tf_op jit(solution)/shard_map/ppermute | solution.py:326
  30.4 0.7 copy-start.13
  30.4 0.7 %copy-start.11 = (bf16[448,256]{1,0:T(8,128)(2,1)}, bf16[448,256]{1,0:T(8,128)(2,1)S(1)}, u32[]{:S(2)}) copy-start(bf16[448,256]{1,0:T(8,128)(2,1)S(1)} %collective-permute-done.6.refs_5_) | copy-start | bytes 688132
  30.4 0.9 %copy-start.5 = (bf16[216,1024]{1,0:T(8,128)(2,1)}, bf16[216,1024]{1,0:T(8,128)(2,1)S(1)}, u32[]{:S(2)}) copy-start(bf16[216,1024]{1,0:T(8,128)(2,1)S(1)} %collective-permute-done.7.refs_9_) | copy-start | bytes 1327108
  30.4 1.1 %copy-start.3 = (bf16[280,1024]{1,0:T(8,128)(2,1)}, bf16[280,1024]{1,0:T(8,128)(2,1)S(1)}, u32[]{:S(2)}) copy-start(bf16[280,1024]{1,0:T(8,128)(2,1)S(1)} %collective-permute-done.8.refs_11_) | copy-start | bytes 1720324
  38.4 1.8 %copy-start.6 = (bf16[216,1024]{1,0:T(8,128)(2,1)}, bf16[216,1024]{1,0:T(8,128)(2,1)S(1)}, u32[]{:S(2)}) copy-start(bf16[216,1024]{1,0:T(8,128)(2,1)S(1)} %collective-permute-done.9.refs_5_.refs_6_) | copy-start | bytes 1327108
  38.4 1.8 %collective-permute-start.10 = (bf16[216,1024]{1,0:T(8,128)(2,1)S(1)}, bf16[216,1024]{1,0:T(8,128)(2,1)S(1)}, u32[]{:S(2)}, u32[]{:S(2)}) collective-permute-start(bf16[216,1024]{1,0:T(8,128)(2,1)S(1)} %collective-permute-done.9.refs_5_.refs_6_), channel_id=1, source_target_pairs={{0,1},{1,0},{2,3},{3,2},{4,5},{5,4},{6,7},{7,6},{8,9},{9,8},{10,11... | collective-permute-start | bytes 1327112 | tf_op jit(solution)/shard_map/ppermute | solution.py:326
  40.2 0.8 %copy-start.7 = (bf16[216,1024]{1,0:T(8,128)(2,1)}, bf16[216,1024]{1,0:T(8,128)(2,1)S(1)}, u32[]{:S(2)}) copy-start(bf16[216,1024]{1,0:T(8,128)(2,1)S(1)} %collective-permute-done.10.refs_6_.refs_7_) | copy-start | bytes 1327108
  44.1 6.6 %copy-start.1 = (bf16[4,512,256]{2,1,0:T(8,128)(2,1)}, bf16[4,512,256]{2,1,0:T(8,128)(2,1)S(1)}, u32[]{:S(2)}) copy-start(bf16[4,512,256]{2,1,0:T(8,128)(2,1)S(1)} %all-to-all-done) | copy-start | bytes 3145732
  44.1 18.4 %all-to-all-start.1 = ((bf16[16,8,1280]{2,1,0:T(8,128)(2,1)}), bf16[16,8,1280]{2,1,0:T(8,128)(2,1)S(1)}, u32[]{:S(2)}, u32[]{:S(2)}) async-start(bf16[16,8,1280]{2,1,0:T(8,128)(2,1)} %bitcast.44), calls=%async_computation.1 | async-start | bytes 655360 | tf_op jit(solution)/shard_map/all_to_all | solution.py:406
  56.2 7.1 %collective-permute-start.11 = (bf16[216,256]{1,0:T(8,128)(2,1)}, bf16[216,256]{1,0:T(8,128)(2,1)S(1)}, u32[]{:S(2)}, u32[]{:S(2)}) collective-permute-start(bf16[216,256]{1,0:T(8,128)(2,1)} %get-tuple-element.73), channel_id=1, source_target_pairs={{0,4},{1,5},{2,6},{3,7},{4,0},{5,1},{6,2},{7,3},{8,12},{9,13},{10,... | collective-permute-start | bytes 331784 | tf_op jit(solution)/shard_map/ppermute | solution.py:326
  58.2 7.5 %collective-permute-start.12 = (bf16[216,256]{1,0:T(8,128)(2,1)}, bf16[216,256]{1,0:T(8,128)(2,1)S(1)}, u32[]{:S(2)}, u32[]{:S(2)}) collective-permute-start(bf16[216,256]{1,0:T(8,128)(2,1)} %get-tuple-element.74), channel_id=1, source_target_pairs={{0,2},{1,3},{2,0},{3,1},{4,6},{5,7},{6,4},{7,5},{8,10},{9,11},{10,... | collective-permute-start | bytes 331784 | tf_op jit(solution)/shard_map/ppermute | solution.py:326
  59.7 6.1 %collective-permute-start.13 = (bf16[216,256]{1,0:T(8,128)(2,1)}, bf16[216,256]{1,0:T(8,128)(2,1)S(1)}, u32[]{:S(2)}, u32[]{:S(2)}) collective-permute-start(bf16[216,256]{1,0:T(8,128)(2,1)} %get-tuple-element.75), channel_id=1, source_target_pairs={{0,6},{1,7},{2,4},{3,5},{4,2},{5,3},{6,0},{7,1},{8,14},{9,15},{10,... | collective-permute-start | bytes 331784 | tf_op jit(solution)/shard_map/ppermute | solution.py:326
  62.6 4.8 %copy-start.14 = (f32[8,4096]{1,0:T(8,128)}, f32[8,4096]{1,0:T(8,128)S(1)}, u32[]{:S(2)}) copy-start(f32[8,4096]{1,0:T(8,128)S(1)} %constant_dynamic-update-slice_fusion) | copy-start | bytes 393220
